TPU v7x, 128 devices: a whole 4x4x4 slice. The times are simulated.
128 devices in a mesh: expert: 8 (over y, z_lo), fsdp: 16 (over x, z_hi, core).
Axes of the slice: x: 4, y: 4, z: 4 (z_hi: 2, z_lo: 2; z = z_hi * 2 + z_lo), core: 2. Of those that a mesh axis runs over, the one named last changes fastest.
Arguments:
- tokens: bfloat16 [18432, 2048], P(('expert', 'fsdp')), may hold values from -6 to 6
- expert_ids: int32 [18432, 6], P(('expert', 'fsdp')), may hold values from 0 to 15, as said below
- combine: float32 [18432, 6], P(('expert', 'fsdp')), may hold values from 0.05 to 1
- gate_weight: bfloat16 [16, 1408, 2048], P('expert', 'fsdp'), may hold values from -0.125 to 0.125
- up_weight: bfloat16 [16, 1408, 2048], P('expert', 'fsdp'), may hold values from -0.125 to 0.125
- down_weight: bfloat16 [16, 1408, 2048], P('expert', 'fsdp'), may hold values from -0.15625 to 0.15625
Outputs:
- mixed: bfloat16 [18432, 2048], P(('expert', 'fsdp'))
Inputs may be any that keep to these rules, and one draw needn't show every extreme that they name: `expert_ids`: each row names 6 different experts. Within the 144 rows of each device no expert is named more than 72 times, and one and the same expert is named exactly 72 times by the rows of every device.
All inputs are finite; a program needn't handle non-finite values.
Results may differ from a plain program's by a relative error of at most 0.0058.
Values may be sent and summed in bfloat16 or wider, within the bound.
A program may use at most 128 MiB of HBM per device.

v0:
```python
import jax
import jax.numpy as jnp
from jax import lax
from jax.sharding import PartitionSpec as P

CAP = 72


def add_piece(expert_rows, pieces):
    gate_piece, up_piece, down_piece = pieces
    gate_pre = jnp.einsum(
        "grd,gfd->grf", expert_rows, gate_piece, preferred_element_type=jnp.float32
    )
    up_pre = jnp.einsum("grd,gfd->grf", expert_rows, up_piece, preferred_element_type=jnp.float32)
    hidden = (jax.nn.silu(gate_pre) * up_pre).astype(jnp.bfloat16)
    return jnp.einsum("grf,gfd->grd", hidden, down_piece, preferred_element_type=jnp.float32)


def per_device(tokens, expert_ids, combine, gate_weight, up_weight, down_weight):
    groups = lax.axis_size("expert")
    per_group = gate_weight.shape[0]
    tok_rows, top_k = expert_ids.shape
    model_width = tokens.shape[1]
    flat_ids = expert_ids.reshape(-1)
    onehot = (flat_ids[:, None] == jnp.arange(per_group * groups, dtype=jnp.int32)[None, :]).astype(
        jnp.int32
    )
    earlier = jnp.cumsum(onehot, axis=0) - onehot
    rank_within = jnp.sum(earlier * onehot, axis=1)
    owner_group = flat_ids // per_group
    within = flat_ids % per_group
    slot_index = (within * groups + owner_group) * CAP + rank_within
    source = jnp.arange(tok_rows * top_k, dtype=jnp.int32) // top_k
    outgoing = (
        jnp.zeros((per_group * groups * CAP, model_width), jnp.bfloat16)
        .at[slot_index]
        .set(tokens[source])
    )
    outgoing = outgoing.reshape(per_group, groups, CAP, model_width)
    arrived = lax.all_to_all(outgoing, "expert", split_axis=1, concat_axis=1, tiled=True)
    expert_rows = arrived.reshape(per_group, groups * CAP, model_width)
    summed = add_piece(
        expert_rows,
        (
            lax.all_gather(gate_weight, "fsdp", axis=1, tiled=True),
            lax.all_gather(up_weight, "fsdp", axis=1, tiled=True),
            lax.all_gather(down_weight, "fsdp", axis=1, tiled=True),
        ),
    )
    produced = summed.astype(jnp.bfloat16)
    produced = produced.reshape(per_group, groups, CAP, model_width)
    returned = lax.all_to_all(produced, "expert", split_axis=1, concat_axis=1, tiled=True)
    back_rows = returned.reshape(per_group * groups * CAP, model_width)[slot_index]
    weighted = (
        back_rows.astype(jnp.float32).reshape(tok_rows, top_k, model_width) * combine[:, :, None]
    )
    return jnp.sum(weighted, axis=1).astype(jnp.bfloat16)


def solution(mesh):
    return jax.shard_map(
        per_device,
        mesh=mesh,
        in_specs=(
            P(("expert", "fsdp"), None),
            P(("expert", "fsdp"), None),
            P(("expert", "fsdp"), None),
            P("expert", "fsdp", None),
            P("expert", "fsdp", None),
            P("expert", "fsdp", None),
        ),
        out_specs=P(("expert", "fsdp"), None),
        check_vma=False,
    )
```

profile of v0, /device:TPU:2, one launch (start us, length us, event | category | flops | bytes accessed | tf_op | source)
XLA Modules:
  0.0 455.4 jit_solution(14942654767058175792)
XLA Ops:
  6.5 0.0 copy-start
  6.5 0.0 all-gather.4.cloned.1.call-start
  6.5 0.7 all-gather.4.cloned.1.call-update
  7.3 0.0 all-gather.6.cloned.1.call-start
  7.3 0.7 all-gather.6.cloned.1.call-update
  8.0 0.0 all-gather.8.cloned.1.call-start
  8.1 0.7 all-gather.8.cloned.1.call-update
  8.7 0.8 copy.21
  9.5 0.1 eq.24
  9.7 0.1 reshape.195
  9.9 2.0 reduce-window.6
  11.9 0.3 slice_reduce_fusion
  12.2 0.1 bitcast_bitcast_fusion
  12.4 0.0 copy-done
  12.4 23.2 %scatter_custom_fusion = bf16[1152,2048]{1,0:T(8,128)(2,1)} fusion(s32[864]{0:T(1024)S(1)} %fusion.5, bf16[144,2048]{1,0:T(8,128)(2,1)S(1)} %copy-done, s32[1024]{0:T(1024)S(1)} %pad_clamp_fusion.1, bf16[]{:T(256)} %constant.42.clone.1), kind=kCustom, calls=%fused_computation.6 | custom fusion | bytes 4718594 | tf_op jit(solution)/shard_map/scatter | solution.py:37
  35.6 2.8 copy.25
  38.4 69.8 %all_to_all.10 = bf16[2,8,72,2048]{3,2,0,1:T(8,128)(2,1)S(1)} all-to-all(bf16[2,8,72,2048]{3,2,0,1:T(8,128)(2,1)S(1)} %copy.25), channel_id=1, replica_groups=mesh['expert'=8,'fsdp'=16] {'expert'}, dimensions={1} | all-to-all | bytes 9437184 | tf_op jit(solution)/shard_map/all_to_all | solution.py:40
  108.2 2.5 copy.26
  110.7 33.1 %all-gather.4.cloned.1.call-done = bf16[2,1408,2048]{2,1,0:T(8,128)(2,1)} async-done(((bf16[2,88,2048]{2,1,0:T(8,128)(2,1)}), bf16[2,1408,2048]{2,1,0:T(8,128)(2,1)}) %all-gather.4.cloned.1.call-update) | async-done | bytes 11534352 | tf_op jit(solution)/shard_map/all_gather | solution.py:45
  143.8 14.4 %fusion.9 = f32[2,576,1408]{2,1,0:T(8,128)} fusion(bf16[2,576,2048]{2,1,0:T(8,128)(2,1)} %bitcast.33, bf16[2,1408,2048]{2,1,0:T(8,128)(2,1)} %all-gather.4.cloned.1.call-done), kind=kOutput, calls=%fused_computation.36 | convolution fusion | flops 6643777536 | bytes 22740992 | tf_op jit(solution)/shard_map/grd,gfd->grf/dot_general | solution.py:11
  158.2 71.9 %all-gather.6.cloned.1.call-done = bf16[2,1408,2048]{2,1,0:T(8,128)(2,1)} async-done(((bf16[2,88,2048]{2,1,0:T(8,128)(2,1)}), bf16[2,1408,2048]{2,1,0:T(8,128)(2,1)}) %all-gather.6.cloned.1.call-update) | async-done | bytes 11534352 | tf_op jit(solution)/shard_map/all_gather | solution.py:46
  230.1 86.3 %all-gather.8.cloned.1.call-done = bf16[2,1408,2048]{2,1,0:T(8,128)(2,1)} async-done(((bf16[2,88,2048]{2,1,0:T(8,128)(2,1)}), bf16[2,1408,2048]{2,1,0:T(8,128)(2,1)}) %all-gather.8.cloned.1.call-update) | async-done | bytes 11534352 | tf_op jit(solution)/shard_map/all_gather | solution.py:47
  316.3 22.8 %convolution_convert_fusion = bf16[2,576,2048]{2,1,0:T(8,128)(2,1)} fusion(bf16[2,1408,2048]{2,1,0:T(8,128)(2,1)} %all-gather.8.cloned.1.call-done, f32[2,576,1408]{2,1,0:T(8,128)} %fusion.9, bf16[2,576,2048]{2,1,0:T(8,128)(2,1)} %bitcast.34, bf16[2,1408,2048]{2,1,0:T(8,128)(2,1)} %all-gather.6.cloned.1.call-done), kind=kOutput, calls=%fused_computation.5 | convolution fusion | flops 13299646464 | bytes 38993920 | tf_op jit(solution)/shard_map/grf,gfd->grd/dot_general | solution.py:16
  339.1 5.2 %copy.27 = bf16[2,8,72,2048]{3,2,0,1:T(8,128)(2,1)} copy(bf16[2,8,72,2048]{3,2,1,0:T(8,128)(2,1)} %bitcast.35) | data formatting | bytes 9437184 | tf_op jit(solution)/shard_map/reshape | solution.py:51
  344.4 4.9 %all-to-all-start.1 = ((bf16[2,8,72,2048]{3,2,0,1:T(8,128)(2,1)}), bf16[2,8,72,2048]{3,2,0,1:T(8,128)(2,1)}, u32[]{:S(2)}, u32[]{:S(2)}) async-start(bf16[2,8,72,2048]{3,2,0,1:T(8,128)(2,1)} %copy.27), calls=%async_computation.1 | async-start | bytes 9437184 | tf_op jit(solution)/shard_map/all_to_all | solution.py:52
  349.3 0.0 copy-done.2
  349.3 0.1 copy.29
  349.4 67.1 %all-to-all-done.1 = bf16[2,8,72,2048]{3,2,0,1:T(8,128)(2,1)} async-done(((bf16[2,8,72,2048]{3,2,0,1:T(8,128)(2,1)}), bf16[2,8,72,2048]{3,2,0,1:T(8,128)(2,1)}, u32[]{:S(2)}, u32[]{:S(2)}) %all-to-all-start.1) | async-done | bytes 4718624 | tf_op jit(solution)/shard_map/all_to_all | solution.py:52
  416.5 5.2 %copy.28 = bf16[2,8,72,2048]{3,2,1,0:T(8,128)(2,1)} copy(bf16[2,8,72,2048]{3,2,0,1:T(8,128)(2,1)} %all-to-all-done.1) | data formatting | bytes 9437184 | tf_op jit(solution)/shard_map/all_to_all | solution.py:52
  421.8 11.7 %gather_fusion = bf16[864,2048]{1,0:T(8,128)(2,1)} fusion(bf16[1152,2048]{1,0:T(8,128)(2,1)} %bitcast.31, s32[1024]{0:T(1024)S(1)} %pad_clamp_fusion), kind=kCustom, calls=%fused_computation.1 | custom fusion | bytes 7081344 | tf_op jit(solution)/shard_map/gather | solution.py:53
  433.5 7.2 %reshape.203 = f32[144,6,2048]{2,1,0:T(8,128)} reshape(bf16[864,2048]{1,0:T(8,128)(2,1)} %gather_fusion) | data formatting | bytes 10616832 | tf_op jit(solution)/shard_map/convert_element_type | solution.py:55
  440.7 8.2 %multiply_reduce_fusion = bf16[144,2048]{1,0:T(8,128)(2,1)} fusion(f32[144,6,2048]{2,1,0:T(8,128)} %reshape.203, f32[144,6]{1,0:T(8,128)S(1)} %copy.29), kind=kLoop, calls=%fused_computation.3 | loop fusion | flops 3244032 | bytes 7671168 | tf_op jit(solution)/shard_map/reduce_sum | solution.py:57
  (11 shorter events, 0.2 us)
Async XLA Ops:
  6.5 5.9 %copy-start = (bf16[144,2048]{1,0:T(8,128)(2,1)S(1)}, bf16[144,2048]{1,0:T(8,128)(2,1)}, u32[]{:S(2)}) copy-start(bf16[144,2048]{1,0:T(8,128)(2,1)} %param.6) | copy-start | bytes 1769476
  6.5 137.2 %all-gather.4.cloned.1.call-start = ((), (), s32[]{:S(2)}) async-start(), calls=%async_computation.2 | async-start | bytes 12255232 | tf_op jit(solution)/shard_map/all_gather | solution.py:45
  7.3 222.8 %all-gather.6.cloned.1.call-start = ((), (), s32[]{:S(2)}) async-start(), calls=%async_computation.3 | async-start | bytes 12255232 | tf_op jit(solution)/shard_map/all_gather | solution.py:46
  8.0 308.3 %all-gather.8.cloned.1.call-start = ((), (), s32[]{:S(2)}) async-start(), calls=%async_computation.4 | async-start | bytes 12255232 | tf_op jit(solution)/shard_map/all_gather | solution.py:47
  344.4 5.0 %copy-start.2 = (f32[144,6]{0,1:T(8,128)S(1)}, f32[144,6]{0,1:T(8,128)}, u32[]{:S(2)}) copy-start(f32[144,6]{0,1:T(8,128)} %param.8) | copy-start | bytes 10372
  344.4 72.2 %all-to-all-start.1 = ((bf16[2,8,72,2048]{3,2,0,1:T(8,128)(2,1)}), bf16[2,8,72,2048]{3,2,0,1:T(8,128)(2,1)}, u32[]{:S(2)}, u32[]{:S(2)}) async-start(bf16[2,8,72,2048]{3,2,0,1:T(8,128)(2,1)} %copy.27), calls=%async_computation.1 | async-start | bytes 9437184 | tf_op jit(solution)/shard_map/all_to_all | solution.py:52
  433.5 15.4 %copy-start.1 = (bf16[144,2048]{1,0:T(8,128)(2,1)S(1)}, bf16[144,2048]{1,0:T(8,128)(2,1)}, u32[]{:S(2)}) copy-start(bf16[144,2048]{1,0:T(8,128)(2,1)} %param.6) | copy-start | bytes 1769476
Sparse Core Ops, SparseCore 0:
  9.8 133.9 all-gather.3
  146.2 83.7 all-gather.5
  232.5 83.7 all-gather.7
where the time goes:
time: 458 us; the launch traced here: 455 us
  waiting for transfers between devices  260 us (57%)
  blocking collectives  69.8 us (15%)
  local copies, waits for them, and re-layouts  59.3 us (13%)
  matrix products  37.2 us (8%)
  between operations  13.2 us (3%)
  other arithmetic  10.4 us (2%)
  starting transfers between devices  5.02 us (1%)
    all_gather x1, waiting for transfers between devices, per_device(): lax.all_gather(down_weight, 'fsdp', axis=1, tiled=True)  86.3 us
    all_gather x1, waiting for transfers between devices, per_device(): lax.all_gather(up_weight, 'fsdp', axis=1, tiled=True)  71.9 us
    all_to_all x1, blocking collectives, per_device(): lax.all_to_all(outgoing, 'expert', split_axis=1, concat_axis=1, tiled=True)  69.8 us
    all_to_all x1, waiting for transfers between devices, per_device(): lax.all_to_all(produced, 'expert', split_axis=1, concat_axis=1, tiled=True)  67.1 us
    all_gather x1, waiting for transfers between devices, per_device(): lax.all_gather(gate_weight, 'fsdp', axis=1, tiled=True)  33.1 us
    scatter x1, local copies, waits for them, and re-layouts, per_device(): outgoing = jnp.zeros((per_group * groups * CAP, model_width), jnp.bfloat1...  23.2 us
    dot_general x1, matrix products, add_piece(): jnp.einsum('grf,gfd->grd', hidden, down_piece, preferred_element_type=jnp...  22.8 us
    dot_general x1, matrix products, add_piece(): jnp.einsum('grd,gfd->grf', expert_rows, gate_piece, preferred_element_typ...  14.4 us
  transfers between devices with their start and end apart: 4, of which 4 were waited for; matrix products, arithmetic and copies ran while one was open for 10% of the time, Pallas kernels for 0%

commit v1 on v0

v1 whole, which is shorter than its diff:
```python
import jax
import jax.numpy as jnp
from jax import lax
from jax.sharding import Mesh
from jax.sharding import PartitionSpec as P

CAP = 72


def gather_expert(piece, core):
    mine = lax.dynamic_index_in_dim(piece, core, 0, keepdims=False)
    other = lax.dynamic_index_in_dim(piece, 1 - core, 0, keepdims=False)
    got = lax.ppermute(other, "core", [(0, 1), (1, 0)])
    pair = jnp.stack([mine, got])
    return lax.all_gather(pair, "chip", axis=0, tiled=True).reshape(-1, piece.shape[-1])


def per_device(tokens, expert_ids, combine, gate_weight, up_weight, down_weight):
    core = lax.axis_index("core")
    per_group = gate_weight.shape[0]
    groups = lax.axis_size("expert")
    n_expert = per_group * groups
    tok_rows, top_k = expert_ids.shape
    model_width = tokens.shape[1]

    gate_full = gather_expert(gate_weight, core)
    up_full = gather_expert(up_weight, core)
    down_full = gather_expert(down_weight, core)

    flat_ids = expert_ids.reshape(-1)
    onehot = (flat_ids[:, None] == jnp.arange(n_expert, dtype=jnp.int32)[None, :]).astype(jnp.int32)
    earlier = jnp.cumsum(onehot, axis=0) - onehot
    rank_within = jnp.sum(earlier * onehot, axis=1)
    slot_index = flat_ids * CAP + rank_within
    source = jnp.arange(tok_rows * top_k, dtype=jnp.int32) // top_k
    outgoing = (
        jnp.zeros((n_expert * CAP, model_width), jnp.bfloat16).at[slot_index].set(tokens[source])
    )
    outgoing = outgoing.reshape(n_expert, CAP, model_width)
    arrived = lax.all_to_all(outgoing, ("expert", "core"), 0, 0, tiled=True)
    rows = arrived.reshape(n_expert * CAP, model_width)

    gate_pre = jnp.dot(rows, gate_full.T, preferred_element_type=jnp.float32)
    up_pre = jnp.dot(rows, up_full.T, preferred_element_type=jnp.float32)
    hidden = (jax.nn.silu(gate_pre) * up_pre).astype(jnp.bfloat16)
    produced = jnp.dot(hidden, down_full, preferred_element_type=jnp.float32).astype(jnp.bfloat16)
    produced = produced.reshape(n_expert, CAP, model_width)
    returned = lax.all_to_all(produced, ("expert", "core"), 0, 0, tiled=True)
    back_rows = returned.reshape(n_expert * CAP, model_width)[slot_index]
    weighted = back_rows.astype(jnp.float32).reshape(tok_rows, top_k, model_width) * combine[:, :, None]
    return jnp.sum(weighted, axis=1).astype(jnp.bfloat16)


def solution(mesh):
    groups = mesh.shape["expert"]
    chips = mesh.shape["fsdp"] // 2
    inner = Mesh(mesh.devices.reshape(groups, chips, 2), ("expert", "chip", "core"))
    rows = P(("expert", "chip", "core"), None)
    weights = P("expert", ("chip", "core"), None)
    return jax.shard_map(
        per_device,
        mesh=inner,
        in_specs=(rows, rows, rows, weights, weights, weights),
        out_specs=rows,
        check_vma=False,
    )
```

time: 458 us -> 446 us (0.974); the launches traced: 455 us -> 438 us
  local copies, waits for them, and re-layouts: 59.3 us -> 45.4 us
  waiting for transfers between devices: 260 us -> 253 us
    reshape x3 -> x0, local copies, waits for them, and re-layouts: 8.14 us -> none  [the longest x1 5.23 us: per_device(): produced = produced.reshape(per_group, groups, CAP, model_width)]
    all_to_all x2 -> x0, local copies, waits for them, and re-layouts: 7.72 us -> none  [the longest x1 5.23 us: per_device(): lax.all_to_all(produced, 'expert', split_axis=1, concat_axis=1, tiled=True)]
    all_to_all x1, waiting for transfers between devices: 67.1 us -> 59.4 us  [per_device(): returned = lax.all_to_all(produced, ('expert', 'core'), 0, 0, tiled=True)]
    ppermute x0 -> x3, waiting for transfers between devices: none -> 4.74 us  [gather_expert(): got = lax.ppermute(other, 'core', [(0, 1), (1, 0)])]
  transfers between devices with their start and end apart: 4 -> 7, of which waited for: 4 -> 7; matrix products, arithmetic and copies ran while one was open for 10% -> 10% of each run, Pallas kernels for 0% -> 0%
where the time goes in v1:
time: 446 us; the launch traced here: 438 us
  waiting for transfers between devices  253 us (57%)
  blocking collectives  71.9 us (16%)
  local copies, waits for them, and re-layouts  45.4 us (10%)
  matrix products  35.5 us (8%)
  between operations  13.3 us (3%)
  other arithmetic  13.2 us (3%)
  starting transfers between devices  5.51 us (1%)
    all_gather x3, waiting for transfers between devices, gather_expert(): lax.all_gather(pair, 'chip', axis=0, tiled=True)  189 us
    all_to_all x1, blocking collectives, per_device(): arrived = lax.all_to_all(outgoing, ('expert', 'core'), 0, 0, tiled=True)  71.9 us
    all_to_all x1, waiting for transfers between devices, per_device(): returned = lax.all_to_all(produced, ('expert', 'core'), 0, 0, tiled=True)  59.4 us
    scatter x1, local copies, waits for them, and re-layouts, per_device(): jnp.zeros((n_expert * CAP, model_width), jnp.bfloat16).at[slot_index]  23.1 us
    dot_general x1, matrix products, per_device(): jnp.dot(hidden, down_full, preferred_element_type=jnp.float32)  22.8 us
    dot_general x1, matrix products, per_device(): gate_pre = jnp.dot(rows, gate_full.T, preferred_element_type=jnp.float32)  12.8 us
    gather x1, local copies, waits for them, and re-layouts, per_device(): back_rows = returned.reshape(n_expert * CAP, model_width)[slot_index]  11.7 us
  transfers between devices with their start and end apart: 7, of which 7 were waited for; matrix products, arithmetic and copies ran while one was open for 10% of the time, Pallas kernels for 0%

profile of v1, /device:TPU:2, one launch (start us, length us, event | category | flops | bytes accessed | tf_op | source)
XLA Modules:
  0.0 438.0 jit_solution(6090683395632843541)
XLA Ops:
  6.5 1.3 constant_dynamic-slice_fusion.2
  7.8 0.1 collective-permute-start
  7.9 1.7 collective-permute-done
  9.6 0.9 pad_maximum_fusion
  10.6 1.2 constant_dynamic-slice_fusion.1
  11.8 0.2 collective-permute-start.1
  12.0 1.5 collective-permute-done.1
  13.5 0.9 pad_maximum_fusion.1
  14.5 0.1 constant_dynamic-slice_fusion
  14.6 0.2 collective-permute-start.2
  14.8 1.5 collective-permute-done.2
  16.3 0.9 pad_maximum_fusion.2
  17.3 0.1 copy.14
  17.4 0.1 eq.22
  17.6 2.0 reduce-window.6
  19.6 0.3 slice_reduce_fusion
  19.9 0.1 copy.13
  20.0 0.1 mul.36
  20.2 0.1 bitcast_bitcast_fusion
  20.4 23.1 %scatter_custom_fusion = bf16[1152,2048]{1,0:T(8,128)(2,1)} fusion(s32[864]{0:T(1024)S(1)} %fusion.6, bf16[144,2048]{1,0:T(8,128)(2,1)S(1)} %copy-done, s32[1024]{0:T(1024)S(1)} %pad_clamp_fusion.1, bf16[]{:T(256)} %constant.40.clone.1), kind=kCustom, calls=%fused_computation.7 | custom fusion | bytes 4718594 | tf_op jit(solution)/shard_map/scatter | solution.py:37
  43.5 71.9 %all_to_all.10 = bf16[16,72,2048]{2,1,0:T(8,128)(2,1)} all-to-all(bf16[16,72,2048]{2,1,0:T(8,128)(2,1)} %bitcast.43), channel_id=1, replica_groups=mesh['expert'=8,'chip'=8,'core'=2] {'expert','core'}, dimensions={0} | all-to-all | bytes 9437184 | tf_op jit(solution)/shard_map/all_to_all | solution.py:40
  115.4 31.9 %all-gather.4.cloned.1.call-done = bf16[16,88,2048]{2,1,0:T(8,128)(2,1)} async-done(((bf16[2,88,2048]{2,1,0:T(8,128)(2,1)}), bf16[16,88,2048]{2,1,0:T(8,128)(2,1)}) %all-gather.4.cloned.1.call-update) | async-done | bytes 5767184 | tf_op jit(solution)/shard_map/all_gather | solution.py:15
  147.3 12.8 %fusion.8 = f32[1152,1408]{1,0:T(8,128)} fusion(bf16[1152,2048]{1,0:T(8,128)(2,1)} %bitcast.44, bf16[1408,2048]{1,0:T(8,128)(2,1)} %bitcast.51), kind=kOutput, calls=%fused_computation.40 | convolution fusion | flops 6643777536 | bytes 16973824 | tf_op jit(solution)/shard_map/dot_general | solution.py:43
  160.1 72.2 %all-gather.6.cloned.1.call-done = bf16[16,88,2048]{2,1,0:T(8,128)(2,1)} async-done(((bf16[2,88,2048]{2,1,0:T(8,128)(2,1)}), bf16[16,88,2048]{2,1,0:T(8,128)(2,1)}) %all-gather.6.cloned.1.call-update) | async-done | bytes 5767184 | tf_op jit(solution)/shard_map/all_gather | solution.py:15
  232.2 84.9 %all-gather.8.cloned.1.call-done = bf16[16,88,2048]{2,1,0:T(8,128)(2,1)} async-done(((bf16[2,88,2048]{2,1,0:T(8,128)(2,1)}), bf16[16,88,2048]{2,1,0:T(8,128)(2,1)}) %all-gather.8.cloned.1.call-update) | async-done | bytes 5767184 | tf_op jit(solution)/shard_map/all_gather | solution.py:15
  317.2 22.8 %convolution_convert_fusion = bf16[1152,2048]{1,0:T(8,128)(2,1)} fusion(bf16[1408,2048]{1,0:T(8,128)(2,1)} %bitcast.53, bf16[1152,2048]{1,0:T(8,128)(2,1)} %bitcast.45, bf16[1408,2048]{1,0:T(8,128)(2,1)} %bitcast.52, f32[1152,1408]{1,0:T(8,128)} %fusion.8), kind=kOutput, calls=%fused_computation.6 | convolution fusion | flops 13299646464 | bytes 27459584 | tf_op jit(solution)/shard_map/dot_general | solution.py:46
  339.9 4.9 %all-to-all-start.1 = ((bf16[16,72,2048]{2,1,0:T(8,128)(2,1)}), bf16[16,72,2048]{2,1,0:T(8,128)(2,1)}, u32[]{:S(2)}, u32[]{:S(2)}) async-start(bf16[16,72,2048]{2,1,0:T(8,128)(2,1)} %bitcast.46), calls=%async_computation.1 | async-start | bytes 9437184 | tf_op jit(solution)/shard_map/all_to_all | solution.py:48
  344.9 0.1 copy.17
  345.0 59.4 %all-to-all-done.1 = bf16[16,72,2048]{2,1,0:T(8,128)(2,1)} async-done(((bf16[16,72,2048]{2,1,0:T(8,128)(2,1)}), bf16[16,72,2048]{2,1,0:T(8,128)(2,1)}, u32[]{:S(2)}, u32[]{:S(2)}) %all-to-all-start.1) | async-done | bytes 4718624 | tf_op jit(solution)/shard_map/all_to_all | solution.py:48
  404.4 11.7 %gather_fusion = bf16[864,2048]{1,0:T(8,128)(2,1)} fusion(bf16[1152,2048]{1,0:T(8,128)(2,1)} %bitcast.13, s32[1024]{0:T(1024)S(1)} %pad_clamp_fusion), kind=kCustom, calls=%fused_computation.1 | custom fusion | bytes 7081344 | tf_op jit(solution)/shard_map/gather | solution.py:49
  416.1 7.1 %reshape.120 = f32[144,6,2048]{2,1,0:T(8,128)} reshape(bf16[864,2048]{1,0:T(8,128)(2,1)} %gather_fusion) | data formatting | bytes 10616832 | tf_op jit(solution)/shard_map/convert_element_type | solution.py:50
  423.2 8.2 %multiply_reduce_fusion = bf16[144,2048]{1,0:T(8,128)(2,1)} fusion(f32[144,6,2048]{2,1,0:T(8,128)} %reshape.120, f32[144,6]{1,0:T(8,128)S(1)} %copy.17), kind=kLoop, calls=%fused_computation.4 | loop fusion | flops 3244032 | bytes 7671168 | tf_op jit(solution)/shard_map/reduce_sum | solution.py:51
  (23 shorter events, 0.3 us)
Async XLA Ops:
  6.5 13.8 %copy-start = (bf16[144,2048]{1,0:T(8,128)(2,1)S(1)}, bf16[144,2048]{1,0:T(8,128)(2,1)}, u32[]{:S(2)}) copy-start(bf16[144,2048]{1,0:T(8,128)(2,1)} %param.6) | copy-start | bytes 1769476
  6.5 8.0 %copy-start.1 = (bf16[2,88,2048]{2,1,0:T(8,128)(2,1)S(1)}, bf16[2,88,2048]{2,1,0:T(8,128)(2,1)}, u32[]{:S(2)}) copy-start(bf16[2,88,2048]{2,1,0:T(8,128)(2,1)} %param.11) | copy-start | bytes 2162692
  6.5 140.8 %all-gather.4.cloned.1.call-start = ((), (), s32[]{:S(2)}) async-start(), calls=%async_computation.2 | async-start | bytes 6488064 | tf_op jit(solution)/shard_map/all_gather | solution.py:15
  7.8 9.5 %copy-start.2 = (s32[144,6]{0,1:T(8,128)S(1)}, s32[144,6]{0,1:T(8,128)}, u32[]{:S(2)}) copy-start(s32[144,6]{0,1:T(8,128)} %param.7) | copy-start | bytes 10372
  7.8 1.8 collective-permute-start
  10.5 221.7 %all-gather.6.cloned.1.call-start = ((), (), s32[]{:S(2)}) async-start(), calls=%async_computation.3 | async-start | bytes 6488064 | tf_op jit(solution)/shard_map/all_gather | solution.py:15
  11.8 1.8 collective-permute-start.1
  14.5 302.7 %all-gather.8.cloned.1.call-start = ((), (), s32[]{:S(2)}) async-start(), calls=%async_computation.4 | async-start | bytes 6488064 | tf_op jit(solution)/shard_map/all_gather | solution.py:15
  14.6 1.8 collective-permute-start.2
  339.9 4.9 %copy-start.3 = (f32[144,6]{0,1:T(8,128)S(1)}, f32[144,6]{0,1:T(8,128)}, u32[]{:S(2)}) copy-start(f32[144,6]{0,1:T(8,128)} %param.8) | copy-start | bytes 10372
  339.9 64.4 %all-to-all-start.1 = ((bf16[16,72,2048]{2,1,0:T(8,128)(2,1)}), bf16[16,72,2048]{2,1,0:T(8,128)(2,1)}, u32[]{:S(2)}, u32[]{:S(2)}) async-start(bf16[16,72,2048]{2,1,0:T(8,128)(2,1)} %bitcast.46), calls=%async_computation.1 | async-start | bytes 9437184 | tf_op jit(solution)/shard_map/all_to_all | solution.py:48
Sparse Core Ops, SparseCore 0:
  10.7 136.5 all-gather.3
  149.6 82.5 all-gather.5
  234.5 82.5 all-gather.7

commit v2 on v1

v2 whole, which is shorter than its diff:
```python
import functools

import jax
import jax.numpy as jnp
from jax import lax
from jax.experimental import pallas as pl
from jax.experimental.pallas import tpu as pltpu
from jax.sharding import Mesh
from jax.sharding import PartitionSpec as P

CAP = 72
MESH_ID = pl.DeviceIdType.MESH


def weight_kernel(n_x, g_in, u_in, d_in, g_out, u_out, d_out, send_sem, recv_sem, local_sem):
    ins = (g_in, u_in, d_in)
    outs = (g_out, u_out, d_out)
    x = lax.axis_index("x")
    h = lax.axis_index("zhi")
    c = lax.axis_index("core")

    def block(xx, hh, cc):
        return (xx * 2 + hh) * 2 + cc

    me = block(x, h, c)
    x_peers = [lax.rem(x + s, n_x) for s in range(1, n_x)]
    partner = {"core": 1 - c}
    z_peer = {"zhi": 1 - h}
    x_devs = [{"x": xp} for xp in x_peers]

    barrier = pltpu.get_barrier_semaphore()
    for dev in [partner, z_peer] + x_devs:
        pl.semaphore_signal(barrier, inc=1, device_id=dev, device_id_type=MESH_ID)
    pl.semaphore_wait(barrier, 2 + len(x_devs))

    count = [0]

    def send(src_of, blk, dev):
        k = count[0]
        count[0] += 1
        copies = []
        for m in range(3):
            cp = pltpu.make_async_remote_copy(
                src_ref=src_of(m),
                dst_ref=outs[m].at[blk],
                send_sem=send_sem.at[m, k],
                recv_sem=recv_sem.at[m, blk],
                device_id=dev,
                device_id_type=MESH_ID,
            )
            cp.start()
            copies.append(cp)
        return copies

    def wait_in(blk):
        for m in range(3):
            pltpu.make_async_remote_copy(
                src_ref=ins[m].at[0],
                dst_ref=outs[m].at[blk],
                send_sem=send_sem.at[m, 0],
                recv_sem=recv_sem.at[m, blk],
                device_id=partner,
                device_id_type=MESH_ID,
            ).wait_recv()

    sent = []
    local = []
    for m in range(3):
        cp = pltpu.make_async_copy(ins[m].at[h], outs[m].at[me], local_sem.at[m])
        cp.start()
        local.append(cp)
    sent += send(lambda m: ins[m].at[1 - h], me, z_peer)
    for dev in [partner] + x_devs:
        sent += send(lambda m: ins[m].at[h], me, dev)

    z_blk = block(x, 1 - h, c)
    wait_in(z_blk)
    for dev in [partner] + x_devs:
        sent += send(lambda m: outs[m].at[z_blk], z_blk, dev)

    for xp in x_peers:
        for hh in (h, 1 - h):
            blk = block(xp, hh, c)
            wait_in(blk)
            sent += send(lambda m: outs[m].at[blk], blk, partner)

    for xx in range(n_x):
        for hh in (0, 1):
            wait_in(block(xx, hh, 1 - c))

    for cp in sent:
        cp.wait_send()
    for cp in local:
        cp.wait()


def gather_weights(gate_weight, up_weight, down_weight, n_x):
    blk_rows, width = gate_weight.shape[1], gate_weight.shape[2]
    n_blocks = n_x * 4
    n_send = 1 + 2 * n_x + 2 * (n_x - 1)
    shape = jax.ShapeDtypeStruct((n_blocks, blk_rows, width), gate_weight.dtype)
    any_spec = pl.BlockSpec(memory_space=pl.ANY)
    nbytes = 3 * n_blocks * blk_rows * width * 2
    return pl.pallas_call(
        functools.partial(weight_kernel, n_x),
        out_shape=(shape, shape, shape),
        in_specs=[any_spec] * 3,
        out_specs=(any_spec, any_spec, any_spec),
        scratch_shapes=[
            pltpu.SemaphoreType.DMA((3, n_send)),
            pltpu.SemaphoreType.DMA((3, n_blocks)),
            pltpu.SemaphoreType.DMA((3,)),
        ],
        compiler_params=pltpu.CompilerParams(collective_id=0, has_side_effects=True),
        cost_estimate=pl.CostEstimate(flops=0, transcendentals=0, bytes_accessed=nbytes),
    )(gate_weight, up_weight, down_weight)


def per_device(tokens, expert_ids, combine, gate_weight, up_weight, down_weight):
    n_x = lax.axis_size("x")
    per_group = gate_weight.shape[0]
    groups = lax.axis_size("expert")
    n_expert = per_group * groups
    tok_rows, top_k = expert_ids.shape
    model_width = tokens.shape[1]

    g_all, u_all, d_all = gather_weights(gate_weight, up_weight, down_weight, n_x)
    gate_full = g_all.reshape(-1, model_width)
    up_full = u_all.reshape(-1, model_width)
    down_full = d_all.reshape(-1, model_width)

    flat_ids = expert_ids.reshape(-1)
    onehot = (flat_ids[:, None] == jnp.arange(n_expert, dtype=jnp.int32)[None, :]).astype(jnp.int32)
    earlier = jnp.cumsum(onehot, axis=0) - onehot
    rank_within = jnp.sum(earlier * onehot, axis=1)
    slot_index = flat_ids * CAP + rank_within
    source = jnp.arange(tok_rows * top_k, dtype=jnp.int32) // top_k
    outgoing = (
        jnp.zeros((n_expert * CAP, model_width), jnp.bfloat16).at[slot_index].set(tokens[source])
    )
    outgoing = outgoing.reshape(n_expert, CAP, model_width)
    arrived = lax.all_to_all(outgoing, ("expert", "zhi"), 0, 0, tiled=True)
    rows = arrived.reshape(n_expert * CAP, model_width)

    gate_pre = jnp.dot(rows, gate_full.T, preferred_element_type=jnp.float32)
    up_pre = jnp.dot(rows, up_full.T, preferred_element_type=jnp.float32)
    hidden = (jax.nn.silu(gate_pre) * up_pre).astype(jnp.bfloat16)
    produced = jnp.dot(hidden, down_full, preferred_element_type=jnp.float32).astype(jnp.bfloat16)
    produced = produced.reshape(n_expert, CAP, model_width)
    returned = lax.all_to_all(produced, ("expert", "zhi"), 0, 0, tiled=True)
    back_rows = returned.reshape(n_expert * CAP, model_width)[slot_index]
    weighted = back_rows.astype(jnp.float32).reshape(tok_rows, top_k, model_width) * combine[:, :, None]
    return jnp.sum(weighted, axis=1).astype(jnp.bfloat16)


def solution(mesh):
    groups = mesh.shape["expert"]
    n_x = mesh.shape["fsdp"] // 4
    inner = Mesh(mesh.devices.reshape(groups, n_x, 2, 2), ("expert", "x", "zhi", "core"))
    rows = P(("expert", "x", "zhi", "core"), None)
    weights = P("expert", ("x", "zhi", "core"), None)
    return jax.shard_map(
        per_device,
        mesh=inner,
        in_specs=(rows, rows, rows, weights, weights, weights),
        out_specs=rows,
        check_vma=False,
    )
```

time: 446 us -> 343 us (0.77); the launches traced: 438 us -> 341 us
  waiting for transfers between devices: 253 us -> 88.3 us
  Pallas kernels: 0 us -> 144 us
  blocking collectives: 71.9 us -> 0 us
  between operations: 13.3 us -> 0.15 us
  starting transfers between devices: 5.51 us -> 18.4 us
    all_gather x3 -> x0, waiting for transfers between devices: 189 us -> none  [gather_expert(): lax.all_gather(pair, 'chip', axis=0, tiled=True)]
    pallas_call x0 -> x1, Pallas kernels: none -> 144 us  [gather_weights(): pl.pallas_call(functools.partial(weight_kernel, n_x), out_shape=(shape, s...]
    all_to_all x1 -> x0, blocking collectives: 71.9 us -> none  [per_device(): arrived = lax.all_to_all(outgoing, ('expert', 'core'), 0, 0, tiled=True)]
    all_to_all x1 -> x2, waiting for transfers between devices: 59.4 us -> 88.3 us  [the longest x1 88.3 us: per_device(): returned = lax.all_to_all(produced, ('expert', 'zhi'), 0, 0, tiled=True)]
    all_to_all x1 -> x2, starting transfers between devices: 4.91 us -> 18.4 us  [the longest x1 10.3 us: per_device(): returned = lax.all_to_all(produced, ('expert', 'zhi'), 0, 0, tiled=True)]
    ppermute x3 -> x0, waiting for transfers between devices: 4.74 us -> none  [gather_expert(): got = lax.ppermute(other, 'core', [(0, 1), (1, 0)])]
  transfers between devices with their start and end apart: 7 -> 2, of which waited for: 7 -> 1; matrix products, arithmetic and copies ran while one was open for 10% -> 0% of each run, Pallas kernels for 0% -> 42%
where the time goes in v2:
time: 343 us; the launch traced here: 341 us
  Pallas kernels  144 us (42%)
  waiting for transfers between devices  88.3 us (26%)
  local copies, waits for them, and re-layouts  43.6 us (13%)
  matrix products  35.5 us (10%)
  starting transfers between devices  18.4 us (5%)
  other arithmetic  11.2 us (3%)
    pallas_call x1, Pallas kernels, gather_weights(): pl.pallas_call(functools.partial(weight_kernel, n_x), out_shape=(shape, s...  144 us
    all_to_all x1, waiting for transfers between devices, per_device(): returned = lax.all_to_all(produced, ('expert', 'zhi'), 0, 0, tiled=True)  88.3 us
    scatter x1, local copies, waits for them, and re-layouts, per_device(): jnp.zeros((n_expert * CAP, model_width), jnp.bfloat16).at[slot_index]  23.1 us
    dot_general x1, matrix products, per_device(): jnp.dot(hidden, down_full, preferred_element_type=jnp.float32)  22.7 us
    dot_general x1, matrix products, per_device(): gate_pre = jnp.dot(rows, gate_full.T, preferred_element_type=jnp.float32)  12.8 us
    gather x1, local copies, waits for them, and re-layouts, per_device(): back_rows = returned.reshape(n_expert * CAP, model_width)[slot_index]  11.7 us
    all_to_all x1, starting transfers between devices, per_device(): returned = lax.all_to_all(produced, ('expert', 'zhi'), 0, 0, tiled=True)  10.3 us
    reduce_sum x1, other arithmetic, per_device(): return jnp.sum(weighted, axis=1).astype(jnp.bfloat16)  8.2 us
  transfers between devices with their start and end apart: 2, of which 1 were waited for; matrix products, arithmetic and copies ran while one was open for 0% of the time, Pallas kernels for 42%

profile of v2, /device:TPU:2, one launch (start us, length us, event | category | flops | bytes accessed | tf_op | source)
XLA Modules:
  0.0 341.3 jit_solution(13914638159749026938)
XLA Ops:
  0.0 0.0 copy-start
  0.0 0.8 broadcast_multiply_fusion
  0.8 0.8 copy.9
  1.6 0.1 copy.8
  1.7 0.1 mul.36
  1.9 0.1 eq.22
  2.0 2.0 reduce-window.6
  4.0 0.3 slice_reduce_fusion
  4.3 0.1 bitcast_bitcast_fusion
  4.5 0.0 copy-done
  4.5 23.1 %scatter_custom_fusion = bf16[1152,2048]{1,0:T(8,128)(2,1)} fusion(s32[864]{0:T(1024)S(1)} %fusion.6, bf16[144,2048]{1,0:T(8,128)(2,1)S(1)} %copy-done, s32[1024]{0:T(1024)S(1)} %pad_clamp_fusion.1, bf16[]{:T(256)} %constant.11.clone.1), kind=kCustom, calls=%fused_computation.7 | custom fusion | bytes 4718594 | tf_op jit(solution)/shard_map/scatter | solution.py:139
  27.7 8.1 %all-to-all-start = ((bf16[16,72,2048]{2,1,0:T(8,128)(2,1)}), bf16[16,72,2048]{2,1,0:T(8,128)(2,1)}, u32[]{:S(2)}, u32[]{:S(2)}) async-start(bf16[16,72,2048]{2,1,0:T(8,128)(2,1)} %bitcast.34), calls=%async_computation | async-start | bytes 9437184 | tf_op jit(solution)/shard_map/all_to_all | solution.py:142
  35.8 144.2 %shard_map.64 = (bf16[16,88,2048]{2,1,0:T(8,128)(2,1)}, bf16[16,88,2048]{2,1,0:T(8,128)(2,1)}, bf16[16,88,2048]{2,1,0:T(8,128)(2,1)}) custom-call(bf16[2,88,2048]{2,1,0:T(8,128)(2,1)} %g_in.1, bf16[2,88,2048]{2,1,0:T(8,128)(2,1)} %u_in.1, bf16[2,88,2048]{2,1,0:T(8,128)(2,1)} %d_in.1), custom_call_target="tpu_custom_call" | custom-call | bytes 17301504 | tf_op jit(solution)/shard_map/pallas_call | solution.py:104
  180.0 0.0 all-to-all-done
  180.0 12.8 %fusion.8 = f32[1152,1408]{1,0:T(8,128)} fusion(bf16[1152,2048]{1,0:T(8,128)(2,1)} %bitcast.2, bf16[1408,2048]{1,0:T(8,128)(2,1)} %bitcast.39), kind=kOutput, calls=%fused_computation.31 | convolution fusion | flops 6643777536 | bytes 16973824 | tf_op jit(solution)/shard_map/dot_general | solution.py:145
  192.7 22.7 %convolution_convert_fusion = bf16[1152,2048]{1,0:T(8,128)(2,1)} fusion(bf16[1408,2048]{1,0:T(8,128)(2,1)} %bitcast.38, bf16[1152,2048]{1,0:T(8,128)(2,1)} %bitcast.2, bf16[1408,2048]{1,0:T(8,128)(2,1)} %bitcast.37, f32[1152,1408]{1,0:T(8,128)} %fusion.8), kind=kOutput, calls=%fused_computation.6 | convolution fusion | flops 13299646464 | bytes 27459584 | tf_op jit(solution)/shard_map/dot_general | solution.py:148
  215.5 0.0 copy-start.1
  215.5 10.3 %all-to-all-start.1 = ((bf16[16,72,2048]{2,1,0:T(8,128)(2,1)}), bf16[16,72,2048]{2,1,0:T(8,128)(2,1)}, u32[]{:S(2)}, u32[]{:S(2)}) async-start(bf16[16,72,2048]{2,1,0:T(8,128)(2,1)} %bitcast.35), calls=%async_computation.1 | async-start | bytes 9437184 | tf_op jit(solution)/shard_map/all_to_all | solution.py:150
  225.8 0.0 copy-done.1
  225.9 0.1 copy.12
  226.0 88.3 %all-to-all-done.1 = bf16[16,72,2048]{2,1,0:T(8,128)(2,1)} async-done(((bf16[16,72,2048]{2,1,0:T(8,128)(2,1)}), bf16[16,72,2048]{2,1,0:T(8,128)(2,1)}, u32[]{:S(2)}, u32[]{:S(2)}) %all-to-all-start.1) | async-done | bytes 4718624 | tf_op jit(solution)/shard_map/all_to_all | solution.py:150
  314.2 11.7 %gather_fusion = bf16[864,2048]{1,0:T(8,128)(2,1)} fusion(bf16[1152,2048]{1,0:T(8,128)(2,1)} %bitcast.7, s32[1024]{0:T(1024)S(1)} %pad_clamp_fusion), kind=kCustom, calls=%fused_computation.1 | custom fusion | bytes 7081344 | tf_op jit(solution)/shard_map/gather | solution.py:151
  325.9 7.1 %reshape.120 = f32[144,6,2048]{2,1,0:T(8,128)} reshape(bf16[864,2048]{1,0:T(8,128)(2,1)} %gather_fusion) | data formatting | bytes 10616832 | tf_op jit(solution)/shard_map/convert_element_type | solution.py:152
  333.1 8.2 %multiply_reduce_fusion = bf16[144,2048]{1,0:T(8,128)(2,1)} fusion(f32[144,6,2048]{2,1,0:T(8,128)} %reshape.120, f32[144,6]{1,0:T(8,128)S(1)} %copy.12), kind=kLoop, calls=%fused_computation.4 | loop fusion | flops 3244032 | bytes 7671168 | tf_op jit(solution)/shard_map/reduce_sum | solution.py:153
  (8 shorter events, 0.1 us)
Async XLA Ops:
  0.0 4.5 %copy-start = (bf16[144,2048]{1,0:T(8,128)(2,1)S(1)}, bf16[144,2048]{1,0:T(8,128)(2,1)}, u32[]{:S(2)}) copy-start(bf16[144,2048]{1,0:T(8,128)(2,1)} %param.6) | copy-start | bytes 1769476
  27.7 152.3 %all-to-all-start = ((bf16[16,72,2048]{2,1,0:T(8,128)(2,1)}), bf16[16,72,2048]{2,1,0:T(8,128)(2,1)}, u32[]{:S(2)}, u32[]{:S(2)}) async-start(bf16[16,72,2048]{2,1,0:T(8,128)(2,1)} %bitcast.34), calls=%async_computation | async-start | bytes 9437184 | tf_op jit(solution)/shard_map/all_to_all | solution.py:142
  215.5 10.4 %copy-start.1 = (f32[144,6]{0,1:T(8,128)S(1)}, f32[144,6]{0,1:T(8,128)}, u32[]{:S(2)}) copy-start(f32[144,6]{0,1:T(8,128)} %param.8) | copy-start | bytes 10372
  215.5 98.7 %all-to-all-start.1 = ((bf16[16,72,2048]{2,1,0:T(8,128)(2,1)}), bf16[16,72,2048]{2,1,0:T(8,128)(2,1)}, u32[]{:S(2)}, u32[]{:S(2)}) async-start(bf16[16,72,2048]{2,1,0:T(8,128)(2,1)} %bitcast.35), calls=%async_computation.1 | async-start | bytes 9437184 | tf_op jit(solution)/shard_map/all_to_all | solution.py:150

commit v3 on v2

--- a/solution.py
+++ b/solution.py
@@ -12,7 +12,77 @@
 MESH_ID = pl.DeviceIdType.MESH
 
 
-def weight_kernel(n_x, g_in, u_in, d_in, g_out, u_out, d_out, send_sem, recv_sem, local_sem):
+def exchange_peers(n_grp):
+    me = lax.axis_index("expert") * 2 + lax.axis_index("zhi")
+    peers = []
+    for s in range(1, n_grp):
+        p = lax.rem(me + s, n_grp)
+        peers.append((p, {"expert": p // 2, "zhi": lax.rem(p, 2)}))
+    return me, peers
+
+
+def start_exchange(me, peers, x_ref, y_ref, send_sem, recv_sem, local_sem):
+    copies = []
+    local = pltpu.make_async_copy(x_ref.at[me], y_ref.at[me], local_sem)
+    local.start()
+    for k, (p, dev) in enumerate(peers):
+        cp = pltpu.make_async_remote_copy(
+            src_ref=x_ref.at[p],
+            dst_ref=y_ref.at[me],
+            send_sem=send_sem.at[k],
+            recv_sem=recv_sem.at[me],
+            device_id=dev,
+            device_id_type=MESH_ID,
+        )
+        cp.start()
+        copies.append(cp)
+    return local, copies
+
+
+def finish_exchange(peers, local, copies, x_ref, y_ref, send_sem, recv_sem):
+    for k, (p, dev) in enumerate(peers):
+        pltpu.make_async_remote_copy(
+            src_ref=x_ref.at[0],
+            dst_ref=y_ref.at[p],
+            send_sem=send_sem.at[k],
+            recv_sem=recv_sem.at[p],
+            device_id=dev,
+            device_id_type=MESH_ID,
+        ).wait_recv()
+    for cp in copies:
+        cp.wait_send()
+    local.wait()
+
+
+def exchange_kernel(n_grp, x_ref, y_ref, send_sem, recv_sem, local_sem):
+    me, peers = exchange_peers(n_grp)
+    barrier = pltpu.get_barrier_semaphore()
+    for p, dev in peers:
+        pl.semaphore_signal(barrier, inc=1, device_id=dev, device_id_type=MESH_ID)
+    pl.semaphore_wait(barrier, len(peers))
+    local, copies = start_exchange(me, peers, x_ref, y_ref, send_sem, recv_sem, local_sem.at[0])
+    finish_exchange(peers, local, copies, x_ref, y_ref, send_sem, recv_sem)
+
+
+def exchange(x, n_grp, collective_id):
+    any_spec = pl.BlockSpec(memory_space=pl.ANY)
+    return pl.pallas_call(
+        functools.partial(exchange_kernel, n_grp),
+        out_shape=jax.ShapeDtypeStruct(x.shape, x.dtype),
+        in_specs=[any_spec],
+        out_specs=any_spec,
+        scratch_shapes=[
+            pltpu.SemaphoreType.DMA((n_grp,)),
+            pltpu.SemaphoreType.DMA((n_grp,)),
+            pltpu.SemaphoreType.DMA((1,)),
+        ],
+        compiler_params=pltpu.CompilerParams(collective_id=collective_id, has_side_effects=True),
+        cost_estimate=pl.CostEstimate(flops=0, transcendentals=0, bytes_accessed=2 * x.size * 2),
+    )(x)
+
+
+def weight_kernel(n_x, n_grp, g_in, u_in, d_in, t_in, g_out, u_out, d_out, t_out, send_sem, recv_sem,
+                  local_sem, t_send, t_recv):
     ins = (g_in, u_in, d_in)
     outs = (g_out, u_out, d_out)
     x = lax.axis_index("x")
@@ -28,10 +98,13 @@
     z_peer = {"zhi": 1 - h}
     x_devs = [{"x": xp} for xp in x_peers]
 
+    t_me, t_peers = exchange_peers(n_grp)
     barrier = pltpu.get_barrier_semaphore()
-    for dev in [partner, z_peer] + x_devs:
+    greet = [partner] + x_devs + [dev for p, dev in t_peers]
+    for dev in greet:
         pl.semaphore_signal(barrier, inc=1, device_id=dev, device_id_type=MESH_ID)
-    pl.semaphore_wait(barrier, 2 + len(x_devs))
+    pl.semaphore_wait(barrier, len(greet))
+    t_local, t_copies = start_exchange(t_me, t_peers, t_in, t_out, t_send, t_recv, local_sem.at[3])
 
     count = [0]
 
@@ -92,9 +165,10 @@
         cp.wait_send()
     for cp in local:
         cp.wait()
-
-
-def gather_weights(gate_weight, up_weight, down_weight, n_x):
+    finish_exchange(t_peers, t_local, t_copies, t_in, t_out, t_send, t_recv)
+
+
+def gather_weights(gate_weight, up_weight, down_weight, outgoing, n_x, n_grp):
     blk_rows, width = gate_weight.shape[1], gate_weight.shape[2]
     n_blocks = n_x * 4
     n_send = 1 + 2 * n_x + 2 * (n_x - 1)
@@ -102,18 +176,20 @@
     any_spec = pl.BlockSpec(memory_space=pl.ANY)
     nbytes = 3 * n_blocks * blk_rows * width * 2
     return pl.pallas_call(
-        functools.partial(weight_kernel, n_x),
-        out_shape=(shape, shape, shape),
-        in_specs=[any_spec] * 3,
-        out_specs=(any_spec, any_spec, any_spec),
+        functools.partial(weight_kernel, n_x, n_grp),
+        out_shape=(shape, shape, shape, jax.ShapeDtypeStruct(outgoing.shape, outgoing.dtype)),
+        in_specs=[any_spec] * 4,
+        out_specs=(any_spec, any_spec, any_spec, any_spec),
         scratch_shapes=[
             pltpu.SemaphoreType.DMA((3, n_send)),
             pltpu.SemaphoreType.DMA((3, n_blocks)),
-            pltpu.SemaphoreType.DMA((3,)),
+            pltpu.SemaphoreType.DMA((4,)),
+            pltpu.SemaphoreType.DMA((n_grp,)),
+            pltpu.SemaphoreType.DMA((n_grp,)),
         ],
         compiler_params=pltpu.CompilerParams(collective_id=0, has_side_effects=True),
         cost_estimate=pl.CostEstimate(flops=0, transcendentals=0, bytes_accessed=nbytes),
-    )(gate_weight, up_weight, down_weight)
+    )(gate_weight, up_weight, down_weight, outgoing)
 
 
 def per_device(tokens, expert_ids, combine, gate_weight, up_weight, down_weight):
@@ -121,36 +197,45 @@
     per_group = gate_weight.shape[0]
     groups = lax.axis_size("expert")
     n_expert = per_group * groups
+    n_grp = groups * 2
     tok_rows, top_k = expert_ids.shape
     model_width = tokens.shape[1]
-
-    g_all, u_all, d_all = gather_weights(gate_weight, up_weight, down_weight, n_x)
-    gate_full = g_all.reshape(-1, model_width)
-    up_full = u_all.reshape(-1, model_width)
-    down_full = d_all.reshape(-1, model_width)
+    n_slot = n_expert * CAP
 
     flat_ids = expert_ids.reshape(-1)
     onehot = (flat_ids[:, None] == jnp.arange(n_expert, dtype=jnp.int32)[None, :]).astype(jnp.int32)
     earlier = jnp.cumsum(onehot, axis=0) - onehot
     rank_within = jnp.sum(earlier * onehot, axis=1)
-    slot_index = flat_ids * CAP + rank_within
-    source = jnp.arange(tok_rows * top_k, dtype=jnp.int32) // top_k
-    outgoing = (
-        jnp.zeros((n_expert * CAP, model_width), jnp.bfloat16).at[slot_index].set(tokens[source])
+    slot_index = (flat_ids * CAP + rank_within).reshape(tok_rows, top_k)
+    hit = slot_index[None, :, :] == jnp.arange(n_slot, dtype=jnp.int32)[:, None, None]
+    pick = jnp.any(hit, axis=2).astype(jnp.bfloat16)
+    outgoing = jnp.dot(pick, tokens, preferred_element_type=jnp.float32).astype(jnp.bfloat16)
+    outgoing = outgoing.reshape(n_expert, CAP, model_width)
+
+    g_all, u_all, d_all, arrived = gather_weights(
+        gate_weight, up_weight, down_weight, outgoing, n_x, n_grp
     )
-    outgoing = outgoing.reshape(n_expert, CAP, model_width)
-    arrived = lax.all_to_all(outgoing, ("expert", "zhi"), 0, 0, tiled=True)
-    rows = arrived.reshape(n_expert * CAP, model_width)
+    gate_full = g_all.reshape(-1, model_width)
+    up_full = u_all.reshape(-1, model_width)
+    down_full = d_all.reshape(-1, model_width)
+    rows = arrived.reshape(n_slot, model_width)
 
     gate_pre = jnp.dot(rows, gate_full.T, preferred_element_type=jnp.float32)
     up_pre = jnp.dot(rows, up_full.T, preferred_element_type=jnp.float32)
     hidden = (jax.nn.silu(gate_pre) * up_pre).astype(jnp.bfloat16)
     produced = jnp.dot(hidden, down_full, preferred_element_type=jnp.float32).astype(jnp.bfloat16)
     produced = produced.reshape(n_expert, CAP, model_width)
-    returned = lax.all_to_all(produced, ("expert", "zhi"), 0, 0, tiled=True)
-    back_rows = returned.reshape(n_expert * CAP, model_width)[slot_index]
-    weighted = back_rows.astype(jnp.float32).reshape(tok_rows, top_k, model_width) * combine[:, :, None]
-    return jnp.sum(weighted, axis=1).astype(jnp.bfloat16)
+    returned = exchange(produced, n_grp, 1).reshape(n_slot, model_width)
+
+    weight_of = jnp.sum(
+        jnp.where(hit, combine[None, :, :], jnp.zeros_like(combine)[None, :, :]), axis=2
+    ).T
+    weight_hi = weight_of.astype(jnp.bfloat16)
+    weight_lo = (weight_of - weight_hi.astype(jnp.float32)).astype(jnp.bfloat16)
+    mixed = jnp.dot(weight_hi, returned, preferred_element_type=jnp.float32) + jnp.dot(
+        weight_lo, returned, preferred_element_type=jnp.float32
+    )
+    return mixed.astype(jnp.bfloat16)
 
 
 def solution(mesh):

time: 343 us -> 318 us (0.927)
  the two profiles are of different devices: /device:TPU:2 before, /device:TPU:112 now
where the time goes in v3:
time: 318 us
  Pallas kernels  268 us (84%)
  matrix products  44.6 us (14%)
  other arithmetic  4.03 us (1%)
    pallas_call x1, Pallas kernels, exchange(): pl.pallas_call(functools.partial(exchange_kernel, n_grp), out_shape=jax.S...  144 us
    pallas_call x1, Pallas kernels, gather_weights(): pl.pallas_call(functools.partial(weight_kernel, n_x, n_grp), out_shape=(s...  124 us
    dot_general x1, matrix products, per_device(): jnp.dot(hidden, down_full, preferred_element_type=jnp.float32)  22.8 us
    dot_general x1, matrix products, per_device(): gate_pre = jnp.dot(rows, gate_full.T, preferred_element_type=jnp.float32)  12.8 us

profile of v3, /device:TPU:112, one launch (start us, length us, event | category | flops | bytes accessed | tf_op | source)
XLA Modules:
  0.0 318.0 jit_solution(2811711104897987396)
XLA Ops:
  0.0 0.0 copy-start
  0.0 0.9 copy.21
  0.9 0.1 eq.35
  1.0 2.0 reduce-window.6
  3.0 0.3 slice_reduce_fusion
  3.4 0.1 bitcast_bitcast_fusion
  3.5 0.1 reduce_sum.21
  3.6 0.1 copy.24
  3.7 0.7 multiply_add_fusion
  4.4 0.6 fusion.1
  5.0 0.0 copy-done
  5.1 3.6 %convolution_convert_fusion.1 = bf16[1152,2048]{1,0:T(8,128)(2,1)} fusion(pred[1152,144]{0,1:T(8,128)(4,1)S(1)} %fusion.1, bf16[144,2048]{1,0:T(8,128)(2,1)S(1)} %copy-done), kind=kOutput, calls=%fused_computation.3 | convolution fusion | flops 681836544 | bytes 5474304 | tf_op jit(solution)/shard_map/dot_general | solution.py:212
  8.7 124.3 %shard_map.64 = (bf16[16,88,2048]{2,1,0:T(8,128)(2,1)}, bf16[16,88,2048]{2,1,0:T(8,128)(2,1)}, bf16[16,88,2048]{2,1,0:T(8,128)(2,1)}, bf16[16,72,2048]{2,1,0:T(8,128)(2,1)}) custom-call(bf16[2,88,2048]{2,1,0:T(8,128)(2,1)} %g_in.1, bf16[2,88,2048]{2,1,0:T(8,128)(2,1)} %u_in.1, bf16[2,88,2048]{2,1,0:T(8,128)(2,1)} %d_in.1, bf16[16,72,2048]{2,1,0:T(8,128)(2,1)} %bitcast.59), custom_call_target="tpu_custom_call" | custom-call | bytes 17301504 | tf_op jit(solution)/shard_map/pallas_call | solution.py:178
  133.0 12.8 %fusion.12 = f32[1152,1408]{1,0:T(8,128)} fusion(bf16[1152,2048]{1,0:T(8,128)(2,1)} %bitcast.65, bf16[1408,2048]{1,0:T(8,128)(2,1)} %bitcast.64), kind=kOutput, calls=%fused_computation.26 | convolution fusion | flops 6643777536 | bytes 16973824 | tf_op jit(solution)/shard_map/dot_general | solution.py:223
  145.8 22.8 %convolution_convert_fusion = bf16[1152,2048]{1,0:T(8,128)(2,1)} fusion(bf16[1408,2048]{1,0:T(8,128)(2,1)} %bitcast.63, bf16[1152,2048]{1,0:T(8,128)(2,1)} %bitcast.66, bf16[1408,2048]{1,0:T(8,128)(2,1)} %bitcast.62, f32[1152,1408]{1,0:T(8,128)} %fusion.12), kind=kOutput, calls=%fused_computation.2 | convolution fusion | flops 13299646464 | bytes 27459584 | tf_op jit(solution)/shard_map/dot_general | solution.py:226
  168.5 0.0 copy-start.2
  168.5 143.5 %shard_map.65 = bf16[16,72,2048]{2,1,0:T(8,128)(2,1)} custom-call(bf16[16,72,2048]{2,1,0:T(8,128)(2,1)} %bitcast.60), custom_call_target="tpu_custom_call" | custom-call | bytes 9437184 | tf_op jit(solution)/shard_map/pallas_call | solution.py:69
  312.0 0.0 copy-start.1
  312.0 0.0 copy-done.2
  312.1 0.5 select_reduce_fusion
  312.6 3.6 %fusion.9 = f32[144,2048]{1,0:T(8,128)S(1)} fusion(bf16[1152,2048]{1,0:T(8,128)(2,1)} %bitcast.57, f32[1152,144]{0,1:T(8,128)S(1)} %select_reduce_fusion), kind=kOutput, calls=%fused_computation.24 | convolution fusion | flops 679477248 | bytes 6561792 | tf_op jit(solution)/shard_map/dot_general | solution.py:235
  316.2 0.0 copy-done.1
  316.2 1.8 fusion.2
  (4 shorter events, 0.1 us)
Async XLA Ops:
  0.0 5.0 %copy-start = (bf16[144,2048]{1,0:T(8,128)(2,1)S(1)}, bf16[144,2048]{1,0:T(8,128)(2,1)}, u32[]{:S(2)}) copy-start(bf16[144,2048]{1,0:T(8,128)(2,1)} %param.6) | copy-start | bytes 1769476
  168.5 143.5 %copy-start.2 = (f32[144,6]{0,1:T(8,128)S(1)}, f32[144,6]{0,1:T(8,128)}, u32[]{:S(2)}) copy-start(f32[144,6]{0,1:T(8,128)} %param.8) | copy-start | bytes 10372
  312.0 4.1 %copy-start.1 = (bf16[16,72,2048]{2,1,0:T(8,128)(2,1)S(1)}, bf16[16,72,2048]{2,1,0:T(8,128)(2,1)}, u32[]{:S(2)}) copy-start(bf16[16,72,2048]{2,1,0:T(8,128)(2,1)} %shard_map.65) | copy-start | bytes 14155780

commit v4 on v3

--- a/solution.py
+++ b/solution.py
@@ -93,10 +93,14 @@
         return (xx * 2 + hh) * 2 + cc
 
     me = block(x, h, c)
-    x_peers = [lax.rem(x + s, n_x) for s in range(1, n_x)]
+    up_x = lax.rem(x + 1, n_x)
+    down_x = lax.rem(x + n_x - 1, n_x)
+    far_x = lax.rem(x + 2, n_x)
+    toward = jnp.where(c == 0, up_x, down_x)
+    away = jnp.where(c == 0, down_x, up_x)
     partner = {"core": 1 - c}
     z_peer = {"zhi": 1 - h}
-    x_devs = [{"x": xp} for xp in x_peers]
+    x_devs = [{"x": up_x}, {"x": down_x}]
 
     t_me, t_peers = exchange_peers(n_grp)
     barrier = pltpu.get_barrier_semaphore()
@@ -151,7 +155,12 @@
     for dev in [partner] + x_devs:
         sent += send(lambda m: outs[m].at[z_blk], z_blk, dev)
 
-    for xp in x_peers:
+    for hh in (h, 1 - h):
+        blk = block(away, hh, c)
+        wait_in(blk)
+        sent += send(lambda m: outs[m].at[blk], blk, partner)
+        sent += send(lambda m: outs[m].at[blk], blk, {"x": toward})
+    for xp in (toward, far_x):
         for hh in (h, 1 - h):
             blk = block(xp, hh, c)
             wait_in(blk)
@@ -171,7 +180,7 @@
 def gather_weights(gate_weight, up_weight, down_weight, outgoing, n_x, n_grp):
     blk_rows, width = gate_weight.shape[1], gate_weight.shape[2]
     n_blocks = n_x * 4
-    n_send = 1 + 2 * n_x + 2 * (n_x - 1)
+    n_send = 16
     shape = jax.ShapeDtypeStruct((n_blocks, blk_rows, width), gate_weight.dtype)
     any_spec = pl.BlockSpec(memory_space=pl.ANY)
     nbytes = 3 * n_blocks * blk_rows * width * 2
@@ -194,6 +203,7 @@
 
 def per_device(tokens, expert_ids, combine, gate_weight, up_weight, down_weight):
     n_x = lax.axis_size("x")
+    assert n_x == 4
     per_group = gate_weight.shape[0]
     groups = lax.axis_size("expert")
     n_expert = per_group * groups
@@ -230,8 +240,9 @@
     weight_of = jnp.sum(
         jnp.where(hit, combine[None, :, :], jnp.zeros_like(combine)[None, :, :]), axis=2
     ).T
-    weight_hi = weight_of.astype(jnp.bfloat16)
-    weight_lo = (weight_of - weight_hi.astype(jnp.float32)).astype(jnp.bfloat16)
+    weight_top = lax.reduce_precision(weight_of, exponent_bits=8, mantissa_bits=7)
+    weight_hi = weight_top.astype(jnp.bfloat16)
+    weight_lo = (weight_of - weight_top).astype(jnp.bfloat16)
     mixed = jnp.dot(weight_hi, returned, preferred_element_type=jnp.float32) + jnp.dot(
         weight_lo, returned, preferred_element_type=jnp.float32
     )

time: 318 us -> 313 us (0.984)
  Pallas kernels: 268 us -> 263 us
    pallas_call x1, Pallas kernels: 124 us -> 119 us  [gather_weights(): pl.pallas_call(functools.partial(weight_kernel, n_x, n_grp), out_shape=(s...]
where the time goes in v4:
time: 313 us
  Pallas kernels  263 us (84%)
  matrix products  44.6 us (14%)
  other arithmetic  4.03 us (1%)
    pallas_call x1, Pallas kernels, exchange(): pl.pallas_call(functools.partial(exchange_kernel, n_grp), out_shape=jax.S...  144 us
    pallas_call x1, Pallas kernels, gather_weights(): pl.pallas_call(functools.partial(weight_kernel, n_x, n_grp), out_shape=(s...  119 us
    dot_general x1, matrix products, per_device(): jnp.dot(hidden, down_full, preferred_element_type=jnp.float32)  22.7 us
    dot_general x1, matrix products, per_device(): gate_pre = jnp.dot(rows, gate_full.T, preferred_element_type=jnp.float32)  12.8 us

profile of v4, /device:TPU:112, one launch (start us, length us, event | category | flops | bytes accessed | tf_op | source)
XLA Modules:
  0.0 313.0 jit_solution(1715388377219006617)
XLA Ops:
  0.0 0.0 copy-start
  0.0 0.9 copy.21
  0.9 0.1 eq.35
  1.0 2.0 reduce-window.6
  3.0 0.3 slice_reduce_fusion
  3.4 0.1 bitcast_bitcast_fusion
  3.5 0.1 reduce_sum.21
  3.6 0.1 copy.24
  3.7 0.7 multiply_add_fusion
  4.4 0.6 fusion.1
  5.0 0.0 copy-done
  5.1 3.6 %convolution_convert_fusion.1 = bf16[1152,2048]{1,0:T(8,128)(2,1)} fusion(pred[1152,144]{0,1:T(8,128)(4,1)S(1)} %fusion.1, bf16[144,2048]{1,0:T(8,128)(2,1)S(1)} %copy-done), kind=kOutput, calls=%fused_computation.3 | convolution fusion | flops 681836544 | bytes 5474304 | tf_op jit(solution)/shard_map/dot_general | solution.py:222
  8.7 119.3 %shard_map.64 = (bf16[16,88,2048]{2,1,0:T(8,128)(2,1)}, bf16[16,88,2048]{2,1,0:T(8,128)(2,1)}, bf16[16,88,2048]{2,1,0:T(8,128)(2,1)}, bf16[16,72,2048]{2,1,0:T(8,128)(2,1)}) custom-call(bf16[2,88,2048]{2,1,0:T(8,128)(2,1)} %g_in.1, bf16[2,88,2048]{2,1,0:T(8,128)(2,1)} %u_in.1, bf16[2,88,2048]{2,1,0:T(8,128)(2,1)} %d_in.1, bf16[16,72,2048]{2,1,0:T(8,128)(2,1)} %bitcast.45), custom_call_target="tpu_custom_call" | custom-call | bytes 17301504 | tf_op jit(solution)/shard_map/pallas_call | solution.py:187
  128.0 12.8 %fusion.8 = f32[1152,1408]{1,0:T(8,128)} fusion(bf16[1152,2048]{1,0:T(8,128)(2,1)} %bitcast.51, bf16[1408,2048]{1,0:T(8,128)(2,1)} %bitcast.50), kind=kOutput, calls=%fused_computation.24 | convolution fusion | flops 6643777536 | bytes 16973824 | tf_op jit(solution)/shard_map/dot_general | solution.py:233
  140.8 22.7 %convolution_convert_fusion = bf16[1152,2048]{1,0:T(8,128)(2,1)} fusion(bf16[1408,2048]{1,0:T(8,128)(2,1)} %bitcast.49, bf16[1152,2048]{1,0:T(8,128)(2,1)} %bitcast.52, bf16[1408,2048]{1,0:T(8,128)(2,1)} %bitcast.48, f32[1152,1408]{1,0:T(8,128)} %fusion.8), kind=kOutput, calls=%fused_computation.2 | convolution fusion | flops 13299646464 | bytes 27459584 | tf_op jit(solution)/shard_map/dot_general | solution.py:236
  163.5 0.0 copy-start.2
  163.5 143.5 %shard_map.65 = bf16[16,72,2048]{2,1,0:T(8,128)(2,1)} custom-call(bf16[16,72,2048]{2,1,0:T(8,128)(2,1)} %bitcast.46), custom_call_target="tpu_custom_call" | custom-call | bytes 9437184 | tf_op jit(solution)/shard_map/pallas_call | solution.py:69
  307.0 0.0 copy-start.1
  307.1 0.0 copy-done.2
  307.1 0.5 select_reduce_fusion
  307.6 3.6 %fusion.5 = f32[144,2048]{1,0:T(8,128)S(1)} fusion(bf16[1152,2048]{1,0:T(8,128)(2,1)} %bitcast.43, f32[1152,144]{0,1:T(8,128)S(1)} %select_reduce_fusion), kind=kOutput, calls=%fused_computation.12 | convolution fusion | flops 679809024 | bytes 6561792 | tf_op jit(solution)/shard_map/dot_general | solution.py:246
  311.2 0.0 copy-done.1
  311.2 1.8 fusion.2
  (4 shorter events, 0.1 us)
Async XLA Ops:
  0.0 5.0 %copy-start = (bf16[144,2048]{1,0:T(8,128)(2,1)S(1)}, bf16[144,2048]{1,0:T(8,128)(2,1)}, u32[]{:S(2)}) copy-start(bf16[144,2048]{1,0:T(8,128)(2,1)} %param.6) | copy-start | bytes 1769476
  163.5 143.5 %copy-start.2 = (f32[144,6]{0,1:T(8,128)S(1)}, f32[144,6]{0,1:T(8,128)}, u32[]{:S(2)}) copy-start(f32[144,6]{0,1:T(8,128)} %param.8) | copy-start | bytes 10372
  307.0 4.1 %copy-start.1 = (bf16[16,72,2048]{2,1,0:T(8,128)(2,1)S(1)}, bf16[16,72,2048]{2,1,0:T(8,128)(2,1)}, u32[]{:S(2)}) copy-start(bf16[16,72,2048]{2,1,0:T(8,128)(2,1)} %shard_map.65) | copy-start | bytes 14155780

commit v5 on v4

--- a/solution.py
+++ b/solution.py
@@ -108,7 +108,6 @@
     for dev in greet:
         pl.semaphore_signal(barrier, inc=1, device_id=dev, device_id_type=MESH_ID)
     pl.semaphore_wait(barrier, len(greet))
-    t_local, t_copies = start_exchange(t_me, t_peers, t_in, t_out, t_send, t_recv, local_sem.at[3])
 
     count = [0]
 
@@ -149,6 +148,7 @@
     sent += send(lambda m: ins[m].at[1 - h], me, z_peer)
     for dev in [partner] + x_devs:
         sent += send(lambda m: ins[m].at[h], me, dev)
+    t_local, t_copies = start_exchange(t_me, t_peers, t_in, t_out, t_send, t_recv, local_sem.at[3])
 
     z_blk = block(x, 1 - h, c)
     wait_in(z_blk)

time: 313 us -> 300 us (0.958)
  Pallas kernels: 263 us -> 250 us
    pallas_call x1, Pallas kernels: 119 us -> 106 us  [gather_weights(): pl.pallas_call(functools.partial(weight_kernel, n_x, n_grp), out_shape=(s...]
where the time goes in v5:
time: 300 us
  Pallas kernels  250 us (83%)
  matrix products  44.6 us (15%)
  other arithmetic  4.03 us (1%)
    pallas_call x1, Pallas kernels, exchange(): pl.pallas_call(functools.partial(exchange_kernel, n_grp), out_shape=jax.S...  144 us
    pallas_call x1, Pallas kernels, gather_weights(): pl.pallas_call(functools.partial(weight_kernel, n_x, n_grp), out_shape=(s...  106 us
    dot_general x1, matrix products, per_device(): jnp.dot(hidden, down_full, preferred_element_type=jnp.float32)  22.8 us
    dot_general x1, matrix products, per_device(): gate_pre = jnp.dot(rows, gate_full.T, preferred_element_type=jnp.float32)  12.8 us

profile of v5, /device:TPU:112, one launch (start us, length us, event | category | flops | bytes accessed | tf_op | source)
XLA Modules:
  0.0 300.3 jit_solution(9685122128578749712)
XLA Ops:
  0.0 0.0 copy-start
  0.0 0.9 copy.21
  0.9 0.1 eq.35
  1.0 2.0 reduce-window.6
  3.0 0.3 slice_reduce_fusion
  3.4 0.1 bitcast_bitcast_fusion
  3.5 0.1 reduce_sum.21
  3.6 0.1 copy.24
  3.7 0.7 multiply_add_fusion
  4.4 0.6 fusion.1
  5.0 0.0 copy-done
  5.1 3.6 %convolution_convert_fusion.1 = bf16[1152,2048]{1,0:T(8,128)(2,1)} fusion(pred[1152,144]{0,1:T(8,128)(4,1)S(1)} %fusion.1, bf16[144,2048]{1,0:T(8,128)(2,1)S(1)} %copy-done), kind=kOutput, calls=%fused_computation.3 | convolution fusion | flops 681836544 | bytes 5474304 | tf_op jit(solution)/shard_map/dot_general | solution.py:222
  8.7 105.7 %shard_map.64 = (bf16[16,88,2048]{2,1,0:T(8,128)(2,1)}, bf16[16,88,2048]{2,1,0:T(8,128)(2,1)}, bf16[16,88,2048]{2,1,0:T(8,128)(2,1)}, bf16[16,72,2048]{2,1,0:T(8,128)(2,1)}) custom-call(bf16[2,88,2048]{2,1,0:T(8,128)(2,1)} %g_in.1, bf16[2,88,2048]{2,1,0:T(8,128)(2,1)} %u_in.1, bf16[2,88,2048]{2,1,0:T(8,128)(2,1)} %d_in.1, bf16[16,72,2048]{2,1,0:T(8,128)(2,1)} %bitcast.45), custom_call_target="tpu_custom_call" | custom-call | bytes 17301504 | tf_op jit(solution)/shard_map/pallas_call | solution.py:187
  114.4 12.8 %fusion.8 = f32[1152,1408]{1,0:T(8,128)} fusion(bf16[1152,2048]{1,0:T(8,128)(2,1)} %bitcast.51, bf16[1408,2048]{1,0:T(8,128)(2,1)} %bitcast.50), kind=kOutput, calls=%fused_computation.24 | convolution fusion | flops 6643777536 | bytes 16973824 | tf_op jit(solution)/shard_map/dot_general | solution.py:233
  127.2 22.8 %convolution_convert_fusion = bf16[1152,2048]{1,0:T(8,128)(2,1)} fusion(bf16[1408,2048]{1,0:T(8,128)(2,1)} %bitcast.49, bf16[1152,2048]{1,0:T(8,128)(2,1)} %bitcast.52, bf16[1408,2048]{1,0:T(8,128)(2,1)} %bitcast.48, f32[1152,1408]{1,0:T(8,128)} %fusion.8), kind=kOutput, calls=%fused_computation.2 | convolution fusion | flops 13299646464 | bytes 27459584 | tf_op jit(solution)/shard_map/dot_general | solution.py:236
  149.9 0.0 copy-start.2
  149.9 144.4 %shard_map.65 = bf16[16,72,2048]{2,1,0:T(8,128)(2,1)} custom-call(bf16[16,72,2048]{2,1,0:T(8,128)(2,1)} %bitcast.46), custom_call_target="tpu_custom_call" | custom-call | bytes 9437184 | tf_op jit(solution)/shard_map/pallas_call | solution.py:69
  294.3 0.0 copy-start.1
  294.4 0.0 copy-done.2
  294.4 0.5 select_reduce_fusion
  294.9 3.6 %fusion.5 = f32[144,2048]{1,0:T(8,128)S(1)} fusion(bf16[1152,2048]{1,0:T(8,128)(2,1)} %bitcast.43, f32[1152,144]{0,1:T(8,128)S(1)} %select_reduce_fusion), kind=kOutput, calls=%fused_computation.12 | convolution fusion | flops 679809024 | bytes 6561792 | tf_op jit(solution)/shard_map/dot_general | solution.py:246
  298.5 0.0 copy-done.1
  298.5 1.8 fusion.2
  (4 shorter events, 0.1 us)
Async XLA Ops:
  0.0 5.0 %copy-start = (bf16[144,2048]{1,0:T(8,128)(2,1)S(1)}, bf16[144,2048]{1,0:T(8,128)(2,1)}, u32[]{:S(2)}) copy-start(bf16[144,2048]{1,0:T(8,128)(2,1)} %param.6) | copy-start | bytes 1769476
  149.9 144.4 %copy-start.2 = (f32[144,6]{0,1:T(8,128)S(1)}, f32[144,6]{0,1:T(8,128)}, u32[]{:S(2)}) copy-start(f32[144,6]{0,1:T(8,128)} %param.8) | copy-start | bytes 10372
  294.3 4.1 %copy-start.1 = (bf16[16,72,2048]{2,1,0:T(8,128)(2,1)S(1)}, bf16[16,72,2048]{2,1,0:T(8,128)(2,1)}, u32[]{:S(2)}) copy-start(bf16[16,72,2048]{2,1,0:T(8,128)(2,1)} %shard_map.65) | copy-start | bytes 14155780

commit v6 on v5

--- a/solution.py
+++ b/solution.py
@@ -81,6 +81,89 @@
     )(x)
 
 
+def down_return_kernel(n_grp, hid_ref, down_ref, y_ref, buf, send_sem, recv_sem, local_sem):
+    me, peers = exchange_peers(n_grp)
+    barrier = pltpu.get_barrier_semaphore()
+    for p, dev in peers:
+        pl.semaphore_signal(barrier, inc=1, device_id=dev, device_id_type=MESH_ID)
+
+    def project(k):
+        p = lax.rem(me + k, n_grp)
+        buf[p] = jnp.dot(hid_ref[p], down_ref[...], preferred_element_type=jnp.float32).astype(
+            buf.dtype
+        )
+
+    def remote(k):
+        p = lax.rem(me + k, n_grp)
+        return pltpu.make_async_remote_copy(
+            src_ref=buf.at[p],
+            dst_ref=y_ref.at[me],
+            send_sem=send_sem.at[k],
+            recv_sem=recv_sem.at[me],
+            device_id={"expert": p // 2, "zhi": lax.rem(p, 2)},
+            device_id_type=MESH_ID,
+        )
+
+    local = pltpu.make_async_copy(buf.at[me], y_ref.at[me], local_sem.at[0])
+    project(0)
+    pl.semaphore_wait(barrier, len(peers))
+
+    def step(k, carry):
+        project(k)
+
+        @pl.when(k == 1)
+        def _():
+            local.start()
+
+        @pl.when(k >= 2)
+        def _():
+            remote(k - 1).start()
+
+        return carry
+
+    lax.fori_loop(1, n_grp, step, 0)
+    remote(n_grp - 1).start()
+
+    local.wait()
+    for k in range(1, n_grp):
+        remote(k).wait_send()
+    for p, dev in peers:
+        pltpu.make_async_remote_copy(
+            src_ref=buf.at[0],
+            dst_ref=y_ref.at[p],
+            send_sem=send_sem.at[0],
+            recv_sem=recv_sem.at[p],
+            device_id=dev,
+            device_id_type=MESH_ID,
+        ).wait_recv()
+
+
+def down_return(hidden, down_full, n_grp, collective_id):
+    n_src, rows, _ = hidden.shape
+    width = down_full.shape[1]
+    out = jax.ShapeDtypeStruct((n_src, rows, width), jnp.bfloat16)
+    vmem = pl.BlockSpec(memory_space=pltpu.VMEM)
+    flops = 2 * n_src * rows * hidden.shape[2] * width
+    return pl.pallas_call(
+        functools.partial(down_return_kernel, n_grp),
+        out_shape=out,
+        in_specs=[vmem, vmem],
+        out_specs=pl.BlockSpec(memory_space=pl.ANY),
+        scratch_shapes=[
+            pltpu.VMEM((n_src, rows, width), jnp.bfloat16),
+            pltpu.SemaphoreType.DMA((n_grp,)),
+            pltpu.SemaphoreType.DMA((n_grp,)),
+            pltpu.SemaphoreType.DMA((1,)),
+        ],
+        compiler_params=pltpu.CompilerParams(
+            collective_id=collective_id, has_side_effects=True, vmem_limit_bytes=48 * 1024 * 1024
+        ),
+        cost_estimate=pl.CostEstimate(
+            flops=flops, transcendentals=0, bytes_accessed=hidden.size * 2 + down_full.size * 2 + 2 * n_src * rows * width * 2
+        ),
+    )(hidden, down_full)
+
+
 def weight_kernel(n_x, n_grp, g_in, u_in, d_in, t_in, g_out, u_out, d_out, t_out, send_sem, recv_sem,
                   local_sem, t_send, t_recv):
     ins = (g_in, u_in, d_in)
@@ -233,9 +316,8 @@
     gate_pre = jnp.dot(rows, gate_full.T, preferred_element_type=jnp.float32)
     up_pre = jnp.dot(rows, up_full.T, preferred_element_type=jnp.float32)
     hidden = (jax.nn.silu(gate_pre) * up_pre).astype(jnp.bfloat16)
-    produced = jnp.dot(hidden, down_full, preferred_element_type=jnp.float32).astype(jnp.bfloat16)
-    produced = produced.reshape(n_expert, CAP, model_width)
-    returned = exchange(produced, n_grp, 1).reshape(n_slot, model_width)
+    hidden = hidden.reshape(n_expert, CAP, hidden.shape[-1])
+    returned = down_return(hidden, down_full, n_grp, 1).reshape(n_slot, model_width)
 
     weight_of = jnp.sum(
         jnp.where(hit, combine[None, :, :], jnp.zeros_like(combine)[None, :, :]), axis=2

time: 300 us -> 279 us (0.930)
  the two profiles are of different devices: /device:TPU:112 before, /device:TPU:114 now
where the time goes in v6:
time: 279 us
  Pallas kernels  241 us (86%)
  matrix products  32.5 us (12%)
  other arithmetic  4.03 us (1%)
    pallas_call x1, Pallas kernels, down_return(): pl.pallas_call(functools.partial(down_return_kernel, n_grp), out_shape=ou...  137 us
    pallas_call x1, Pallas kernels, gather_weights(): pl.pallas_call(functools.partial(weight_kernel, n_x, n_grp), out_shape=(s...  103 us
    dot_general x1, matrix products, per_device(): gate_pre = jnp.dot(rows, gate_full.T, preferred_element_type=jnp.float32)  12.9 us
    dot_general x1, matrix products, per_device(): up_pre = jnp.dot(rows, up_full.T, preferred_element_type=jnp.float32)  10.5 us

profile of v6, /device:TPU:114, one launch (start us, length us, event | category | flops | bytes accessed | tf_op | source)
XLA Modules:
  0.0 278.8 jit_solution(13545621756227201125)
XLA Ops:
  0.0 0.0 copy-start
  0.0 0.9 copy.21
  0.9 0.1 eq.35
  1.0 2.0 reduce-window.6
  3.0 0.3 slice_reduce_fusion
  3.4 0.1 bitcast_bitcast_fusion
  3.5 0.1 reduce_sum.21
  3.6 0.1 copy.24
  3.7 0.7 multiply_add_fusion
  4.4 0.6 fusion.1
  5.0 0.0 copy-done
  5.1 3.6 %convolution_convert_fusion = bf16[1152,2048]{1,0:T(8,128)(2,1)} fusion(pred[1152,144]{0,1:T(8,128)(4,1)S(1)} %fusion.1, bf16[144,2048]{1,0:T(8,128)(2,1)S(1)} %copy-done), kind=kOutput, calls=%fused_computation.2 | convolution fusion | flops 681836544 | bytes 5474304 | tf_op jit(solution)/shard_map/dot_general | solution.py:305
  8.7 103.2 %shard_map.64 = (bf16[16,88,2048]{2,1,0:T(8,128)(2,1)}, bf16[16,88,2048]{2,1,0:T(8,128)(2,1)}, bf16[16,88,2048]{2,1,0:T(8,128)(2,1)}, bf16[16,72,2048]{2,1,0:T(8,128)(2,1)}) custom-call(bf16[2,88,2048]{2,1,0:T(8,128)(2,1)} %g_in.1, bf16[2,88,2048]{2,1,0:T(8,128)(2,1)} %u_in.1, bf16[2,88,2048]{2,1,0:T(8,128)(2,1)} %d_in.1, bf16[16,72,2048]{2,1,0:T(8,128)(2,1)} %bitcast.34), custom_call_target="tpu_custom_call" | custom-call | bytes 17301504 | tf_op jit(solution)/shard_map/pallas_call | solution.py:270
  111.9 0.0 copy-start.3
  111.9 12.9 %fusion.8 = f32[1152,1408]{1,0:T(8,128)} fusion(bf16[1152,2048]{1,0:T(8,128)(2,1)} %bitcast.41, bf16[1408,2048]{1,0:T(8,128)(2,1)} %bitcast.40), kind=kOutput, calls=%fused_computation.23 | convolution fusion | flops 6643777536 | bytes 16973824 | tf_op jit(solution)/shard_map/dot_general | solution.py:316
  124.8 0.0 copy-done.3
  124.8 10.5 %fusion = bf16[1152,1408]{1,0:T(8,128)(2,1)S(1)} fusion(bf16[1152,2048]{1,0:T(8,128)(2,1)} %bitcast.42, bf16[1408,2048]{1,0:T(8,128)(2,1)S(1)} %bitcast.39, f32[1152,1408]{1,0:T(8,128)} %fusion.8), kind=kOutput, calls=%fused_computation.1 | convolution fusion | flops 6653509632 | bytes 20217856 | tf_op jit(solution)/shard_map/dot_general | solution.py:317
  135.4 0.0 copy-start.2
  135.4 137.4 %shard_map.65 = bf16[16,72,2048]{2,1,0:T(8,128)(2,1)} custom-call(bf16[16,72,1408]{2,1,0:T(8,128)(2,1)S(1)} %bitcast.33, bf16[1408,2048]{1,0:T(8,128)(2,1)} %bitcast.38), custom_call_target="tpu_custom_call" | custom-call | flops 6643777536 | bytes 18448384 | tf_op jit(solution)/shard_map/pallas_call | solution.py:147
  272.8 0.0 copy-start.1
  272.8 0.0 copy-done.2
  272.8 0.5 select_reduce_fusion
  273.4 3.6 %fusion.5 = f32[144,2048]{1,0:T(8,128)S(1)} fusion(bf16[1152,2048]{1,0:T(8,128)(2,1)} %bitcast.35, f32[1152,144]{0,1:T(8,128)S(1)} %select_reduce_fusion), kind=kOutput, calls=%fused_computation.11 | convolution fusion | flops 679809024 | bytes 6561792 | tf_op jit(solution)/shard_map/dot_general | solution.py:328
  276.9 0.0 copy-done.1
  276.9 1.8 fusion.2
  (4 shorter events, 0.1 us)
Async XLA Ops:
  0.0 5.0 %copy-start = (bf16[144,2048]{1,0:T(8,128)(2,1)S(1)}, bf16[144,2048]{1,0:T(8,128)(2,1)}, u32[]{:S(2)}) copy-start(bf16[144,2048]{1,0:T(8,128)(2,1)} %param.6) | copy-start | bytes 1769476
  111.9 12.9 %copy-start.3 = (bf16[16,88,2048]{2,1,0:T(8,128)(2,1)S(1)}, bf16[16,88,2048]{2,1,0:T(8,128)(2,1)}, u32[]{:S(2)}) copy-start(bf16[16,88,2048]{2,1,0:T(8,128)(2,1)} %get-tuple-element.11) | copy-start | bytes 17301508
  135.4 137.4 %copy-start.2 = (f32[144,6]{0,1:T(8,128)S(1)}, f32[144,6]{0,1:T(8,128)}, u32[]{:S(2)}) copy-start(f32[144,6]{0,1:T(8,128)} %param.8) | copy-start | bytes 10372
  272.8 4.1 %copy-start.1 = (bf16[16,72,2048]{2,1,0:T(8,128)(2,1)S(1)}, bf16[16,72,2048]{2,1,0:T(8,128)(2,1)}, u32[]{:S(2)}) copy-start(bf16[16,72,2048]{2,1,0:T(8,128)(2,1)} %shard_map.65) | copy-start | bytes 14155780

commit v7 on v6

--- a/solution.py
+++ b/solution.py
@@ -81,7 +81,8 @@
     )(x)
 
 
-def down_return_kernel(n_grp, hid_ref, down_ref, y_ref, buf, send_sem, recv_sem, local_sem):
+def expert_return_kernel(n_grp, rows_ref, gate_ref, up_ref, down_ref, y_ref, buf, send_sem, recv_sem,
+                         local_sem):
     me, peers = exchange_peers(n_grp)
     barrier = pltpu.get_barrier_semaphore()
     for p, dev in peers:
@@ -89,9 +90,12 @@
 
     def project(k):
         p = lax.rem(me + k, n_grp)
-        buf[p] = jnp.dot(hid_ref[p], down_ref[...], preferred_element_type=jnp.float32).astype(
-            buf.dtype
-        )
+        r = rows_ref[p]
+        nt = (((1,), (1,)), ((), ()))
+        gate_pre = lax.dot_general(r, gate_ref[...], nt, preferred_element_type=jnp.float32)
+        up_pre = lax.dot_general(r, up_ref[...], nt, preferred_element_type=jnp.float32)
+        hidden = (jax.nn.silu(gate_pre) * up_pre).astype(jnp.bfloat16)
+        buf[p] = jnp.dot(hidden, down_ref[...], preferred_element_type=jnp.float32).astype(buf.dtype)
 
     def remote(k):
         p = lax.rem(me + k, n_grp)
@@ -138,30 +142,29 @@
         ).wait_recv()
 
 
-def down_return(hidden, down_full, n_grp, collective_id):
-    n_src, rows, _ = hidden.shape
-    width = down_full.shape[1]
-    out = jax.ShapeDtypeStruct((n_src, rows, width), jnp.bfloat16)
+def expert_return(rows, gate_full, up_full, down_full, n_grp, collective_id):
+    n_src, cap, width = rows.shape
+    ff = gate_full.shape[0]
+    out = jax.ShapeDtypeStruct((n_src, cap, width), jnp.bfloat16)
     vmem = pl.BlockSpec(memory_space=pltpu.VMEM)
-    flops = 2 * n_src * rows * hidden.shape[2] * width
+    flops = 6 * n_src * cap * ff * width
+    nbytes = rows.size * 2 + 3 * gate_full.size * 2 + 2 * n_src * cap * width * 2
     return pl.pallas_call(
-        functools.partial(down_return_kernel, n_grp),
+        functools.partial(expert_return_kernel, n_grp),
         out_shape=out,
-        in_specs=[vmem, vmem],
+        in_specs=[vmem] * 4,
         out_specs=pl.BlockSpec(memory_space=pl.ANY),
         scratch_shapes=[
-            pltpu.VMEM((n_src, rows, width), jnp.bfloat16),
+            pltpu.VMEM((n_src, cap, width), jnp.bfloat16),
             pltpu.SemaphoreType.DMA((n_grp,)),
             pltpu.SemaphoreType.DMA((n_grp,)),
             pltpu.SemaphoreType.DMA((1,)),
         ],
         compiler_params=pltpu.CompilerParams(
-            collective_id=collective_id, has_side_effects=True, vmem_limit_bytes=48 * 1024 * 1024
+            collective_id=collective_id, has_side_effects=True, vmem_limit_bytes=56 * 1024 * 1024
         ),
-        cost_estimate=pl.CostEstimate(
-            flops=flops, transcendentals=0, bytes_accessed=hidden.size * 2 + down_full.size * 2 + 2 * n_src * rows * width * 2
-        ),
-    )(hidden, down_full)
+        cost_estimate=pl.CostEstimate(flops=flops, transcendentals=n_src * cap * ff, bytes_accessed=nbytes),
+    )(rows, gate_full, up_full, down_full)
 
 
 def weight_kernel(n_x, n_grp, g_in, u_in, d_in, t_in, g_out, u_out, d_out, t_out, send_sem, recv_sem,
@@ -311,13 +314,8 @@
     gate_full = g_all.reshape(-1, model_width)
     up_full = u_all.reshape(-1, model_width)
     down_full = d_all.reshape(-1, model_width)
-    rows = arrived.reshape(n_slot, model_width)
-
-    gate_pre = jnp.dot(rows, gate_full.T, preferred_element_type=jnp.float32)
-    up_pre = jnp.dot(rows, up_full.T, preferred_element_type=jnp.float32)
-    hidden = (jax.nn.silu(gate_pre) * up_pre).astype(jnp.bfloat16)
-    hidden = hidden.reshape(n_expert, CAP, hidden.shape[-1])
-    returned = down_return(hidden, down_full, n_grp, 1).reshape(n_slot, model_width)
+    returned = expert_return(arrived, gate_full, up_full, down_full, n_grp, 1)
+    returned = returned.reshape(n_slot, model_width)
 
     weight_of = jnp.sum(
         jnp.where(hit, combine[None, :, :], jnp.zeros_like(combine)[None, :, :]), axis=2

time: 279 us -> 271 us (0.971)
  the two profiles are of different devices: /device:TPU:114 before, /device:TPU:112 now
where the time goes in v7:
time: 271 us
  Pallas kernels  256 us (94%)
  matrix products  9.06 us (3%)
  other arithmetic  4.03 us (1%)
    pallas_call x1, Pallas kernels, expert_return(): pl.pallas_call(functools.partial(expert_return_kernel, n_grp), out_shape=...  150 us
    pallas_call x1, Pallas kernels, gather_weights(): pl.pallas_call(functools.partial(weight_kernel, n_x, n_grp), out_shape=(s...  106 us

profile of v7, /device:TPU:112, one launch (start us, length us, event | category | flops | bytes accessed | tf_op | source)
XLA Modules:
  0.0 271.0 jit_solution(6888973302554469866)
XLA Ops:
  0.0 0.0 copy-start
  0.0 0.9 copy.21
  0.9 0.1 eq.35
  1.0 2.0 reduce-window.6
  3.0 0.3 slice_reduce_fusion
  3.4 0.1 bitcast_bitcast_fusion
  3.5 0.1 reduce_sum.21
  3.6 0.1 copy.24
  3.7 0.7 multiply_add_fusion
  4.4 0.6 fusion
  5.0 0.0 copy-done
  5.1 3.7 %convolution_convert_fusion = bf16[1152,2048]{1,0:T(8,128)(2,1)} fusion(pred[1152,144]{0,1:T(8,128)(4,1)S(1)} %fusion, bf16[144,2048]{1,0:T(8,128)(2,1)S(1)} %copy-done), kind=kOutput, calls=%fused_computation | convolution fusion | flops 681836544 | bytes 5474304 | tf_op jit(solution)/shard_map/dot_general | solution.py:308
  8.7 106.1 %shard_map.64 = (bf16[16,88,2048]{2,1,0:T(8,128)(2,1)}, bf16[16,88,2048]{2,1,0:T(8,128)(2,1)}, bf16[16,88,2048]{2,1,0:T(8,128)(2,1)}, bf16[16,72,2048]{2,1,0:T(8,128)(2,1)}) custom-call(bf16[2,88,2048]{2,1,0:T(8,128)(2,1)} %g_in.1, bf16[2,88,2048]{2,1,0:T(8,128)(2,1)} %u_in.1, bf16[2,88,2048]{2,1,0:T(8,128)(2,1)} %d_in.1, bf16[16,72,2048]{2,1,0:T(8,128)(2,1)} %bitcast.27), custom_call_target="tpu_custom_call" | custom-call | bytes 17301504 | tf_op jit(solution)/shard_map/pallas_call | solution.py:273
  114.8 0.0 copy-start.2
  114.8 150.2 %shard_map.65 = bf16[16,72,2048]{2,1,0:T(8,128)(2,1)} custom-call(bf16[16,72,2048]{2,1,0:T(8,128)(2,1)} %get-tuple-element.9.rows_ref, bf16[1408,2048]{1,0:T(8,128)(2,1)} %bitcast.31, bf16[1408,2048]{1,0:T(8,128)(2,1)} %bitcast.32, bf16[1408,2048]{1,0:T(8,128)(2,1)} %bitcast.33), custom_call_target="tpu_custom_call" | custom-call | flops 19931332608 | bytes 31457280 | tf_op jit(solution)/shard_map/pallas_call | solution.py:152
  265.0 0.0 copy-start.1
  265.0 0.0 copy-done.2
  265.0 0.5 select_reduce_fusion
  265.6 3.6 %fusion.4 = f32[144,2048]{1,0:T(8,128)S(1)} fusion(bf16[1152,2048]{1,0:T(8,128)(2,1)} %bitcast.28, f32[1152,144]{0,1:T(8,128)S(1)} %select_reduce_fusion), kind=kOutput, calls=%fused_computation.9 | convolution fusion | flops 679809024 | bytes 6561792 | tf_op jit(solution)/shard_map/dot_general | solution.py:326
  269.1 0.0 copy-done.1
  269.2 1.8 fusion.1
  (4 shorter events, 0.1 us)
Async XLA Ops:
  0.0 5.0 %copy-start = (bf16[144,2048]{1,0:T(8,128)(2,1)S(1)}, bf16[144,2048]{1,0:T(8,128)(2,1)}, u32[]{:S(2)}) copy-start(bf16[144,2048]{1,0:T(8,128)(2,1)} %param.6) | copy-start | bytes 1769476
  114.8 150.2 %copy-start.2 = (f32[144,6]{0,1:T(8,128)S(1)}, f32[144,6]{0,1:T(8,128)}, u32[]{:S(2)}) copy-start(f32[144,6]{0,1:T(8,128)} %param.8) | copy-start | bytes 10372
  265.0 4.1 %copy-start.1 = (bf16[16,72,2048]{2,1,0:T(8,128)(2,1)S(1)}, bf16[16,72,2048]{2,1,0:T(8,128)(2,1)}, u32[]{:S(2)}) copy-start(bf16[16,72,2048]{2,1,0:T(8,128)(2,1)} %shard_map.65) | copy-start | bytes 14155780

commit v8 on v7

--- a/solution.py
+++ b/solution.py
@@ -52,6 +52,81 @@
     for cp in copies:
         cp.wait_send()
     local.wait()
+
+
+def plane_plan(n_grp):
+    e_idx = lax.axis_index("expert")
+    h = lax.axis_index("zhi")
+    c = lax.axis_index("core")
+    y = e_idx // 2
+    z = h * 2 + lax.rem(e_idx, 2)
+    s = 1 - 2 * c
+
+    def at(dy, dz):
+        yy = lax.rem(y + dy + 4, 4)
+        zz = lax.rem(z + dz + 4, 4)
+        p = (yy * 2 + lax.rem(zz, 2)) * 2 + zz // 2
+        return p, {"expert": yy * 2 + lax.rem(zz, 2), "zhi": zz // 2}
+
+    direct = [(dy, dz) for dy in (0, 1, 3) for dz in (0, 1, 3) if (dy, dz) != (0, 0)]
+    relayed = [((2, dz), (s, 0)) for dz in (0, 1, 3)]
+    relayed += [((dy, 2), (0, s)) for dy in (0, 1, 3)]
+    relayed += [((2, 2), (s, s))]
+    me = (y * 2 + lax.rem(z, 2)) * 2 + z // 2
+    return me, at, direct, relayed
+
+
+def start_plane(n_grp, x_ref, y_ref, stage, send_sem, recv_sem, stage_sem, local_sem):
+    me, at, direct, relayed = plane_plan(n_grp)
+    copies = []
+    local = pltpu.make_async_copy(x_ref.at[me], y_ref.at[me], local_sem)
+    local.start()
+    k = 0
+    for j, (off, rel) in enumerate(relayed):
+        p, _ = at(*off)
+        _, dev = at(*rel)
+        cp = pltpu.make_async_remote_copy(
+            src_ref=x_ref.at[p], dst_ref=stage.at[j], send_sem=send_sem.at[k],
+            recv_sem=stage_sem.at[j], device_id=dev, device_id_type=MESH_ID,
+        )
+        cp.start()
+        copies.append(cp)
+        k += 1
+    for off in direct:
+        p, dev = at(*off)
+        cp = pltpu.make_async_remote_copy(
+            src_ref=x_ref.at[p], dst_ref=y_ref.at[me], send_sem=send_sem.at[k],
+            recv_sem=recv_sem.at[me], device_id=dev, device_id_type=MESH_ID,
+        )
+        cp.start()
+        copies.append(cp)
+        k += 1
+    return local, copies, k
+
+
+def relay_plane(n_grp, k, x_ref, y_ref, stage, send_sem, recv_sem, stage_sem):
+    me, at, direct, relayed = plane_plan(n_grp)
+    copies = []
+    for j, (off, rel) in enumerate(relayed):
+        src_p, _ = at(-rel[0], -rel[1])
+        _, dev = at(off[0] - rel[0], off[1] - rel[1])
+        pltpu.make_async_remote_copy(
+            src_ref=x_ref.at[0], dst_ref=stage.at[j], send_sem=send_sem.at[0],
+            recv_sem=stage_sem.at[j], device_id=dev, device_id_type=MESH_ID,
+        ).wait_recv()
+        cp = pltpu.make_async_remote_copy(
+            src_ref=stage.at[j], dst_ref=y_ref.at[src_p], send_sem=send_sem.at[k],
+            recv_sem=recv_sem.at[src_p], device_id=dev, device_id_type=MESH_ID,
+        )
+        cp.start()
+        copies.append(cp)
+        k += 1
+    return copies
+
+
+def plane_devices(n_grp):
+    me, at, direct, relayed = plane_plan(n_grp)
+    return [at(*off)[1] for off in direct]
 
 
 def exchange_kernel(n_grp, x_ref, y_ref, send_sem, recv_sem, local_sem):
@@ -168,7 +243,7 @@
 
 
 def weight_kernel(n_x, n_grp, g_in, u_in, d_in, t_in, g_out, u_out, d_out, t_out, send_sem, recv_sem,
-                  local_sem, t_send, t_recv):
+                  local_sem, t_send, t_recv, stage, stage_sem):
     ins = (g_in, u_in, d_in)
     outs = (g_out, u_out, d_out)
     x = lax.axis_index("x")
@@ -190,7 +265,7 @@
 
     t_me, t_peers = exchange_peers(n_grp)
     barrier = pltpu.get_barrier_semaphore()
-    greet = [partner] + x_devs + [dev for p, dev in t_peers]
+    greet = [partner, z_peer] + x_devs + plane_devices(n_grp)
     for dev in greet:
         pl.semaphore_signal(barrier, inc=1, device_id=dev, device_id_type=MESH_ID)
     pl.semaphore_wait(barrier, len(greet))
@@ -234,12 +309,15 @@
     sent += send(lambda m: ins[m].at[1 - h], me, z_peer)
     for dev in [partner] + x_devs:
         sent += send(lambda m: ins[m].at[h], me, dev)
-    t_local, t_copies = start_exchange(t_me, t_peers, t_in, t_out, t_send, t_recv, local_sem.at[3])
+    t_local, t_copies, t_k = start_plane(
+        n_grp, t_in, t_out, stage, t_send, t_recv, stage_sem, local_sem.at[3]
+    )
 
     z_blk = block(x, 1 - h, c)
     wait_in(z_blk)
     for dev in [partner] + x_devs:
         sent += send(lambda m: outs[m].at[z_blk], z_blk, dev)
+    t_copies += relay_plane(n_grp, t_k, t_in, t_out, stage, t_send, t_recv, stage_sem)
 
     for hh in (h, 1 - h):
         blk = block(away, hh, c)
@@ -279,8 +357,10 @@
             pltpu.SemaphoreType.DMA((3, n_send)),
             pltpu.SemaphoreType.DMA((3, n_blocks)),
             pltpu.SemaphoreType.DMA((4,)),
+            pltpu.SemaphoreType.DMA((n_grp + 8,)),
             pltpu.SemaphoreType.DMA((n_grp,)),
-            pltpu.SemaphoreType.DMA((n_grp,)),
+            pltpu.VMEM((7,) + outgoing.shape[1:], outgoing.dtype),
+            pltpu.SemaphoreType.DMA((7,)),
         ],
         compiler_params=pltpu.CompilerParams(collective_id=0, has_side_effects=True),
         cost_estimate=pl.CostEstimate(flops=0, transcendentals=0, bytes_accessed=nbytes),
@@ -294,6 +374,7 @@
     groups = lax.axis_size("expert")
     n_expert = per_group * groups
     n_grp = groups * 2
+    assert n_grp == 16
     tok_rows, top_k = expert_ids.shape
     model_width = tokens.shape[1]
     n_slot = n_expert * CAP

time: 271 us -> 235 us (0.87)
  the two profiles are of different devices: /device:TPU:112 before, /device:TPU:98 now
where the time goes in v8:
time: 235 us
  Pallas kernels  220 us (94%)
  matrix products  9.07 us (4%)
  other arithmetic  4.03 us (2%)
    pallas_call x1, Pallas kernels, expert_return(): pl.pallas_call(functools.partial(expert_return_kernel, n_grp), out_shape=...  118 us
    pallas_call x1, Pallas kernels, gather_weights(): pl.pallas_call(functools.partial(weight_kernel, n_x, n_grp), out_shape=(s...  102 us

profile of v8, /device:TPU:98, one launch (start us, length us, event | category | flops | bytes accessed | tf_op | source)
XLA Modules:
  0.0 235.0 jit_solution(4841956708293619690)
XLA Ops:
  0.0 0.0 copy-start
  0.0 0.9 copy.21
  0.9 0.1 eq.35
  1.0 2.0 reduce-window.6
  3.0 0.3 slice_reduce_fusion
  3.4 0.1 bitcast_bitcast_fusion
  3.5 0.1 reduce_sum.21
  3.6 0.1 copy.24
  3.7 0.7 multiply_add_fusion
  4.4 0.6 fusion
  5.0 0.0 copy-done
  5.1 3.7 %convolution_convert_fusion = bf16[1152,2048]{1,0:T(8,128)(2,1)} fusion(pred[1152,144]{0,1:T(8,128)(4,1)S(1)} %fusion, bf16[144,2048]{1,0:T(8,128)(2,1)S(1)} %copy-done), kind=kOutput, calls=%fused_computation | convolution fusion | flops 681836544 | bytes 5474304 | tf_op jit(solution)/shard_map/dot_general | solution.py:389
  8.7 102.3 %shard_map.64 = (bf16[16,88,2048]{2,1,0:T(8,128)(2,1)}, bf16[16,88,2048]{2,1,0:T(8,128)(2,1)}, bf16[16,88,2048]{2,1,0:T(8,128)(2,1)}, bf16[16,72,2048]{2,1,0:T(8,128)(2,1)}) custom-call(bf16[2,88,2048]{2,1,0:T(8,128)(2,1)} %g_in.1, bf16[2,88,2048]{2,1,0:T(8,128)(2,1)} %u_in.1, bf16[2,88,2048]{2,1,0:T(8,128)(2,1)} %d_in.1, bf16[16,72,2048]{2,1,0:T(8,128)(2,1)} %bitcast.27), custom_call_target="tpu_custom_call" | custom-call | bytes 17301504 | tf_op jit(solution)/shard_map/pallas_call | solution.py:351
  111.1 0.0 copy-start.2
  111.1 117.9 %shard_map.65 = bf16[16,72,2048]{2,1,0:T(8,128)(2,1)} custom-call(bf16[16,72,2048]{2,1,0:T(8,128)(2,1)} %get-tuple-element.9.rows_ref, bf16[1408,2048]{1,0:T(8,128)(2,1)} %bitcast.31, bf16[1408,2048]{1,0:T(8,128)(2,1)} %bitcast.32, bf16[1408,2048]{1,0:T(8,128)(2,1)} %bitcast.33), custom_call_target="tpu_custom_call" | custom-call | flops 19931332608 | bytes 31457280 | tf_op jit(solution)/shard_map/pallas_call | solution.py:227
  229.0 0.0 copy-start.1
  229.0 0.0 copy-done.2
  229.0 0.5 select_reduce_fusion
  229.6 3.6 %fusion.4 = f32[144,2048]{1,0:T(8,128)S(1)} fusion(bf16[1152,2048]{1,0:T(8,128)(2,1)} %bitcast.28, f32[1152,144]{0,1:T(8,128)S(1)} %select_reduce_fusion), kind=kOutput, calls=%fused_computation.9 | convolution fusion | flops 679809024 | bytes 6561792 | tf_op jit(solution)/shard_map/dot_general | solution.py:407
  233.1 0.0 copy-done.1
  233.2 1.8 fusion.1
  (4 shorter events, 0.1 us)
Async XLA Ops:
  0.0 5.0 %copy-start = (bf16[144,2048]{1,0:T(8,128)(2,1)S(1)}, bf16[144,2048]{1,0:T(8,128)(2,1)}, u32[]{:S(2)}) copy-start(bf16[144,2048]{1,0:T(8,128)(2,1)} %param.6) | copy-start | bytes 1769476
  111.1 117.9 %copy-start.2 = (f32[144,6]{0,1:T(8,128)S(1)}, f32[144,6]{0,1:T(8,128)}, u32[]{:S(2)}) copy-start(f32[144,6]{0,1:T(8,128)} %param.8) | copy-start | bytes 10372
  229.0 4.1 %copy-start.1 = (bf16[16,72,2048]{2,1,0:T(8,128)(2,1)S(1)}, bf16[16,72,2048]{2,1,0:T(8,128)(2,1)}, u32[]{:S(2)}) copy-start(bf16[16,72,2048]{2,1,0:T(8,128)(2,1)} %shard_map.65) | copy-start | bytes 14155780

commit v9 on v8

--- a/solution.py
+++ b/solution.py
@@ -156,15 +156,30 @@
     )(x)
 
 
-def expert_return_kernel(n_grp, rows_ref, gate_ref, up_ref, down_ref, y_ref, buf, send_sem, recv_sem,
-                         local_sem):
-    me, peers = exchange_peers(n_grp)
+def expert_return_kernel(n_grp, rows_ref, gate_ref, up_ref, down_ref, y_ref, buf, stage, send_sem,
+                         recv_sem, stage_sem, local_sem):
+    me, at, direct, relayed = plane_plan(n_grp)
+    n_rel = len(relayed)
+    order = [off for off, rel in relayed] + direct + [(0, 0)]
+    rel_of = [rel for off, rel in relayed]
     barrier = pltpu.get_barrier_semaphore()
-    for p, dev in peers:
+    peers = plane_devices(n_grp)
+    for dev in peers:
         pl.semaphore_signal(barrier, inc=1, device_id=dev, device_id_type=MESH_ID)
 
+    def pick(k, values):
+        out = values[-1]
+        for i in range(len(values) - 2, -1, -1):
+            out = jnp.where(k == i, values[i], out)
+        return out
+
+    def chunk_of(k):
+        dy = pick(k, [o[0] for o in order])
+        dz = pick(k, [o[1] for o in order])
+        return at(dy, dz)
+
     def project(k):
-        p = lax.rem(me + k, n_grp)
+        p, _ = chunk_of(k)
         r = rows_ref[p]
         nt = (((1,), (1,)), ((), ()))
         gate_pre = lax.dot_general(r, gate_ref[...], nt, preferred_element_type=jnp.float32)
@@ -172,16 +187,35 @@
         hidden = (jax.nn.silu(gate_pre) * up_pre).astype(jnp.bfloat16)
         buf[p] = jnp.dot(hidden, down_ref[...], preferred_element_type=jnp.float32).astype(buf.dtype)
 
-    def remote(k):
-        p = lax.rem(me + k, n_grp)
+    def first_hop(k):
+        p, _ = chunk_of(k)
+        ry = pick(k, [r[0] for r in rel_of])
+        rz = pick(k, [r[1] for r in rel_of])
+        _, dev = at(ry, rz)
         return pltpu.make_async_remote_copy(
-            src_ref=buf.at[p],
-            dst_ref=y_ref.at[me],
-            send_sem=send_sem.at[k],
-            recv_sem=recv_sem.at[me],
-            device_id={"expert": p // 2, "zhi": lax.rem(p, 2)},
-            device_id_type=MESH_ID,
-        )
+            src_ref=buf.at[p], dst_ref=stage.at[k], send_sem=send_sem.at[k],
+            recv_sem=stage_sem.at[k], device_id=dev, device_id_type=MESH_ID,
+        )
+
+    def direct_send(k):
+        p, dev = chunk_of(k)
+        return pltpu.make_async_remote_copy(
+            src_ref=buf.at[p], dst_ref=y_ref.at[me], send_sem=send_sem.at[k],
+            recv_sem=recv_sem.at[me], device_id=dev, device_id_type=MESH_ID,
+        )
+
+    def forwards():
+        for j, (off, rel) in enumerate(relayed):
+            src_p, _ = at(-rel[0], -rel[1])
+            _, dev = at(off[0] - rel[0], off[1] - rel[1])
+            pltpu.make_async_remote_copy(
+                src_ref=buf.at[0], dst_ref=stage.at[j], send_sem=send_sem.at[0],
+                recv_sem=stage_sem.at[j], device_id=dev, device_id_type=MESH_ID,
+            ).wait_recv()
+            pltpu.make_async_remote_copy(
+                src_ref=stage.at[j], dst_ref=y_ref.at[src_p], send_sem=send_sem.at[n_grp - 1 + j],
+                recv_sem=recv_sem.at[src_p], device_id=dev, device_id_type=MESH_ID,
+            ).start()
 
     local = pltpu.make_async_copy(buf.at[me], y_ref.at[me], local_sem.at[0])
     project(0)
@@ -190,30 +224,40 @@
     def step(k, carry):
         project(k)
 
-        @pl.when(k == 1)
+        @pl.when(k - 1 < n_rel)
         def _():
-            local.start()
-
-        @pl.when(k >= 2)
+            first_hop(k - 1).start()
+
+        @pl.when(k - 1 >= n_rel)
         def _():
-            remote(k - 1).start()
+            direct_send(k - 1).start()
+
+        @pl.when(k == n_rel + 4)
+        def _():
+            forwards()
 
         return carry
 
     lax.fori_loop(1, n_grp, step, 0)
-    remote(n_grp - 1).start()
+    local.start()
 
     local.wait()
-    for k in range(1, n_grp):
-        remote(k).wait_send()
-    for p, dev in peers:
+    for k in range(n_grp - 1):
+        if k < n_rel:
+            first_hop(k).wait_send()
+        else:
+            direct_send(k).wait_send()
+    for j, (off, rel) in enumerate(relayed):
+        _, dev = at(off[0] - rel[0], off[1] - rel[1])
         pltpu.make_async_remote_copy(
-            src_ref=buf.at[0],
-            dst_ref=y_ref.at[p],
-            send_sem=send_sem.at[0],
-            recv_sem=recv_sem.at[p],
-            device_id=dev,
-            device_id_type=MESH_ID,
+            src_ref=stage.at[j], dst_ref=y_ref.at[0], send_sem=send_sem.at[n_grp - 1 + j],
+            recv_sem=recv_sem.at[0], device_id=dev, device_id_type=MESH_ID,
+        ).wait_send()
+    for s in range(1, n_grp):
+        q = lax.rem(me + s, n_grp)
+        pltpu.make_async_remote_copy(
+            src_ref=buf.at[0], dst_ref=y_ref.at[q], send_sem=send_sem.at[0],
+            recv_sem=recv_sem.at[q], device_id=peers[0], device_id_type=MESH_ID,
         ).wait_recv()
 
 
@@ -231,8 +275,10 @@
         out_specs=pl.BlockSpec(memory_space=pl.ANY),
         scratch_shapes=[
             pltpu.VMEM((n_src, cap, width), jnp.bfloat16),
+            pltpu.VMEM((7, cap, width), jnp.bfloat16),
+            pltpu.SemaphoreType.DMA((n_grp + 8,)),
             pltpu.SemaphoreType.DMA((n_grp,)),
-            pltpu.SemaphoreType.DMA((n_grp,)),
+            pltpu.SemaphoreType.DMA((7,)),
             pltpu.SemaphoreType.DMA((1,)),
         ],
         compiler_params=pltpu.CompilerParams(

time: 235 us -> 230 us (0.979)
  the two profiles are of different devices: /device:TPU:98 before, /device:TPU:15 now
where the time goes in v9:
time: 230 us
  Pallas kernels  216 us (94%)
  matrix products  9.07 us (4%)
  other arithmetic  4.03 us (2%)
    pallas_call x1, Pallas kernels, expert_return(): pl.pallas_call(functools.partial(expert_return_kernel, n_grp), out_shape=...  117 us
    pallas_call x1, Pallas kernels, gather_weights(): pl.pallas_call(functools.partial(weight_kernel, n_x, n_grp), out_shape=(s...  98.3 us

profile of v9, /device:TPU:15, one launch (start us, length us, event | category | flops | bytes accessed | tf_op | source)
XLA Modules:
  0.0 230.2 jit_solution(11245824921507205794)
XLA Ops:
  0.0 0.0 copy-start
  0.0 0.9 copy.21
  0.9 0.1 eq.35
  1.0 2.0 reduce-window.6
  3.0 0.3 slice_reduce_fusion
  3.4 0.1 bitcast_bitcast_fusion
  3.5 0.1 reduce_sum.21
  3.6 0.1 copy.24
  3.7 0.7 multiply_add_fusion
  4.4 0.6 fusion
  5.0 0.0 copy-done
  5.1 3.7 %convolution_convert_fusion = bf16[1152,2048]{1,0:T(8,128)(2,1)} fusion(pred[1152,144]{0,1:T(8,128)(4,1)S(1)} %fusion, bf16[144,2048]{1,0:T(8,128)(2,1)S(1)} %copy-done), kind=kOutput, calls=%fused_computation | convolution fusion | flops 681836544 | bytes 5474304 | tf_op jit(solution)/shard_map/dot_general | solution.py:435
  8.7 98.3 %shard_map.64 = (bf16[16,88,2048]{2,1,0:T(8,128)(2,1)}, bf16[16,88,2048]{2,1,0:T(8,128)(2,1)}, bf16[16,88,2048]{2,1,0:T(8,128)(2,1)}, bf16[16,72,2048]{2,1,0:T(8,128)(2,1)}) custom-call(bf16[2,88,2048]{2,1,0:T(8,128)(2,1)} %g_in.1, bf16[2,88,2048]{2,1,0:T(8,128)(2,1)} %u_in.1, bf16[2,88,2048]{2,1,0:T(8,128)(2,1)} %d_in.1, bf16[16,72,2048]{2,1,0:T(8,128)(2,1)} %bitcast.27), custom_call_target="tpu_custom_call" | custom-call | bytes 17301504 | tf_op jit(solution)/shard_map/pallas_call | solution.py:397
  107.1 0.0 copy-start.2
  107.1 117.2 %shard_map.65 = bf16[16,72,2048]{2,1,0:T(8,128)(2,1)} custom-call(bf16[16,72,2048]{2,1,0:T(8,128)(2,1)} %get-tuple-element.9.rows_ref, bf16[1408,2048]{1,0:T(8,128)(2,1)} %bitcast.31, bf16[1408,2048]{1,0:T(8,128)(2,1)} %bitcast.32, bf16[1408,2048]{1,0:T(8,128)(2,1)} %bitcast.33), custom_call_target="tpu_custom_call" | custom-call | flops 19931332608 | bytes 31457280 | tf_op jit(solution)/shard_map/pallas_call | solution.py:271
  224.3 0.0 copy-start.1
  224.3 0.0 copy-done.2
  224.3 0.5 select_reduce_fusion
  224.8 3.6 %fusion.4 = f32[144,2048]{1,0:T(8,128)S(1)} fusion(bf16[1152,2048]{1,0:T(8,128)(2,1)} %bitcast.28, f32[1152,144]{0,1:T(8,128)S(1)} %select_reduce_fusion), kind=kOutput, calls=%fused_computation.9 | convolution fusion | flops 679809024 | bytes 6561792 | tf_op jit(solution)/shard_map/dot_general | solution.py:453
  228.4 0.0 copy-done.1
  228.4 1.8 fusion.1
  (4 shorter events, 0.1 us)
Async XLA Ops:
  0.0 5.0 %copy-start = (bf16[144,2048]{1,0:T(8,128)(2,1)S(1)}, bf16[144,2048]{1,0:T(8,128)(2,1)}, u32[]{:S(2)}) copy-start(bf16[144,2048]{1,0:T(8,128)(2,1)} %param.6) | copy-start | bytes 1769476
  107.1 117.2 %copy-start.2 = (f32[144,6]{0,1:T(8,128)S(1)}, f32[144,6]{0,1:T(8,128)}, u32[]{:S(2)}) copy-start(f32[144,6]{0,1:T(8,128)} %param.8) | copy-start | bytes 10372
  224.3 4.1 %copy-start.1 = (bf16[16,72,2048]{2,1,0:T(8,128)(2,1)S(1)}, bf16[16,72,2048]{2,1,0:T(8,128)(2,1)}, u32[]{:S(2)}) copy-start(bf16[16,72,2048]{2,1,0:T(8,128)(2,1)} %shard_map.65) | copy-start | bytes 14155780

commit v10 on v9

--- a/solution.py
+++ b/solution.py
@@ -156,8 +156,8 @@
     )(x)
 
 
-def expert_return_kernel(n_grp, rows_ref, gate_ref, up_ref, down_ref, y_ref, buf, stage, send_sem,
-                         recv_sem, stage_sem, local_sem):
+def expert_return_kernel(n_grp, hid_ref, down_ref, y_ref, buf, stage, send_sem, recv_sem, stage_sem,
+                         local_sem):
     me, at, direct, relayed = plane_plan(n_grp)
     n_rel = len(relayed)
     order = [off for off, rel in relayed] + direct + [(0, 0)]
@@ -180,12 +180,7 @@
 
     def project(k):
         p, _ = chunk_of(k)
-        r = rows_ref[p]
-        nt = (((1,), (1,)), ((), ()))
-        gate_pre = lax.dot_general(r, gate_ref[...], nt, preferred_element_type=jnp.float32)
-        up_pre = lax.dot_general(r, up_ref[...], nt, preferred_element_type=jnp.float32)
-        hidden = (jax.nn.silu(gate_pre) * up_pre).astype(jnp.bfloat16)
-        buf[p] = jnp.dot(hidden, down_ref[...], preferred_element_type=jnp.float32).astype(buf.dtype)
+        buf[p] = jnp.dot(hid_ref[p], down_ref[...], preferred_element_type=jnp.float32).astype(buf.dtype)
 
     def first_hop(k):
         p, _ = chunk_of(k)
@@ -261,17 +256,17 @@
         ).wait_recv()
 
 
-def expert_return(rows, gate_full, up_full, down_full, n_grp, collective_id):
-    n_src, cap, width = rows.shape
-    ff = gate_full.shape[0]
+def expert_return(hidden, down_full, n_grp, collective_id):
+    n_src, cap, ff = hidden.shape
+    width = down_full.shape[1]
     out = jax.ShapeDtypeStruct((n_src, cap, width), jnp.bfloat16)
     vmem = pl.BlockSpec(memory_space=pltpu.VMEM)
-    flops = 6 * n_src * cap * ff * width
-    nbytes = rows.size * 2 + 3 * gate_full.size * 2 + 2 * n_src * cap * width * 2
+    flops = 2 * n_src * cap * ff * width
+    nbytes = hidden.size * 2 + down_full.size * 2 + 2 * n_src * cap * width * 2
     return pl.pallas_call(
         functools.partial(expert_return_kernel, n_grp),
         out_shape=out,
-        in_specs=[vmem] * 4,
+        in_specs=[vmem] * 2,
         out_specs=pl.BlockSpec(memory_space=pl.ANY),
         scratch_shapes=[
             pltpu.VMEM((n_src, cap, width), jnp.bfloat16),
@@ -284,8 +279,8 @@
         compiler_params=pltpu.CompilerParams(
             collective_id=collective_id, has_side_effects=True, vmem_limit_bytes=56 * 1024 * 1024
         ),
-        cost_estimate=pl.CostEstimate(flops=flops, transcendentals=n_src * cap * ff, bytes_accessed=nbytes),
-    )(rows, gate_full, up_full, down_full)
+        cost_estimate=pl.CostEstimate(flops=flops, transcendentals=0, bytes_accessed=nbytes),
+    )(hidden, down_full)
 
 
 def weight_kernel(n_x, n_grp, g_in, u_in, d_in, t_in, g_out, u_out, d_out, t_out, send_sem, recv_sem,
@@ -441,7 +436,10 @@
     gate_full = g_all.reshape(-1, model_width)
     up_full = u_all.reshape(-1, model_width)
     down_full = d_all.reshape(-1, model_width)
-    returned = expert_return(arrived, gate_full, up_full, down_full, n_grp, 1)
+    gate_pre = jnp.einsum("scd,fd->scf", arrived, gate_full, preferred_element_type=jnp.float32)
+    up_pre = jnp.einsum("scd,fd->scf", arrived, up_full, preferred_element_type=jnp.float32)
+    hidden = (jax.nn.silu(gate_pre) * up_pre).astype(jnp.bfloat16)
+    returned = expert_return(hidden, down_full, n_grp, 1)
     returned = returned.reshape(n_slot, model_width)
 
     weight_of = jnp.sum(

time: 230 us -> 212 us (0.922)
  the two profiles are of different devices: /device:TPU:15 before, /device:TPU:2 now
where the time goes in v10:
time: 212 us; the launch traced here: 209 us
  Pallas kernels  173 us (82%)
  matrix products  30.6 us (14%)
  other arithmetic  4.03 us (2%)
    pallas_call x1, Pallas kernels, gather_weights(): pl.pallas_call(functools.partial(weight_kernel, n_x, n_grp), out_shape=(s...  99.6 us
    pallas_call x1, Pallas kernels, expert_return(): pl.pallas_call(functools.partial(expert_return_kernel, n_grp), out_shape=...  73.4 us
    dot_general x1, matrix products, per_device(): jnp.einsum('scd,fd->scf', arrived, up_full, preferred_element_type=jnp.fl...  11.8 us
    dot_general x1, matrix products, per_device(): jnp.einsum('scd,fd->scf', arrived, gate_full, preferred_element_type=jnp....  9.75 us

profile of v10, /device:TPU:2, one launch (start us, length us, event | category | flops | bytes accessed | tf_op | source)
XLA Modules:
  0.0 209.3 jit_solution(5400742926942409374)
XLA Ops:
  0.0 0.0 copy-start
  0.0 0.9 copy.21
  0.9 0.1 eq.35
  1.0 2.0 reduce-window.6
  3.0 0.3 slice_reduce_fusion
  3.4 0.1 bitcast_bitcast_fusion
  3.5 0.1 reduce_sum.21
  3.6 0.1 copy.24
  3.7 0.7 multiply_add_fusion
  4.4 0.6 fusion
  5.0 0.0 copy-done
  5.1 3.7 %convolution_convert_fusion = bf16[1152,2048]{1,0:T(8,128)(2,1)} fusion(pred[1152,144]{0,1:T(8,128)(4,1)S(1)} %fusion, bf16[144,2048]{1,0:T(8,128)(2,1)S(1)} %copy-done), kind=kOutput, calls=%fused_computation | convolution fusion | flops 681836544 | bytes 5474304 | tf_op jit(solution)/shard_map/dot_general | solution.py:430
  8.7 99.6 %shard_map.64 = (bf16[16,88,2048]{2,1,0:T(8,128)(2,1)}, bf16[16,88,2048]{2,1,0:T(8,128)(2,1)}, bf16[16,88,2048]{2,1,0:T(8,128)(2,1)}, bf16[16,72,2048]{2,1,0:T(8,128)(2,1)}) custom-call(bf16[2,88,2048]{2,1,0:T(8,128)(2,1)} %g_in.1, bf16[2,88,2048]{2,1,0:T(8,128)(2,1)} %u_in.1, bf16[2,88,2048]{2,1,0:T(8,128)(2,1)} %d_in.1, bf16[16,72,2048]{2,1,0:T(8,128)(2,1)} %bitcast.35), custom_call_target="tpu_custom_call" | custom-call | bytes 17301504 | tf_op jit(solution)/shard_map/pallas_call | solution.py:392
  108.3 0.0 copy-start.3
  108.3 0.0 copy-start.4
  108.3 11.8 %fusion.7 = f32[16,72,1408]{2,1,0:T(8,128)S(1)} fusion(bf16[16,72,2048]{2,1,0:T(8,128)(2,1)} %get-tuple-element.9, bf16[1408,2048,1]{1,0,2:T(8,128)(2,1)} %bitcast.41), kind=kOutput, calls=%fused_computation.22 | convolution fusion | flops 6643777536 | bytes 16973824 | tf_op jit(solution)/shard_map/scd,fd->scf/dot_general | solution.py:440
  120.1 0.0 copy-done.3
  120.1 0.0 copy-done.4
  120.1 9.8 %multiply_convert_fusion.hid_ref = bf16[16,72,1408]{2,1,0:T(8,128)(2,1)} fusion(f32[16,72,1408]{2,1,0:T(8,128)S(1)} %fusion.7, bf16[16,72,2048]{2,1,0:T(8,128)(2,1)S(1)} %copy-done.4, bf16[1408,2048,1]{1,0,2:T(8,128)(2,1)S(1)} %bitcast.40), kind=kOutput, calls=%fused_computation.1 | convolution fusion | flops 6653509632 | bytes 20217856 | tf_op jit(solution)/shard_map/scd,fd->scf/dot_general | solution.py:439
  129.9 0.0 copy-start.2
  129.9 73.4 %shard_map.65 = bf16[16,72,2048]{2,1,0:T(8,128)(2,1)} custom-call(bf16[16,72,1408]{2,1,0:T(8,128)(2,1)} %multiply_convert_fusion.hid_ref, bf16[1408,2048]{1,0:T(8,128)(2,1)} %bitcast.39), custom_call_target="tpu_custom_call" | custom-call | flops 6643777536 | bytes 18448384 | tf_op jit(solution)/shard_map/pallas_call | solution.py:266
  203.3 0.0 copy-start.1
  203.3 0.0 copy-done.2
  203.4 0.5 select_reduce_fusion
  203.9 3.6 %fusion.4 = f32[144,2048]{1,0:T(8,128)S(1)} fusion(bf16[1152,2048]{1,0:T(8,128)(2,1)} %bitcast.36, f32[1152,144]{0,1:T(8,128)S(1)} %select_reduce_fusion), kind=kOutput, calls=%fused_computation.10 | convolution fusion | flops 679809024 | bytes 6561792 | tf_op jit(solution)/shard_map/dot_general | solution.py:451
  207.5 0.0 copy-done.1
  207.5 1.8 fusion.1
  (4 shorter events, 0.1 us)
Async XLA Ops:
  0.0 5.0 %copy-start = (bf16[144,2048]{1,0:T(8,128)(2,1)S(1)}, bf16[144,2048]{1,0:T(8,128)(2,1)}, u32[]{:S(2)}) copy-start(bf16[144,2048]{1,0:T(8,128)(2,1)} %param.6) | copy-start | bytes 1769476
  108.3 11.8 %copy-start.3 = (bf16[16,88,2048]{2,1,0:T(8,128)(2,1)S(1)}, bf16[16,88,2048]{2,1,0:T(8,128)(2,1)}, u32[]{:S(2)}) copy-start(bf16[16,88,2048]{2,1,0:T(8,128)(2,1)} %get-tuple-element.10) | copy-start | bytes 17301508
  108.3 11.8 %copy-start.4 = (bf16[16,72,2048]{2,1,0:T(8,128)(2,1)S(1)}, bf16[16,72,2048]{2,1,0:T(8,128)(2,1)}, u32[]{:S(2)}) copy-start(bf16[16,72,2048]{2,1,0:T(8,128)(2,1)} %get-tuple-element.9) | copy-start | bytes 14155780
  129.9 73.5 %copy-start.2 = (f32[144,6]{0,1:T(8,128)S(1)}, f32[144,6]{0,1:T(8,128)}, u32[]{:S(2)}) copy-start(f32[144,6]{0,1:T(8,128)} %param.8) | copy-start | bytes 10372
  203.3 4.1 %copy-start.1 = (bf16[16,72,2048]{2,1,0:T(8,128)(2,1)S(1)}, bf16[16,72,2048]{2,1,0:T(8,128)(2,1)}, u32[]{:S(2)}) copy-start(bf16[16,72,2048]{2,1,0:T(8,128)(2,1)} %shard_map.65) | copy-start | bytes 14155780

commit v11 on v10

--- a/solution.py
+++ b/solution.py
@@ -156,8 +156,8 @@
     )(x)
 
 
-def expert_return_kernel(n_grp, hid_ref, down_ref, y_ref, buf, stage, send_sem, recv_sem, stage_sem,
-                         local_sem):
+def expert_return_kernel(n_grp, gate_ref, up_ref, down_ref, y_ref, buf, stage, send_sem, recv_sem,
+                         stage_sem, local_sem):
     me, at, direct, relayed = plane_plan(n_grp)
     n_rel = len(relayed)
     order = [off for off, rel in relayed] + direct + [(0, 0)]
@@ -180,7 +180,8 @@
 
     def project(k):
         p, _ = chunk_of(k)
-        buf[p] = jnp.dot(hid_ref[p], down_ref[...], preferred_element_type=jnp.float32).astype(buf.dtype)
+        hidden = (jax.nn.silu(gate_ref[p]) * up_ref[p]).astype(jnp.bfloat16)
+        buf[p] = jnp.dot(hidden, down_ref[...], preferred_element_type=jnp.float32).astype(buf.dtype)
 
     def first_hop(k):
         p, _ = chunk_of(k)
@@ -256,17 +257,17 @@
         ).wait_recv()
 
 
-def expert_return(hidden, down_full, n_grp, collective_id):
-    n_src, cap, ff = hidden.shape
+def expert_return(gate_pre, up_pre, down_full, n_grp, collective_id):
+    n_src, cap, ff = gate_pre.shape
     width = down_full.shape[1]
     out = jax.ShapeDtypeStruct((n_src, cap, width), jnp.bfloat16)
     vmem = pl.BlockSpec(memory_space=pltpu.VMEM)
     flops = 2 * n_src * cap * ff * width
-    nbytes = hidden.size * 2 + down_full.size * 2 + 2 * n_src * cap * width * 2
+    nbytes = gate_pre.size * 8 + down_full.size * 2 + 2 * n_src * cap * width * 2
     return pl.pallas_call(
         functools.partial(expert_return_kernel, n_grp),
         out_shape=out,
-        in_specs=[vmem] * 2,
+        in_specs=[vmem] * 3,
         out_specs=pl.BlockSpec(memory_space=pl.ANY),
         scratch_shapes=[
             pltpu.VMEM((n_src, cap, width), jnp.bfloat16),
@@ -279,8 +280,8 @@
         compiler_params=pltpu.CompilerParams(
             collective_id=collective_id, has_side_effects=True, vmem_limit_bytes=56 * 1024 * 1024
         ),
-        cost_estimate=pl.CostEstimate(flops=flops, transcendentals=0, bytes_accessed=nbytes),
-    )(hidden, down_full)
+        cost_estimate=pl.CostEstimate(flops=flops, transcendentals=gate_pre.size, bytes_accessed=nbytes),
+    )(gate_pre, up_pre, down_full)
 
 
 def weight_kernel(n_x, n_grp, g_in, u_in, d_in, t_in, g_out, u_out, d_out, t_out, send_sem, recv_sem,
@@ -438,8 +439,7 @@
     down_full = d_all.reshape(-1, model_width)
     gate_pre = jnp.einsum("scd,fd->scf", arrived, gate_full, preferred_element_type=jnp.float32)
     up_pre = jnp.einsum("scd,fd->scf", arrived, up_full, preferred_element_type=jnp.float32)
-    hidden = (jax.nn.silu(gate_pre) * up_pre).astype(jnp.bfloat16)
-    returned = expert_return(hidden, down_full, n_grp, 1)
+    returned = expert_return(gate_pre, up_pre, down_full, n_grp, 1)
     returned = returned.reshape(n_slot, model_width)
 
     weight_of = jnp.sum(

time: 212 us -> 216 us (1.019)
  Pallas kernels: 173 us -> 176 us
    pallas_call x1, Pallas kernels: 73.4 us -> 76 us  [expert_return(): pl.pallas_call(functools.partial(expert_return_kernel, n_grp), out_shape=...]
where the time goes in v11:
time: 216 us; the launch traced here: 213 us
  Pallas kernels  176 us (81%)
  matrix products  31.4 us (15%)
  other arithmetic  4.03 us (2%)
    pallas_call x1, Pallas kernels, gather_weights(): pl.pallas_call(functools.partial(weight_kernel, n_x, n_grp), out_shape=(s...  99.6 us
    pallas_call x1, Pallas kernels, expert_return(): pl.pallas_call(functools.partial(expert_return_kernel, n_grp), out_shape=...  76 us
    dot_general x1, matrix products, per_device(): jnp.einsum('scd,fd->scf', arrived, up_full, preferred_element_type=jnp.fl...  12.9 us
    dot_general x1, matrix products, per_device(): jnp.einsum('scd,fd->scf', arrived, gate_full, preferred_element_type=jnp....  9.4 us

profile of v11, /device:TPU:2, one launch (start us, length us, event | category | flops | bytes accessed | tf_op | source)
XLA Modules:
  0.0 212.7 jit_solution(5914186351002076260)
XLA Ops:
  0.0 0.0 copy-start
  0.0 0.9 copy.21
  0.9 0.1 eq.35
  1.0 2.0 reduce-window.6
  3.0 0.3 slice_reduce_fusion
  3.4 0.1 bitcast_bitcast_fusion
  3.5 0.1 reduce_sum.21
  3.6 0.1 copy.24
  3.7 0.7 multiply_add_fusion
  4.4 0.6 fusion
  5.0 0.0 copy-done
  5.1 3.7 %convolution_convert_fusion = bf16[1152,2048]{1,0:T(8,128)(2,1)} fusion(pred[1152,144]{0,1:T(8,128)(4,1)S(1)} %fusion, bf16[144,2048]{1,0:T(8,128)(2,1)S(1)} %copy-done), kind=kOutput, calls=%fused_computation | convolution fusion | flops 681836544 | bytes 5474304 | tf_op jit(solution)/shard_map/dot_general | solution.py:431
  8.7 99.6 %shard_map.64 = (bf16[16,88,2048]{2,1,0:T(8,128)(2,1)}, bf16[16,88,2048]{2,1,0:T(8,128)(2,1)}, bf16[16,88,2048]{2,1,0:T(8,128)(2,1)}, bf16[16,72,2048]{2,1,0:T(8,128)(2,1)}) custom-call(bf16[2,88,2048]{2,1,0:T(8,128)(2,1)} %g_in.1, bf16[2,88,2048]{2,1,0:T(8,128)(2,1)} %u_in.1, bf16[2,88,2048]{2,1,0:T(8,128)(2,1)} %d_in.1, bf16[16,72,2048]{2,1,0:T(8,128)(2,1)} %bitcast.35), custom_call_target="tpu_custom_call" | custom-call | bytes 17301504 | tf_op jit(solution)/shard_map/pallas_call | solution.py:393
  108.3 0.0 copy-start.3
  108.4 0.0 copy-start.4
  108.4 12.9 %fusion.8.up_ref = f32[16,72,1408]{2,1,0:T(8,128)} fusion(bf16[16,72,2048]{2,1,0:T(8,128)(2,1)} %get-tuple-element.9, bf16[1408,2048,1]{1,0,2:T(8,128)(2,1)} %bitcast.41), kind=kOutput, calls=%fused_computation.22 | convolution fusion | flops 6643777536 | bytes 16973824 | tf_op jit(solution)/shard_map/scd,fd->scf/dot_general | solution.py:441
  121.3 0.0 copy-done.3
  121.3 0.0 copy-done.4
  121.3 9.4 %fusion.7.gate_ref = f32[16,72,1408]{2,1,0:T(8,128)} fusion(bf16[16,72,2048]{2,1,0:T(8,128)(2,1)S(1)} %copy-done.4, bf16[1408,2048,1]{1,0,2:T(8,128)(2,1)S(1)} %bitcast.40), kind=kOutput, calls=%fused_computation.21 | convolution fusion | flops 6643777536 | bytes 16973824 | tf_op jit(solution)/shard_map/scd,fd->scf/dot_general | solution.py:440
  130.7 0.0 copy-start.2
  130.7 76.0 %shard_map.65 = bf16[16,72,2048]{2,1,0:T(8,128)(2,1)} custom-call(f32[16,72,1408]{2,1,0:T(8,128)} %fusion.7.gate_ref, f32[16,72,1408]{2,1,0:T(8,128)} %fusion.8.up_ref, bf16[1408,2048]{1,0:T(8,128)(2,1)} %bitcast.39), custom_call_target="tpu_custom_call" | custom-call | flops 6643777536 | bytes 28180480 | tf_op jit(solution)/shard_map/pallas_call | solution.py:267
  206.7 0.0 copy-start.1
  206.7 0.0 copy-done.2
  206.8 0.5 select_reduce_fusion
  207.3 3.6 %fusion.4 = f32[144,2048]{1,0:T(8,128)S(1)} fusion(bf16[1152,2048]{1,0:T(8,128)(2,1)} %bitcast.36, f32[1152,144]{0,1:T(8,128)S(1)} %select_reduce_fusion), kind=kOutput, calls=%fused_computation.9 | convolution fusion | flops 679809024 | bytes 6561792 | tf_op jit(solution)/shard_map/dot_general | solution.py:451
  210.9 0.0 copy-done.1
  210.9 1.8 fusion.1
  (4 shorter events, 0.1 us)
Async XLA Ops:
  0.0 5.0 %copy-start = (bf16[144,2048]{1,0:T(8,128)(2,1)S(1)}, bf16[144,2048]{1,0:T(8,128)(2,1)}, u32[]{:S(2)}) copy-start(bf16[144,2048]{1,0:T(8,128)(2,1)} %param.6) | copy-start | bytes 1769476
  108.3 12.9 %copy-start.3 = (bf16[16,88,2048]{2,1,0:T(8,128)(2,1)S(1)}, bf16[16,88,2048]{2,1,0:T(8,128)(2,1)}, u32[]{:S(2)}) copy-start(bf16[16,88,2048]{2,1,0:T(8,128)(2,1)} %get-tuple-element.10) | copy-start | bytes 17301508
  108.4 12.9 %copy-start.4 = (bf16[16,72,2048]{2,1,0:T(8,128)(2,1)S(1)}, bf16[16,72,2048]{2,1,0:T(8,128)(2,1)}, u32[]{:S(2)}) copy-start(bf16[16,72,2048]{2,1,0:T(8,128)(2,1)} %get-tuple-element.9) | copy-start | bytes 14155780
  130.7 76.1 %copy-start.2 = (f32[144,6]{0,1:T(8,128)S(1)}, f32[144,6]{0,1:T(8,128)}, u32[]{:S(2)}) copy-start(f32[144,6]{0,1:T(8,128)} %param.8) | copy-start | bytes 10372
  206.7 4.1 %copy-start.1 = (bf16[16,72,2048]{2,1,0:T(8,128)(2,1)S(1)}, bf16[16,72,2048]{2,1,0:T(8,128)(2,1)}, u32[]{:S(2)}) copy-start(bf16[16,72,2048]{2,1,0:T(8,128)(2,1)} %shard_map.65) | copy-start | bytes 14155780

commit v12 on v10

--- a/solution.py
+++ b/solution.py
@@ -350,14 +350,14 @@
     sent += send(lambda m: ins[m].at[1 - h], me, z_peer)
     for dev in [partner] + x_devs:
         sent += send(lambda m: ins[m].at[h], me, dev)
-    t_local, t_copies, t_k = start_plane(
-        n_grp, t_in, t_out, stage, t_send, t_recv, stage_sem, local_sem.at[3]
-    )
 
     z_blk = block(x, 1 - h, c)
     wait_in(z_blk)
     for dev in [partner] + x_devs:
         sent += send(lambda m: outs[m].at[z_blk], z_blk, dev)
+    t_local, t_copies, t_k = start_plane(
+        n_grp, t_in, t_out, stage, t_send, t_recv, stage_sem, local_sem.at[3]
+    )
     t_copies += relay_plane(n_grp, t_k, t_in, t_out, stage, t_send, t_recv, stage_sem)
 
     for hh in (h, 1 - h):

time: 212 us -> 200 us (0.943); the launches traced: 209 us -> 199 us
  Pallas kernels: 173 us -> 163 us
    pallas_call x1, Pallas kernels: 99.6 us -> 88 us  [gather_weights(): pl.pallas_call(functools.partial(weight_kernel, n_x, n_grp), out_shape=(s...]
where the time goes in v12:
time: 200 us; the launch traced here: 199 us
  Pallas kernels  163 us (82%)
  matrix products  30.6 us (15%)
  other arithmetic  4.03 us (2%)
    pallas_call x1, Pallas kernels, gather_weights(): pl.pallas_call(functools.partial(weight_kernel, n_x, n_grp), out_shape=(s...  88 us
    pallas_call x1, Pallas kernels, expert_return(): pl.pallas_call(functools.partial(expert_return_kernel, n_grp), out_shape=...  75.2 us
    dot_general x1, matrix products, per_device(): jnp.einsum('scd,fd->scf', arrived, up_full, preferred_element_type=jnp.fl...  11.8 us
    dot_general x1, matrix products, per_device(): jnp.einsum('scd,fd->scf', arrived, gate_full, preferred_element_type=jnp....  9.76 us

profile of v12, /device:TPU:2, one launch (start us, length us, event | category | flops | bytes accessed | tf_op | source)
XLA Modules:
  0.0 199.4 jit_solution(18101105195380439354)
XLA Ops:
  0.0 0.0 copy-start
  0.0 0.9 copy.21
  0.9 0.1 eq.35
  1.0 2.0 %reduce-window.6 = s32[16,7,128]{2,0,1:T(8,128)S(1)} reduce-window(s32[16,7,128]{2,0,1:T(8,128)S(1)} %copy_bitcast_fusion, s32[]{:T(128)} %constant.14.clone.1), window={size=1x1x128 pad=0_0x0_0x127_0}, to_apply=%region_0.0 | reduce-window | flops 1820672 | bytes 114692 | tf_op jit(solution)/shard_map/reduce-window
  3.0 0.3 slice_reduce_fusion
  3.4 0.1 bitcast_bitcast_fusion
  3.5 0.1 reduce_sum.21
  3.6 0.1 copy.24
  3.7 0.7 multiply_add_fusion
  4.4 0.6 fusion
  5.0 0.0 copy-done
  5.1 3.7 %convolution_convert_fusion = bf16[1152,2048]{1,0:T(8,128)(2,1)} fusion(pred[1152,144]{0,1:T(8,128)(4,1)S(1)} %fusion, bf16[144,2048]{1,0:T(8,128)(2,1)S(1)} %copy-done), kind=kOutput, calls=%fused_computation | convolution fusion | flops 681836544 | bytes 5474304 | tf_op jit(solution)/shard_map/dot_general | solution.py:430
  8.7 88.0 %shard_map.64 = (bf16[16,88,2048]{2,1,0:T(8,128)(2,1)}, bf16[16,88,2048]{2,1,0:T(8,128)(2,1)}, bf16[16,88,2048]{2,1,0:T(8,128)(2,1)}, bf16[16,72,2048]{2,1,0:T(8,128)(2,1)}) custom-call(bf16[2,88,2048]{2,1,0:T(8,128)(2,1)} %g_in.1, bf16[2,88,2048]{2,1,0:T(8,128)(2,1)} %u_in.1, bf16[2,88,2048]{2,1,0:T(8,128)(2,1)} %d_in.1, bf16[16,72,2048]{2,1,0:T(8,128)(2,1)} %bitcast.35), custom_call_target="tpu_custom_call" | custom-call | bytes 17301504 | tf_op jit(solution)/shard_map/pallas_call | solution.py:392
  96.7 0.0 copy-start.3
  96.7 0.0 copy-start.4
  96.7 11.8 %fusion.7 = f32[16,72,1408]{2,1,0:T(8,128)S(1)} fusion(bf16[16,72,2048]{2,1,0:T(8,128)(2,1)} %get-tuple-element.9, bf16[1408,2048,1]{1,0,2:T(8,128)(2,1)} %bitcast.41), kind=kOutput, calls=%fused_computation.22 | convolution fusion | flops 6643777536 | bytes 16973824 | tf_op jit(solution)/shard_map/scd,fd->scf/dot_general | solution.py:440
  108.5 0.0 copy-done.3
  108.5 0.0 copy-done.4
  108.5 9.8 %multiply_convert_fusion.hid_ref = bf16[16,72,1408]{2,1,0:T(8,128)(2,1)} fusion(f32[16,72,1408]{2,1,0:T(8,128)S(1)} %fusion.7, bf16[16,72,2048]{2,1,0:T(8,128)(2,1)S(1)} %copy-done.4, bf16[1408,2048,1]{1,0,2:T(8,128)(2,1)S(1)} %bitcast.40), kind=kOutput, calls=%fused_computation.1 | convolution fusion | flops 6653509632 | bytes 20217856 | tf_op jit(solution)/shard_map/scd,fd->scf/dot_general | solution.py:439
  118.3 0.0 copy-start.2
  118.3 75.2 %shard_map.65 = bf16[16,72,2048]{2,1,0:T(8,128)(2,1)} custom-call(bf16[16,72,1408]{2,1,0:T(8,128)(2,1)} %multiply_convert_fusion.hid_ref, bf16[1408,2048]{1,0:T(8,128)(2,1)} %bitcast.39), custom_call_target="tpu_custom_call" | custom-call | flops 6643777536 | bytes 18448384 | tf_op jit(solution)/shard_map/pallas_call | solution.py:266
  193.5 0.0 copy-start.1
  193.5 0.0 copy-done.2
  193.5 0.5 select_reduce_fusion
  194.0 3.6 %fusion.4 = f32[144,2048]{1,0:T(8,128)S(1)} fusion(bf16[1152,2048]{1,0:T(8,128)(2,1)} %bitcast.36, f32[1152,144]{0,1:T(8,128)S(1)} %select_reduce_fusion), kind=kOutput, calls=%fused_computation.10 | convolution fusion | flops 679809024 | bytes 6561792 | tf_op jit(solution)/shard_map/dot_general | solution.py:451
  197.6 0.0 copy-done.1
  197.6 1.8 fusion.1
  (4 shorter events, 0.1 us)
Async XLA Ops:
  0.0 5.0 %copy-start = (bf16[144,2048]{1,0:T(8,128)(2,1)S(1)}, bf16[144,2048]{1,0:T(8,128)(2,1)}, u32[]{:S(2)}) copy-start(bf16[144,2048]{1,0:T(8,128)(2,1)} %param.6) | copy-start | bytes 1769476
  96.7 11.8 %copy-start.3 = (bf16[16,88,2048]{2,1,0:T(8,128)(2,1)S(1)}, bf16[16,88,2048]{2,1,0:T(8,128)(2,1)}, u32[]{:S(2)}) copy-start(bf16[16,88,2048]{2,1,0:T(8,128)(2,1)} %get-tuple-element.10) | copy-start | bytes 17301508
  96.7 11.8 %copy-start.4 = (bf16[16,72,2048]{2,1,0:T(8,128)(2,1)S(1)}, bf16[16,72,2048]{2,1,0:T(8,128)(2,1)}, u32[]{:S(2)}) copy-start(bf16[16,72,2048]{2,1,0:T(8,128)(2,1)} %get-tuple-element.9) | copy-start | bytes 14155780
  118.3 75.2 %copy-start.2 = (f32[144,6]{0,1:T(8,128)S(1)}, f32[144,6]{0,1:T(8,128)}, u32[]{:S(2)}) copy-start(f32[144,6]{0,1:T(8,128)} %param.8) | copy-start | bytes 10372
  193.5 4.1 %copy-start.1 = (bf16[16,72,2048]{2,1,0:T(8,128)(2,1)S(1)}, bf16[16,72,2048]{2,1,0:T(8,128)(2,1)}, u32[]{:S(2)}) copy-start(bf16[16,72,2048]{2,1,0:T(8,128)(2,1)} %shard_map.65) | copy-start | bytes 14155780

commit v13 on v12

--- a/solution.py
+++ b/solution.py
@@ -358,13 +358,13 @@
     t_local, t_copies, t_k = start_plane(
         n_grp, t_in, t_out, stage, t_send, t_recv, stage_sem, local_sem.at[3]
     )
-    t_copies += relay_plane(n_grp, t_k, t_in, t_out, stage, t_send, t_recv, stage_sem)
 
     for hh in (h, 1 - h):
         blk = block(away, hh, c)
         wait_in(blk)
         sent += send(lambda m: outs[m].at[blk], blk, partner)
         sent += send(lambda m: outs[m].at[blk], blk, {"x": toward})
+    t_copies += relay_plane(n_grp, t_k, t_in, t_out, stage, t_send, t_recv, stage_sem)
     for xp in (toward, far_x):
         for hh in (h, 1 - h):
             blk = block(xp, hh, c)

time: 200 us -> 204 us (1.020)
  the two profiles are of different devices: /device:TPU:2 before, /device:TPU:29 now
where the time goes in v13:
time: 204 us
  Pallas kernels  168 us (82%)
  matrix products  30.6 us (15%)
  other arithmetic  4.03 us (2%)
    pallas_call x1, Pallas kernels, gather_weights(): pl.pallas_call(functools.partial(weight_kernel, n_x, n_grp), out_shape=(s...  90.8 us
    pallas_call x1, Pallas kernels, expert_return(): pl.pallas_call(functools.partial(expert_return_kernel, n_grp), out_shape=...  77.1 us
    dot_general x1, matrix products, per_device(): jnp.einsum('scd,fd->scf', arrived, up_full, preferred_element_type=jnp.fl...  11.8 us
    dot_general x1, matrix products, per_device(): jnp.einsum('scd,fd->scf', arrived, gate_full, preferred_element_type=jnp....  9.75 us

profile of v13, /device:TPU:29, one launch (start us, length us, event | category | flops | bytes accessed | tf_op | source)
XLA Modules:
  0.0 204.3 jit_solution(14566531963224282785)
XLA Ops:
  0.0 0.0 copy-start
  0.0 0.9 copy.21
  0.9 0.1 eq.35
  1.0 2.0 reduce-window.6
  3.0 0.3 slice_reduce_fusion
  3.4 0.1 bitcast_bitcast_fusion
  3.5 0.1 reduce_sum.21
  3.6 0.1 copy.24
  3.7 0.7 multiply_add_fusion
  4.4 0.6 fusion
  5.0 0.0 copy-done
  5.1 3.7 %convolution_convert_fusion = bf16[1152,2048]{1,0:T(8,128)(2,1)} fusion(pred[1152,144]{0,1:T(8,128)(4,1)S(1)} %fusion, bf16[144,2048]{1,0:T(8,128)(2,1)S(1)} %copy-done), kind=kOutput, calls=%fused_computation | convolution fusion | flops 681836544 | bytes 5474304 | tf_op jit(solution)/shard_map/dot_general | solution.py:430
  8.7 90.8 %shard_map.64 = (bf16[16,88,2048]{2,1,0:T(8,128)(2,1)}, bf16[16,88,2048]{2,1,0:T(8,128)(2,1)}, bf16[16,88,2048]{2,1,0:T(8,128)(2,1)}, bf16[16,72,2048]{2,1,0:T(8,128)(2,1)}) custom-call(bf16[2,88,2048]{2,1,0:T(8,128)(2,1)} %g_in.1, bf16[2,88,2048]{2,1,0:T(8,128)(2,1)} %u_in.1, bf16[2,88,2048]{2,1,0:T(8,128)(2,1)} %d_in.1, bf16[16,72,2048]{2,1,0:T(8,128)(2,1)} %bitcast.35), custom_call_target="tpu_custom_call" | custom-call | bytes 17301504 | tf_op jit(solution)/shard_map/pallas_call | solution.py:392
  99.6 0.0 copy-start.3
  99.6 0.0 copy-start.4
  99.6 11.8 %fusion.7 = f32[16,72,1408]{2,1,0:T(8,128)S(1)} fusion(bf16[16,72,2048]{2,1,0:T(8,128)(2,1)} %get-tuple-element.9, bf16[1408,2048,1]{1,0,2:T(8,128)(2,1)} %bitcast.41), kind=kOutput, calls=%fused_computation.22 | convolution fusion | flops 6643777536 | bytes 16973824 | tf_op jit(solution)/shard_map/scd,fd->scf/dot_general | solution.py:440
  111.4 0.0 copy-done.3
  111.4 0.0 copy-done.4
  111.4 9.8 %multiply_convert_fusion.hid_ref = bf16[16,72,1408]{2,1,0:T(8,128)(2,1)} fusion(f32[16,72,1408]{2,1,0:T(8,128)S(1)} %fusion.7, bf16[16,72,2048]{2,1,0:T(8,128)(2,1)S(1)} %copy-done.4, bf16[1408,2048,1]{1,0,2:T(8,128)(2,1)S(1)} %bitcast.40), kind=kOutput, calls=%fused_computation.1 | convolution fusion | flops 6653509632 | bytes 20217856 | tf_op jit(solution)/shard_map/scd,fd->scf/dot_general | solution.py:439
  121.1 0.0 copy-start.2
  121.1 77.1 %shard_map.65 = bf16[16,72,2048]{2,1,0:T(8,128)(2,1)} custom-call(bf16[16,72,1408]{2,1,0:T(8,128)(2,1)} %multiply_convert_fusion.hid_ref, bf16[1408,2048]{1,0:T(8,128)(2,1)} %bitcast.39), custom_call_target="tpu_custom_call" | custom-call | flops 6643777536 | bytes 18448384 | tf_op jit(solution)/shard_map/pallas_call | solution.py:266
  198.3 0.0 copy-start.1
  198.3 0.0 copy-done.2
  198.3 0.5 select_reduce_fusion
  198.9 3.6 %fusion.4 = f32[144,2048]{1,0:T(8,128)S(1)} fusion(bf16[1152,2048]{1,0:T(8,128)(2,1)} %bitcast.36, f32[1152,144]{0,1:T(8,128)S(1)} %select_reduce_fusion), kind=kOutput, calls=%fused_computation.10 | convolution fusion | flops 679809024 | bytes 6561792 | tf_op jit(solution)/shard_map/dot_general | solution.py:451
  202.4 0.0 copy-done.1
  202.4 1.8 fusion.1
  (4 shorter events, 0.1 us)
Async XLA Ops:
  0.0 5.0 %copy-start = (bf16[144,2048]{1,0:T(8,128)(2,1)S(1)}, bf16[144,2048]{1,0:T(8,128)(2,1)}, u32[]{:S(2)}) copy-start(bf16[144,2048]{1,0:T(8,128)(2,1)} %param.6) | copy-start | bytes 1769476
  99.6 11.8 %copy-start.3 = (bf16[16,88,2048]{2,1,0:T(8,128)(2,1)S(1)}, bf16[16,88,2048]{2,1,0:T(8,128)(2,1)}, u32[]{:S(2)}) copy-start(bf16[16,88,2048]{2,1,0:T(8,128)(2,1)} %get-tuple-element.10) | copy-start | bytes 17301508
  99.6 11.8 %copy-start.4 = (bf16[16,72,2048]{2,1,0:T(8,128)(2,1)S(1)}, bf16[16,72,2048]{2,1,0:T(8,128)(2,1)}, u32[]{:S(2)}) copy-start(bf16[16,72,2048]{2,1,0:T(8,128)(2,1)} %get-tuple-element.9) | copy-start | bytes 14155780
  121.1 77.2 %copy-start.2 = (f32[144,6]{0,1:T(8,128)S(1)}, f32[144,6]{0,1:T(8,128)}, u32[]{:S(2)}) copy-start(f32[144,6]{0,1:T(8,128)} %param.8) | copy-start | bytes 10372
  198.3 4.1 %copy-start.1 = (bf16[16,72,2048]{2,1,0:T(8,128)(2,1)S(1)}, bf16[16,72,2048]{2,1,0:T(8,128)(2,1)}, u32[]{:S(2)}) copy-start(bf16[16,72,2048]{2,1,0:T(8,128)(2,1)} %shard_map.65) | copy-start | bytes 14155780

commit v14 on v12

--- a/solution.py
+++ b/solution.py
@@ -227,7 +227,7 @@
         def _():
             direct_send(k - 1).start()
 
-        @pl.when(k == n_rel + 4)
+        @pl.when(k == n_rel + 2)
         def _():
             forwards()
 

time: 200 us -> 204 us (1.020)
  the two profiles are of different devices: /device:TPU:2 before, /device:TPU:42 now
where the time goes in v14:
time: 204 us
  Pallas kernels  168 us (82%)
  matrix products  30.6 us (15%)
  other arithmetic  4.03 us (2%)
    pallas_call x1, Pallas kernels, gather_weights(): pl.pallas_call(functools.partial(weight_kernel, n_x, n_grp), out_shape=(s...  87.2 us
    pallas_call x1, Pallas kernels, expert_return(): pl.pallas_call(functools.partial(expert_return_kernel, n_grp), out_shape=...  80.4 us
    dot_general x1, matrix products, per_device(): jnp.einsum('scd,fd->scf', arrived, up_full, preferred_element_type=jnp.fl...  11.8 us
    dot_general x1, matrix products, per_device(): jnp.einsum('scd,fd->scf', arrived, gate_full, preferred_element_type=jnp....  9.76 us

profile of v14, /device:TPU:42, one launch (start us, length us, event | category | flops | bytes accessed | tf_op | source)
XLA Modules:
  0.0 203.9 jit_solution(9215037450288838536)
XLA Ops:
  0.0 0.0 copy-start
  0.0 0.9 copy.21
  0.9 0.1 eq.35
  1.0 2.0 reduce-window.6
  3.0 0.3 slice_reduce_fusion
  3.4 0.1 bitcast_bitcast_fusion
  3.5 0.1 reduce_sum.21
  3.6 0.1 copy.24
  3.7 0.7 multiply_add_fusion
  4.4 0.6 fusion
  5.0 0.0 copy-done
  5.1 3.7 %convolution_convert_fusion = bf16[1152,2048]{1,0:T(8,128)(2,1)} fusion(pred[1152,144]{0,1:T(8,128)(4,1)S(1)} %fusion, bf16[144,2048]{1,0:T(8,128)(2,1)S(1)} %copy-done), kind=kOutput, calls=%fused_computation | convolution fusion | flops 681836544 | bytes 5474304 | tf_op jit(solution)/shard_map/dot_general | solution.py:430
  8.7 87.2 %shard_map.64 = (bf16[16,88,2048]{2,1,0:T(8,128)(2,1)}, bf16[16,88,2048]{2,1,0:T(8,128)(2,1)}, bf16[16,88,2048]{2,1,0:T(8,128)(2,1)}, bf16[16,72,2048]{2,1,0:T(8,128)(2,1)}) custom-call(bf16[2,88,2048]{2,1,0:T(8,128)(2,1)} %g_in.1, bf16[2,88,2048]{2,1,0:T(8,128)(2,1)} %u_in.1, bf16[2,88,2048]{2,1,0:T(8,128)(2,1)} %d_in.1, bf16[16,72,2048]{2,1,0:T(8,128)(2,1)} %bitcast.35), custom_call_target="tpu_custom_call" | custom-call | bytes 17301504 | tf_op jit(solution)/shard_map/pallas_call | solution.py:392
  96.0 0.0 copy-start.3
  96.0 0.0 copy-start.4
  96.0 11.8 %fusion.7 = f32[16,72,1408]{2,1,0:T(8,128)S(1)} fusion(bf16[16,72,2048]{2,1,0:T(8,128)(2,1)} %get-tuple-element.9, bf16[1408,2048,1]{1,0,2:T(8,128)(2,1)} %bitcast.41), kind=kOutput, calls=%fused_computation.22 | convolution fusion | flops 6643777536 | bytes 16973824 | tf_op jit(solution)/shard_map/scd,fd->scf/dot_general | solution.py:440
  107.8 0.0 copy-done.3
  107.8 0.0 copy-done.4
  107.8 9.8 %multiply_convert_fusion.hid_ref = bf16[16,72,1408]{2,1,0:T(8,128)(2,1)} fusion(f32[16,72,1408]{2,1,0:T(8,128)S(1)} %fusion.7, bf16[16,72,2048]{2,1,0:T(8,128)(2,1)S(1)} %copy-done.4, bf16[1408,2048,1]{1,0,2:T(8,128)(2,1)S(1)} %bitcast.40), kind=kOutput, calls=%fused_computation.1 | convolution fusion | flops 6653509632 | bytes 20217856 | tf_op jit(solution)/shard_map/scd,fd->scf/dot_general | solution.py:439
  117.6 0.0 copy-start.2
  117.6 80.4 %shard_map.65 = bf16[16,72,2048]{2,1,0:T(8,128)(2,1)} custom-call(bf16[16,72,1408]{2,1,0:T(8,128)(2,1)} %multiply_convert_fusion.hid_ref, bf16[1408,2048]{1,0:T(8,128)(2,1)} %bitcast.39), custom_call_target="tpu_custom_call" | custom-call | flops 6643777536 | bytes 18448384 | tf_op jit(solution)/shard_map/pallas_call | solution.py:266
  198.0 0.0 copy-start.1
  198.0 0.0 copy-done.2
  198.0 0.5 select_reduce_fusion
  198.5 3.6 %fusion.4 = f32[144,2048]{1,0:T(8,128)S(1)} fusion(bf16[1152,2048]{1,0:T(8,128)(2,1)} %bitcast.36, f32[1152,144]{0,1:T(8,128)S(1)} %select_reduce_fusion), kind=kOutput, calls=%fused_computation.10 | convolution fusion | flops 679809024 | bytes 6561792 | tf_op jit(solution)/shard_map/dot_general | solution.py:451
  202.1 0.0 copy-done.1
  202.1 1.8 fusion.1
  (4 shorter events, 0.1 us)
Async XLA Ops:
  0.0 5.0 %copy-start = (bf16[144,2048]{1,0:T(8,128)(2,1)S(1)}, bf16[144,2048]{1,0:T(8,128)(2,1)}, u32[]{:S(2)}) copy-start(bf16[144,2048]{1,0:T(8,128)(2,1)} %param.6) | copy-start | bytes 1769476
  96.0 11.8 %copy-start.3 = (bf16[16,88,2048]{2,1,0:T(8,128)(2,1)S(1)}, bf16[16,88,2048]{2,1,0:T(8,128)(2,1)}, u32[]{:S(2)}) copy-start(bf16[16,88,2048]{2,1,0:T(8,128)(2,1)} %get-tuple-element.10) | copy-start | bytes 17301508
  96.0 11.8 %copy-start.4 = (bf16[16,72,2048]{2,1,0:T(8,128)(2,1)S(1)}, bf16[16,72,2048]{2,1,0:T(8,128)(2,1)}, u32[]{:S(2)}) copy-start(bf16[16,72,2048]{2,1,0:T(8,128)(2,1)} %get-tuple-element.9) | copy-start | bytes 14155780
  117.6 80.4 %copy-start.2 = (f32[144,6]{0,1:T(8,128)S(1)}, f32[144,6]{0,1:T(8,128)}, u32[]{:S(2)}) copy-start(f32[144,6]{0,1:T(8,128)} %param.8) | copy-start | bytes 10372
  198.0 4.1 %copy-start.1 = (bf16[16,72,2048]{2,1,0:T(8,128)(2,1)S(1)}, bf16[16,72,2048]{2,1,0:T(8,128)(2,1)}, u32[]{:S(2)}) copy-start(bf16[16,72,2048]{2,1,0:T(8,128)(2,1)} %shard_map.65) | copy-start | bytes 14155780

commit v15 on v10

--- a/solution.py
+++ b/solution.py
@@ -76,12 +76,13 @@
     return me, at, direct, relayed
 
 
-def start_plane(n_grp, x_ref, y_ref, stage, send_sem, recv_sem, stage_sem, local_sem):
+def start_plane(n_grp, x_ref, y_ref, stage, send_sem, recv_sem, stage_sem, local_sem, part, k=0):
     me, at, direct, relayed = plane_plan(n_grp)
     copies = []
-    local = pltpu.make_async_copy(x_ref.at[me], y_ref.at[me], local_sem)
-    local.start()
-    k = 0
+    if part == "relayed":
+        direct = []
+    else:
+        relayed = []
     for j, (off, rel) in enumerate(relayed):
         p, _ = at(*off)
         _, dev = at(*rel)
@@ -101,6 +102,10 @@
         cp.start()
         copies.append(cp)
         k += 1
+    if part == "relayed":
+        return copies, k
+    local = pltpu.make_async_copy(x_ref.at[me], y_ref.at[me], local_sem)
+    local.start()
     return local, copies, k
 
 
@@ -351,13 +356,17 @@
     for dev in [partner] + x_devs:
         sent += send(lambda m: ins[m].at[h], me, dev)
     t_local, t_copies, t_k = start_plane(
-        n_grp, t_in, t_out, stage, t_send, t_recv, stage_sem, local_sem.at[3]
+        n_grp, t_in, t_out, stage, t_send, t_recv, stage_sem, local_sem.at[3], "direct"
     )
 
     z_blk = block(x, 1 - h, c)
     wait_in(z_blk)
     for dev in [partner] + x_devs:
         sent += send(lambda m: outs[m].at[z_blk], z_blk, dev)
+    more, t_k = start_plane(
+        n_grp, t_in, t_out, stage, t_send, t_recv, stage_sem, local_sem.at[3], "relayed", t_k
+    )
+    t_copies += more
     t_copies += relay_plane(n_grp, t_k, t_in, t_out, stage, t_send, t_recv, stage_sem)
 
     for hh in (h, 1 - h):

time: 212 us -> 221 us (1.042); the launches traced: 209 us -> 221 us
  Pallas kernels: 173 us -> 185 us
    pallas_call x1, Pallas kernels: 99.6 us -> 107 us  [gather_weights(): pl.pallas_call(functools.partial(weight_kernel, n_x, n_grp), out_shape=(s...]
    pallas_call x1, Pallas kernels: 73.4 us -> 78.1 us  [expert_return(): pl.pallas_call(functools.partial(expert_return_kernel, n_grp), out_shape=...]
where the time goes in v15:
time: 221 us
  Pallas kernels  185 us (84%)
  matrix products  30.6 us (14%)
  other arithmetic  4.03 us (2%)
    pallas_call x1, Pallas kernels, gather_weights(): pl.pallas_call(functools.partial(weight_kernel, n_x, n_grp), out_shape=(s...  107 us
    pallas_call x1, Pallas kernels, expert_return(): pl.pallas_call(functools.partial(expert_return_kernel, n_grp), out_shape=...  78.1 us
    dot_general x1, matrix products, per_device(): jnp.einsum('scd,fd->scf', arrived, up_full, preferred_element_type=jnp.fl...  11.8 us
    dot_general x1, matrix products, per_device(): jnp.einsum('scd,fd->scf', arrived, gate_full, preferred_element_type=jnp....  9.76 us

profile of v15, /device:TPU:2, one launch (start us, length us, event | category | flops | bytes accessed | tf_op | source)
XLA Modules:
  0.0 220.9 jit_solution(14365228546127502680)
XLA Ops:
  0.0 0.0 copy-start
  0.0 0.9 copy.21
  0.9 0.1 eq.35
  1.0 2.0 reduce-window.6
  3.0 0.3 slice_reduce_fusion
  3.4 0.1 bitcast_bitcast_fusion
  3.5 0.1 reduce_sum.21
  3.6 0.1 copy.24
  3.7 0.7 multiply_add_fusion
  4.4 0.6 fusion
  5.0 0.0 copy-done
  5.1 3.7 %convolution_convert_fusion = bf16[1152,2048]{1,0:T(8,128)(2,1)} fusion(pred[1152,144]{0,1:T(8,128)(4,1)S(1)} %fusion, bf16[144,2048]{1,0:T(8,128)(2,1)S(1)} %copy-done), kind=kOutput, calls=%fused_computation | convolution fusion | flops 681836544 | bytes 5474304 | tf_op jit(solution)/shard_map/dot_general | solution.py:439
  8.7 106.5 %shard_map.64 = (bf16[16,88,2048]{2,1,0:T(8,128)(2,1)}, bf16[16,88,2048]{2,1,0:T(8,128)(2,1)}, bf16[16,88,2048]{2,1,0:T(8,128)(2,1)}, bf16[16,72,2048]{2,1,0:T(8,128)(2,1)}) custom-call(bf16[2,88,2048]{2,1,0:T(8,128)(2,1)} %g_in.1, bf16[2,88,2048]{2,1,0:T(8,128)(2,1)} %u_in.1, bf16[2,88,2048]{2,1,0:T(8,128)(2,1)} %d_in.1, bf16[16,72,2048]{2,1,0:T(8,128)(2,1)} %bitcast.35), custom_call_target="tpu_custom_call" | custom-call | bytes 17301504 | tf_op jit(solution)/shard_map/pallas_call | solution.py:401
  115.2 0.0 copy-start.3
  115.3 0.0 copy-start.4
  115.3 11.8 %fusion.7 = f32[16,72,1408]{2,1,0:T(8,128)S(1)} fusion(bf16[16,72,2048]{2,1,0:T(8,128)(2,1)} %get-tuple-element.9, bf16[1408,2048,1]{1,0,2:T(8,128)(2,1)} %bitcast.41), kind=kOutput, calls=%fused_computation.22 | convolution fusion | flops 6643777536 | bytes 16973824 | tf_op jit(solution)/shard_map/scd,fd->scf/dot_general | solution.py:449
  127.0 0.0 copy-done.3
  127.1 0.0 copy-done.4
  127.1 9.8 %multiply_convert_fusion.hid_ref = bf16[16,72,1408]{2,1,0:T(8,128)(2,1)} fusion(f32[16,72,1408]{2,1,0:T(8,128)S(1)} %fusion.7, bf16[16,72,2048]{2,1,0:T(8,128)(2,1)S(1)} %copy-done.4, bf16[1408,2048,1]{1,0,2:T(8,128)(2,1)S(1)} %bitcast.40), kind=kOutput, calls=%fused_computation.1 | convolution fusion | flops 6653509632 | bytes 20217856 | tf_op jit(solution)/shard_map/scd,fd->scf/dot_general | solution.py:448
  136.8 0.0 copy-start.2
  136.8 78.1 %shard_map.65 = bf16[16,72,2048]{2,1,0:T(8,128)(2,1)} custom-call(bf16[16,72,1408]{2,1,0:T(8,128)(2,1)} %multiply_convert_fusion.hid_ref, bf16[1408,2048]{1,0:T(8,128)(2,1)} %bitcast.39), custom_call_target="tpu_custom_call" | custom-call | flops 6643777536 | bytes 18448384 | tf_op jit(solution)/shard_map/pallas_call | solution.py:271
  215.0 0.0 copy-start.1
  215.0 0.0 copy-done.2
  215.0 0.5 select_reduce_fusion
  215.5 3.6 %fusion.4 = f32[144,2048]{1,0:T(8,128)S(1)} fusion(bf16[1152,2048]{1,0:T(8,128)(2,1)} %bitcast.36, f32[1152,144]{0,1:T(8,128)S(1)} %select_reduce_fusion), kind=kOutput, calls=%fused_computation.10 | convolution fusion | flops 679809024 | bytes 6561792 | tf_op jit(solution)/shard_map/dot_general | solution.py:460
  219.1 0.0 copy-done.1
  219.1 1.8 fusion.1
  (4 shorter events, 0.1 us)
Async XLA Ops:
  0.0 5.0 %copy-start = (bf16[144,2048]{1,0:T(8,128)(2,1)S(1)}, bf16[144,2048]{1,0:T(8,128)(2,1)}, u32[]{:S(2)}) copy-start(bf16[144,2048]{1,0:T(8,128)(2,1)} %param.6) | copy-start | bytes 1769476
  115.2 11.8 %copy-start.3 = (bf16[16,88,2048]{2,1,0:T(8,128)(2,1)S(1)}, bf16[16,88,2048]{2,1,0:T(8,128)(2,1)}, u32[]{:S(2)}) copy-start(bf16[16,88,2048]{2,1,0:T(8,128)(2,1)} %get-tuple-element.10) | copy-start | bytes 17301508
  115.3 11.8 %copy-start.4 = (bf16[16,72,2048]{2,1,0:T(8,128)(2,1)S(1)}, bf16[16,72,2048]{2,1,0:T(8,128)(2,1)}, u32[]{:S(2)}) copy-start(bf16[16,72,2048]{2,1,0:T(8,128)(2,1)} %get-tuple-element.9) | copy-start | bytes 14155780
  136.8 78.2 %copy-start.2 = (f32[144,6]{0,1:T(8,128)S(1)}, f32[144,6]{0,1:T(8,128)}, u32[]{:S(2)}) copy-start(f32[144,6]{0,1:T(8,128)} %param.8) | copy-start | bytes 10372
  215.0 4.1 %copy-start.1 = (bf16[16,72,2048]{2,1,0:T(8,128)(2,1)S(1)}, bf16[16,72,2048]{2,1,0:T(8,128)(2,1)}, u32[]{:S(2)}) copy-start(bf16[16,72,2048]{2,1,0:T(8,128)(2,1)} %shard_map.65) | copy-start | bytes 14155780

commit v16 on v13

--- a/solution.py
+++ b/solution.py
@@ -355,15 +355,15 @@
     wait_in(z_blk)
     for dev in [partner] + x_devs:
         sent += send(lambda m: outs[m].at[z_blk], z_blk, dev)
-    t_local, t_copies, t_k = start_plane(
-        n_grp, t_in, t_out, stage, t_send, t_recv, stage_sem, local_sem.at[3]
-    )
 
     for hh in (h, 1 - h):
         blk = block(away, hh, c)
         wait_in(blk)
         sent += send(lambda m: outs[m].at[blk], blk, partner)
         sent += send(lambda m: outs[m].at[blk], blk, {"x": toward})
+    t_local, t_copies, t_k = start_plane(
+        n_grp, t_in, t_out, stage, t_send, t_recv, stage_sem, local_sem.at[3]
+    )
     t_copies += relay_plane(n_grp, t_k, t_in, t_out, stage, t_send, t_recv, stage_sem)
     for xp in (toward, far_x):
         for hh in (h, 1 - h):

time: 204 us -> 229 us (1.12)
  the two profiles are of different devices: /device:TPU:29 before, /device:TPU:2 now
where the time goes in v16:
time: 229 us; the launch traced here: 224 us
  Pallas kernels  188 us (82%)
  matrix products  30.6 us (13%)
  other arithmetic  4.03 us (2%)
    pallas_call x1, Pallas kernels, gather_weights(): pl.pallas_call(functools.partial(weight_kernel, n_x, n_grp), out_shape=(s...  112 us
    pallas_call x1, Pallas kernels, expert_return(): pl.pallas_call(functools.partial(expert_return_kernel, n_grp), out_shape=...  76.6 us
    dot_general x1, matrix products, per_device(): jnp.einsum('scd,fd->scf', arrived, up_full, preferred_element_type=jnp.fl...  11.8 us
    dot_general x1, matrix products, per_device(): jnp.einsum('scd,fd->scf', arrived, gate_full, preferred_element_type=jnp....  9.76 us

profile of v16, /device:TPU:2, one launch (start us, length us, event | category | flops | bytes accessed | tf_op | source)
XLA Modules:
  0.0 224.4 jit_solution(9183802624594751919)
XLA Ops:
  0.0 0.0 copy-start
  0.0 0.9 copy.21
  0.9 0.1 eq.35
  1.0 2.0 reduce-window.6
  3.0 0.3 slice_reduce_fusion
  3.4 0.1 bitcast_bitcast_fusion
  3.5 0.1 reduce_sum.21
  3.6 0.1 copy.24
  3.7 0.7 multiply_add_fusion
  4.4 0.6 fusion
  5.0 0.0 copy-done
  5.1 3.7 %convolution_convert_fusion = bf16[1152,2048]{1,0:T(8,128)(2,1)} fusion(pred[1152,144]{0,1:T(8,128)(4,1)S(1)} %fusion, bf16[144,2048]{1,0:T(8,128)(2,1)S(1)} %copy-done), kind=kOutput, calls=%fused_computation | convolution fusion | flops 681836544 | bytes 5474304 | tf_op jit(solution)/shard_map/dot_general | solution.py:430
  8.7 111.6 %shard_map.64 = (bf16[16,88,2048]{2,1,0:T(8,128)(2,1)}, bf16[16,88,2048]{2,1,0:T(8,128)(2,1)}, bf16[16,88,2048]{2,1,0:T(8,128)(2,1)}, bf16[16,72,2048]{2,1,0:T(8,128)(2,1)}) custom-call(bf16[2,88,2048]{2,1,0:T(8,128)(2,1)} %g_in.1, bf16[2,88,2048]{2,1,0:T(8,128)(2,1)} %u_in.1, bf16[2,88,2048]{2,1,0:T(8,128)(2,1)} %d_in.1, bf16[16,72,2048]{2,1,0:T(8,128)(2,1)} %bitcast.35), custom_call_target="tpu_custom_call" | custom-call | bytes 17301504 | tf_op jit(solution)/shard_map/pallas_call | solution.py:392
  120.3 0.0 copy-start.3
  120.3 0.0 copy-start.4
  120.3 11.8 %fusion.7 = f32[16,72,1408]{2,1,0:T(8,128)S(1)} fusion(bf16[16,72,2048]{2,1,0:T(8,128)(2,1)} %get-tuple-element.9, bf16[1408,2048,1]{1,0,2:T(8,128)(2,1)} %bitcast.41), kind=kOutput, calls=%fused_computation.22 | convolution fusion | flops 6643777536 | bytes 16973824 | tf_op jit(solution)/shard_map/scd,fd->scf/dot_general | solution.py:440
  132.1 0.0 copy-done.3
  132.1 0.0 copy-done.4
  132.1 9.8 %multiply_convert_fusion.hid_ref = bf16[16,72,1408]{2,1,0:T(8,128)(2,1)} fusion(f32[16,72,1408]{2,1,0:T(8,128)S(1)} %fusion.7, bf16[16,72,2048]{2,1,0:T(8,128)(2,1)S(1)} %copy-done.4, bf16[1408,2048,1]{1,0,2:T(8,128)(2,1)S(1)} %bitcast.40), kind=kOutput, calls=%fused_computation.1 | convolution fusion | flops 6653509632 | bytes 20217856 | tf_op jit(solution)/shard_map/scd,fd->scf/dot_general | solution.py:439
  141.9 0.0 copy-start.2
  141.9 76.6 %shard_map.65 = bf16[16,72,2048]{2,1,0:T(8,128)(2,1)} custom-call(bf16[16,72,1408]{2,1,0:T(8,128)(2,1)} %multiply_convert_fusion.hid_ref, bf16[1408,2048]{1,0:T(8,128)(2,1)} %bitcast.39), custom_call_target="tpu_custom_call" | custom-call | flops 6643777536 | bytes 18448384 | tf_op jit(solution)/shard_map/pallas_call | solution.py:266
  218.5 0.0 copy-start.1
  218.5 0.0 copy-done.2
  218.5 0.5 select_reduce_fusion
  219.0 3.6 %fusion.4 = f32[144,2048]{1,0:T(8,128)S(1)} fusion(bf16[1152,2048]{1,0:T(8,128)(2,1)} %bitcast.36, f32[1152,144]{0,1:T(8,128)S(1)} %select_reduce_fusion), kind=kOutput, calls=%fused_computation.10 | convolution fusion | flops 679809024 | bytes 6561792 | tf_op jit(solution)/shard_map/dot_general | solution.py:451
  222.6 0.0 copy-done.1
  222.6 1.8 fusion.1
  (4 shorter events, 0.1 us)
Async XLA Ops:
  0.0 5.0 %copy-start = (bf16[144,2048]{1,0:T(8,128)(2,1)S(1)}, bf16[144,2048]{1,0:T(8,128)(2,1)}, u32[]{:S(2)}) copy-start(bf16[144,2048]{1,0:T(8,128)(2,1)} %param.6) | copy-start | bytes 1769476
  120.3 11.8 %copy-start.3 = (bf16[16,88,2048]{2,1,0:T(8,128)(2,1)S(1)}, bf16[16,88,2048]{2,1,0:T(8,128)(2,1)}, u32[]{:S(2)}) copy-start(bf16[16,88,2048]{2,1,0:T(8,128)(2,1)} %get-tuple-element.10) | copy-start | bytes 17301508
  120.3 11.8 %copy-start.4 = (bf16[16,72,2048]{2,1,0:T(8,128)(2,1)S(1)}, bf16[16,72,2048]{2,1,0:T(8,128)(2,1)}, u32[]{:S(2)}) copy-start(bf16[16,72,2048]{2,1,0:T(8,128)(2,1)} %get-tuple-element.9) | copy-start | bytes 14155780
  141.9 76.6 %copy-start.2 = (f32[144,6]{0,1:T(8,128)S(1)}, f32[144,6]{0,1:T(8,128)}, u32[]{:S(2)}) copy-start(f32[144,6]{0,1:T(8,128)} %param.8) | copy-start | bytes 10372
  218.5 4.1 %copy-start.1 = (bf16[16,72,2048]{2,1,0:T(8,128)(2,1)S(1)}, bf16[16,72,2048]{2,1,0:T(8,128)(2,1)}, u32[]{:S(2)}) copy-start(bf16[16,72,2048]{2,1,0:T(8,128)(2,1)} %shard_map.65) | copy-start | bytes 14155780

commit v17 on v9

--- a/solution.py
+++ b/solution.py
@@ -156,8 +156,8 @@
     )(x)
 
 
-def expert_return_kernel(n_grp, rows_ref, gate_ref, up_ref, down_ref, y_ref, buf, stage, send_sem,
-                         recv_sem, stage_sem, local_sem):
+def expert_return_kernel(n_grp, rows_ref, gate_ref, up_ref, down_ref, y_ref, buf, stage, hid_ref,
+                         send_sem, recv_sem, stage_sem, local_sem):
     me, at, direct, relayed = plane_plan(n_grp)
     n_rel = len(relayed)
     order = [off for off, rel in relayed] + direct + [(0, 0)]
@@ -180,11 +180,8 @@
 
     def project(k):
         p, _ = chunk_of(k)
-        r = rows_ref[p]
-        nt = (((1,), (1,)), ((), ()))
-        gate_pre = lax.dot_general(r, gate_ref[...], nt, preferred_element_type=jnp.float32)
-        up_pre = lax.dot_general(r, up_ref[...], nt, preferred_element_type=jnp.float32)
-        hidden = (jax.nn.silu(gate_pre) * up_pre).astype(jnp.bfloat16)
+        cap = buf.shape[1]
+        hidden = hid_ref[pl.ds(pl.multiple_of(p * cap, 8), cap)].astype(jnp.bfloat16)
         buf[p] = jnp.dot(hidden, down_ref[...], preferred_element_type=jnp.float32).astype(buf.dtype)
 
     def first_hop(k):
@@ -216,6 +213,15 @@
                 src_ref=stage.at[j], dst_ref=y_ref.at[src_p], send_sem=send_sem.at[n_grp - 1 + j],
                 recv_sem=recv_sem.at[src_p], device_id=dev, device_id_type=MESH_ID,
             ).start()
+
+    n_rows = rows_ref.shape[0]
+    piece = n_rows // 2
+    nt = (((1,), (1,)), ((), ()))
+    for i in range(2):
+        r = rows_ref[pl.ds(i * piece, piece)]
+        gate_pre = lax.dot_general(r, gate_ref[...], nt, preferred_element_type=jnp.float32)
+        up_pre = lax.dot_general(r, up_ref[...], nt, preferred_element_type=jnp.float32)
+        hid_ref[pl.ds(i * piece, piece)] = jax.nn.silu(gate_pre) * up_pre
 
     local = pltpu.make_async_copy(buf.at[me], y_ref.at[me], local_sem.at[0])
     project(0)
@@ -262,12 +268,14 @@
 
 
 def expert_return(rows, gate_full, up_full, down_full, n_grp, collective_id):
-    n_src, cap, width = rows.shape
+    n_rows, width = rows.shape
     ff = gate_full.shape[0]
+    n_src = n_grp
+    cap = n_rows // n_src
     out = jax.ShapeDtypeStruct((n_src, cap, width), jnp.bfloat16)
     vmem = pl.BlockSpec(memory_space=pltpu.VMEM)
-    flops = 6 * n_src * cap * ff * width
-    nbytes = rows.size * 2 + 3 * gate_full.size * 2 + 2 * n_src * cap * width * 2
+    flops = 6 * n_rows * ff * width
+    nbytes = rows.size * 2 + 3 * gate_full.size * 2 + 2 * n_rows * width * 2
     return pl.pallas_call(
         functools.partial(expert_return_kernel, n_grp),
         out_shape=out,
@@ -276,15 +284,16 @@
         scratch_shapes=[
             pltpu.VMEM((n_src, cap, width), jnp.bfloat16),
             pltpu.VMEM((7, cap, width), jnp.bfloat16),
+            pltpu.VMEM((n_rows, ff), jnp.float32),
             pltpu.SemaphoreType.DMA((n_grp + 8,)),
             pltpu.SemaphoreType.DMA((n_grp,)),
             pltpu.SemaphoreType.DMA((7,)),
             pltpu.SemaphoreType.DMA((1,)),
         ],
         compiler_params=pltpu.CompilerParams(
-            collective_id=collective_id, has_side_effects=True, vmem_limit_bytes=56 * 1024 * 1024
+            collective_id=collective_id, has_side_effects=True, vmem_limit_bytes=64 * 1024 * 1024 - 1024 * 1024
         ),
-        cost_estimate=pl.CostEstimate(flops=flops, transcendentals=n_src * cap * ff, bytes_accessed=nbytes),
+        cost_estimate=pl.CostEstimate(flops=flops, transcendentals=n_rows * ff, bytes_accessed=nbytes),
     )(rows, gate_full, up_full, down_full)
 
 
@@ -355,14 +364,14 @@
     sent += send(lambda m: ins[m].at[1 - h], me, z_peer)
     for dev in [partner] + x_devs:
         sent += send(lambda m: ins[m].at[h], me, dev)
-    t_local, t_copies, t_k = start_plane(
-        n_grp, t_in, t_out, stage, t_send, t_recv, stage_sem, local_sem.at[3]
-    )
 
     z_blk = block(x, 1 - h, c)
     wait_in(z_blk)
     for dev in [partner] + x_devs:
         sent += send(lambda m: outs[m].at[z_blk], z_blk, dev)
+    t_local, t_copies, t_k = start_plane(
+        n_grp, t_in, t_out, stage, t_send, t_recv, stage_sem, local_sem.at[3]
+    )
     t_copies += relay_plane(n_grp, t_k, t_in, t_out, stage, t_send, t_recv, stage_sem)
 
     for hh in (h, 1 - h):
@@ -441,7 +450,9 @@
     gate_full = g_all.reshape(-1, model_width)
     up_full = u_all.reshape(-1, model_width)
     down_full = d_all.reshape(-1, model_width)
-    returned = expert_return(arrived, gate_full, up_full, down_full, n_grp, 1)
+    returned = expert_return(
+        arrived.reshape(n_slot, model_width), gate_full, up_full, down_full, n_grp, 1
+    )
     returned = returned.reshape(n_slot, model_width)
 
     weight_of = jnp.sum(

time: 230 us -> 196 us (0.85)
  the two profiles are of different devices: /device:TPU:15 before, /device:TPU:2 now
where the time goes in v17:
time: 196 us; the launch traced here: 193 us
  Pallas kernels  178 us (91%)
  matrix products  9.07 us (5%)
  other arithmetic  4.03 us (2%)
    pallas_call x1, Pallas kernels, expert_return(): pl.pallas_call(functools.partial(expert_return_kernel, n_grp), out_shape=...  90.1 us
    pallas_call x1, Pallas kernels, gather_weights(): pl.pallas_call(functools.partial(weight_kernel, n_x, n_grp), out_shape=(s...  88 us

profile of v17, /device:TPU:2, one launch (start us, length us, event | category | flops | bytes accessed | tf_op | source)
XLA Modules:
  0.0 192.9 jit_solution(1621559899725838471)
XLA Ops:
  0.0 0.0 copy-start
  0.0 0.9 copy.21
  0.9 0.1 eq.35
  1.0 2.0 %reduce-window.6 = s32[16,7,128]{2,0,1:T(8,128)S(1)} reduce-window(s32[16,7,128]{2,0,1:T(8,128)S(1)} %copy_bitcast_fusion, s32[]{:T(128)} %constant.12.clone.1), window={size=1x1x128 pad=0_0x0_0x127_0}, to_apply=%region_0.0 | reduce-window | flops 1820672 | bytes 114692 | tf_op jit(solution)/shard_map/reduce-window
  3.0 0.3 slice_reduce_fusion
  3.4 0.1 bitcast_bitcast_fusion
  3.5 0.1 reduce_sum.21
  3.6 0.1 copy.24
  3.7 0.7 multiply_add_fusion
  4.4 0.6 fusion
  5.0 0.0 copy-done
  5.1 3.7 %convolution_convert_fusion = bf16[1152,2048]{1,0:T(8,128)(2,1)} fusion(pred[1152,144]{0,1:T(8,128)(4,1)S(1)} %fusion, bf16[144,2048]{1,0:T(8,128)(2,1)S(1)} %copy-done), kind=kOutput, calls=%fused_computation | convolution fusion | flops 681836544 | bytes 5474304 | tf_op jit(solution)/shard_map/dot_general | solution.py:444
  8.7 88.0 %shard_map.64 = (bf16[16,88,2048]{2,1,0:T(8,128)(2,1)}, bf16[16,88,2048]{2,1,0:T(8,128)(2,1)}, bf16[16,88,2048]{2,1,0:T(8,128)(2,1)}, bf16[16,72,2048]{2,1,0:T(8,128)(2,1)}) custom-call(bf16[2,88,2048]{2,1,0:T(8,128)(2,1)} %g_in.1, bf16[2,88,2048]{2,1,0:T(8,128)(2,1)} %u_in.1, bf16[2,88,2048]{2,1,0:T(8,128)(2,1)} %d_in.1, bf16[16,72,2048]{2,1,0:T(8,128)(2,1)} %bitcast.28), custom_call_target="tpu_custom_call" | custom-call | bytes 17301504 | tf_op jit(solution)/shard_map/pallas_call | solution.py:406
  96.7 0.0 copy-start.2
  96.7 90.1 %shard_map.65 = bf16[16,72,2048]{2,1,0:T(8,128)(2,1)} custom-call(bf16[1152,2048]{1,0:T(8,128)(2,1)} %bitcast.35, bf16[1408,2048]{1,0:T(8,128)(2,1)} %bitcast.32, bf16[1408,2048]{1,0:T(8,128)(2,1)} %bitcast.33, bf16[1408,2048]{1,0:T(8,128)(2,1)} %bitcast.34), custom_call_target="tpu_custom_call" | custom-call | flops 19931332608 | bytes 31457280 | tf_op jit(solution)/shard_map/pallas_call | solution.py:279
  186.9 0.0 copy-start.1
  186.9 0.0 copy-done.2
  186.9 0.5 select_reduce_fusion
  187.4 3.6 %fusion.4 = f32[144,2048]{1,0:T(8,128)S(1)} fusion(bf16[1152,2048]{1,0:T(8,128)(2,1)} %bitcast.29, f32[1152,144]{0,1:T(8,128)S(1)} %select_reduce_fusion), kind=kOutput, calls=%fused_computation.9 | convolution fusion | flops 679809024 | bytes 6561792 | tf_op jit(solution)/shard_map/dot_general | solution.py:464
  191.0 0.0 copy-done.1
  191.0 1.8 fusion.1
  (4 shorter events, 0.1 us)
Async XLA Ops:
  0.0 5.0 %copy-start = (bf16[144,2048]{1,0:T(8,128)(2,1)S(1)}, bf16[144,2048]{1,0:T(8,128)(2,1)}, u32[]{:S(2)}) copy-start(bf16[144,2048]{1,0:T(8,128)(2,1)} %param.6) | copy-start | bytes 1769476
  96.7 90.2 %copy-start.2 = (f32[144,6]{0,1:T(8,128)S(1)}, f32[144,6]{0,1:T(8,128)}, u32[]{:S(2)}) copy-start(f32[144,6]{0,1:T(8,128)} %param.8) | copy-start | bytes 10372
  186.9 4.1 %copy-start.1 = (bf16[16,72,2048]{2,1,0:T(8,128)(2,1)S(1)}, bf16[16,72,2048]{2,1,0:T(8,128)(2,1)}, u32[]{:S(2)}) copy-start(bf16[16,72,2048]{2,1,0:T(8,128)(2,1)} %shard_map.65) | copy-start | bytes 14155780

commit v18 on v17

--- a/solution.py
+++ b/solution.py
@@ -461,9 +461,10 @@
     weight_top = lax.reduce_precision(weight_of, exponent_bits=8, mantissa_bits=7)
     weight_hi = weight_top.astype(jnp.bfloat16)
     weight_lo = (weight_of - weight_top).astype(jnp.bfloat16)
-    mixed = jnp.dot(weight_hi, returned, preferred_element_type=jnp.float32) + jnp.dot(
-        weight_lo, returned, preferred_element_type=jnp.float32
+    both = jnp.dot(
+        jnp.concatenate([weight_hi, weight_lo], axis=0), returned, preferred_element_type=jnp.float32
     )
+    mixed = both[:tok_rows] + both[tok_rows:]
     return mixed.astype(jnp.bfloat16)
 
 

time: 196 us -> 196 us (level)
    dot_general x2 -> x1, matrix products: 5.39 us -> 4.07 us  [per_device(): jnp.dot(jnp.concatenate([weight_hi, weight_lo], axis=0), returned, prefer...]
where the time goes in v18:
time: 196 us; the launch traced here: 193 us
  Pallas kernels  178 us (91%)
  matrix products  7.76 us (4%)
  other arithmetic  5.06 us (3%)
    pallas_call x1, Pallas kernels, expert_return(): pl.pallas_call(functools.partial(expert_return_kernel, n_grp), out_shape=...  90.1 us
    pallas_call x1, Pallas kernels, gather_weights(): pl.pallas_call(functools.partial(weight_kernel, n_x, n_grp), out_shape=(s...  88 us
    dot_general x1, matrix products, per_device(): jnp.dot(jnp.concatenate([weight_hi, weight_lo], axis=0), returned, prefer...  4.07 us

profile of v18, /device:TPU:2, one launch (start us, length us, event | category | flops | bytes accessed | tf_op | source)
XLA Modules:
  0.0 192.6 jit_solution(7428316309859231280)
XLA Ops:
  0.0 0.0 copy-start
  0.0 0.9 copy.21
  0.9 0.1 eq.35
  1.0 2.0 %reduce-window.6 = s32[16,7,128]{2,0,1:T(8,128)S(1)} reduce-window(s32[16,7,128]{2,0,1:T(8,128)S(1)} %copy_bitcast_fusion, s32[]{:T(128)} %constant.12.clone.1), window={size=1x1x128 pad=0_0x0_0x127_0}, to_apply=%region_0.0 | reduce-window | flops 1820672 | bytes 114692 | tf_op jit(solution)/shard_map/reduce-window
  3.0 0.3 slice_reduce_fusion
  3.4 0.1 bitcast_bitcast_fusion
  3.5 0.1 reduce_sum.21
  3.6 0.1 copy.24
  3.7 0.7 multiply_add_fusion
  4.4 0.6 fusion
  5.0 0.0 copy-done
  5.1 3.7 %convolution_convert_fusion = bf16[1152,2048]{1,0:T(8,128)(2,1)} fusion(pred[1152,144]{0,1:T(8,128)(4,1)S(1)} %fusion, bf16[144,2048]{1,0:T(8,128)(2,1)S(1)} %copy-done), kind=kOutput, calls=%fused_computation | convolution fusion | flops 681836544 | bytes 5474304 | tf_op jit(solution)/shard_map/dot_general | solution.py:444
  8.7 88.0 %shard_map.64 = (bf16[16,88,2048]{2,1,0:T(8,128)(2,1)}, bf16[16,88,2048]{2,1,0:T(8,128)(2,1)}, bf16[16,88,2048]{2,1,0:T(8,128)(2,1)}, bf16[16,72,2048]{2,1,0:T(8,128)(2,1)}) custom-call(bf16[2,88,2048]{2,1,0:T(8,128)(2,1)} %g_in.1, bf16[2,88,2048]{2,1,0:T(8,128)(2,1)} %u_in.1, bf16[2,88,2048]{2,1,0:T(8,128)(2,1)} %d_in.1, bf16[16,72,2048]{2,1,0:T(8,128)(2,1)} %bitcast.25), custom_call_target="tpu_custom_call" | custom-call | bytes 17301504 | tf_op jit(solution)/shard_map/pallas_call | solution.py:406
  96.7 0.0 copy-start.1
  96.7 90.1 %shard_map.65 = bf16[16,72,2048]{2,1,0:T(8,128)(2,1)} custom-call(bf16[1152,2048]{1,0:T(8,128)(2,1)} %bitcast.30, bf16[1408,2048]{1,0:T(8,128)(2,1)} %bitcast.27, bf16[1408,2048]{1,0:T(8,128)(2,1)} %bitcast.28, bf16[1408,2048]{1,0:T(8,128)(2,1)} %bitcast.29), custom_call_target="tpu_custom_call" | custom-call | flops 19931332608 | bytes 31457280 | tf_op jit(solution)/shard_map/pallas_call | solution.py:279
  186.9 0.0 copy-done.1
  186.9 0.5 select_reduce_fusion
  187.4 0.1 reduce-precision_convert_fusion
  187.5 4.1 %fusion.3 = f32[288,2048]{1,0:T(8,128)S(1)} fusion(bf16[1152,2048]{1,0:T(8,128)(2,1)} %bitcast.31, bf16[144,1152]{1,0:T(8,128)(2,1)S(1)} %get-tuple-element.14, bf16[144,1152]{1,0:T(8,128)(2,1)S(1)} %get-tuple-element.13), kind=kOutput, calls=%fused_computation.9 | convolution fusion | flops 1360281600 | bytes 7741440 | tf_op jit(solution)/shard_map/dot_general | solution.py:464
  191.6 0.9 fusion.1
  (4 shorter events, 0.1 us)
Async XLA Ops:
  0.0 5.0 %copy-start = (bf16[144,2048]{1,0:T(8,128)(2,1)S(1)}, bf16[144,2048]{1,0:T(8,128)(2,1)}, u32[]{:S(2)}) copy-start(bf16[144,2048]{1,0:T(8,128)(2,1)} %param.6) | copy-start | bytes 1769476
  96.7 90.2 %copy-start.1 = (f32[144,6]{0,1:T(8,128)S(1)}, f32[144,6]{0,1:T(8,128)}, u32[]{:S(2)}) copy-start(f32[144,6]{0,1:T(8,128)} %param.8) | copy-start | bytes 10372

commit v19 on v18

--- a/solution.py
+++ b/solution.py
@@ -436,7 +436,13 @@
 
     flat_ids = expert_ids.reshape(-1)
     onehot = (flat_ids[:, None] == jnp.arange(n_expert, dtype=jnp.int32)[None, :]).astype(jnp.int32)
-    earlier = jnp.cumsum(onehot, axis=0) - onehot
+    n_pair = flat_ids.shape[0]
+    before = (
+        lax.broadcasted_iota(jnp.int32, (n_pair, n_pair), 0)
+        > lax.broadcasted_iota(jnp.int32, (n_pair, n_pair), 1)
+    ).astype(jnp.bfloat16)
+    earlier = jnp.dot(before, onehot.astype(jnp.bfloat16), preferred_element_type=jnp.float32)
+    earlier = earlier.astype(jnp.int32)
     rank_within = jnp.sum(earlier * onehot, axis=1)
     slot_index = (flat_ids * CAP + rank_within).reshape(tok_rows, top_k)
     hit = slot_index[None, :, :] == jnp.arange(n_slot, dtype=jnp.int32)[:, None, None]

time: 196 us -> 194 us (0.990)
  other arithmetic: 5.06 us -> 2.9 us
    another operation x4 -> x0, other arithmetic: 2.12 us -> none
where the time goes in v19:
time: 194 us; the launch traced here: 191 us
  Pallas kernels  178 us (92%)
  matrix products  8.17 us (4%)
  other arithmetic  2.9 us (1%)
    pallas_call x1, Pallas kernels, expert_return(): pl.pallas_call(functools.partial(expert_return_kernel, n_grp), out_shape=...  90.3 us
    pallas_call x1, Pallas kernels, gather_weights(): pl.pallas_call(functools.partial(weight_kernel, n_x, n_grp), out_shape=(s...  88 us
    dot_general x1, matrix products, per_device(): jnp.dot(jnp.concatenate([weight_hi, weight_lo], axis=0), returned, prefer...  4.08 us

profile of v19, /device:TPU:2, one launch (start us, length us, event | category | flops | bytes accessed | tf_op | source)
XLA Modules:
  0.0 190.7 jit_solution(15142497128317202192)
XLA Ops:
  0.0 0.0 copy-start
  0.0 0.9 copy.17
  0.9 0.1 eq.28
  1.0 0.4 fusion.5
  1.4 0.1 reduce_sum.21
  1.6 0.1 copy.18
  1.6 0.7 multiply_add_fusion
  2.3 0.6 fusion
  3.0 0.0 copy-done
  3.0 3.7 %convolution_convert_fusion = bf16[1152,2048]{1,0:T(8,128)(2,1)} fusion(pred[1152,144]{0,1:T(8,128)(4,1)S(1)} %fusion, bf16[144,2048]{1,0:T(8,128)(2,1)S(1)} %copy-done), kind=kOutput, calls=%fused_computation | convolution fusion | flops 681836544 | bytes 5474304 | tf_op jit(solution)/shard_map/dot_general | solution.py:450
  6.7 88.0 %shard_map.64 = (bf16[16,88,2048]{2,1,0:T(8,128)(2,1)}, bf16[16,88,2048]{2,1,0:T(8,128)(2,1)}, bf16[16,88,2048]{2,1,0:T(8,128)(2,1)}, bf16[16,72,2048]{2,1,0:T(8,128)(2,1)}) custom-call(bf16[2,88,2048]{2,1,0:T(8,128)(2,1)} %g_in.1, bf16[2,88,2048]{2,1,0:T(8,128)(2,1)} %u_in.1, bf16[2,88,2048]{2,1,0:T(8,128)(2,1)} %d_in.1, bf16[16,72,2048]{2,1,0:T(8,128)(2,1)} %bitcast.12), custom_call_target="tpu_custom_call" | custom-call | bytes 17301504 | tf_op jit(solution)/shard_map/pallas_call | solution.py:406
  94.7 0.0 copy-start.1
  94.7 90.3 %shard_map.65 = bf16[16,72,2048]{2,1,0:T(8,128)(2,1)} custom-call(bf16[1152,2048]{1,0:T(8,128)(2,1)} %bitcast.16, bf16[1408,2048]{1,0:T(8,128)(2,1)} %bitcast.13, bf16[1408,2048]{1,0:T(8,128)(2,1)} %bitcast.14, bf16[1408,2048]{1,0:T(8,128)(2,1)} %bitcast.15), custom_call_target="tpu_custom_call" | custom-call | flops 19931332608 | bytes 31457280 | tf_op jit(solution)/shard_map/pallas_call | solution.py:279
  185.0 0.0 copy-done.1
  185.0 0.5 select_reduce_fusion
  185.6 0.1 reduce-precision_convert_fusion
  185.6 4.1 %fusion.7 = f32[288,2048]{1,0:T(8,128)S(1)} fusion(bf16[1152,2048]{1,0:T(8,128)(2,1)} %bitcast.17, bf16[144,1152]{1,0:T(8,128)(2,1)S(1)} %get-tuple-element.14, bf16[144,1152]{1,0:T(8,128)(2,1)S(1)} %get-tuple-element.13), kind=kOutput, calls=%fused_computation.14 | convolution fusion | flops 1360281600 | bytes 7741440 | tf_op jit(solution)/shard_map/dot_general | solution.py:470
  189.7 0.9 fusion.2
Async XLA Ops:
  0.0 3.0 %copy-start = (bf16[144,2048]{1,0:T(8,128)(2,1)S(1)}, bf16[144,2048]{1,0:T(8,128)(2,1)}, u32[]{:S(2)}) copy-start(bf16[144,2048]{1,0:T(8,128)(2,1)} %param.6) | copy-start | bytes 1769476
  94.7 90.3 %copy-start.1 = (f32[144,6]{0,1:T(8,128)S(1)}, f32[144,6]{0,1:T(8,128)}, u32[]{:S(2)}) copy-start(f32[144,6]{0,1:T(8,128)} %param.8) | copy-start | bytes 10372

commit v20 on v19

--- a/solution.py
+++ b/solution.py
@@ -445,8 +445,10 @@
     earlier = earlier.astype(jnp.int32)
     rank_within = jnp.sum(earlier * onehot, axis=1)
     slot_index = (flat_ids * CAP + rank_within).reshape(tok_rows, top_k)
-    hit = slot_index[None, :, :] == jnp.arange(n_slot, dtype=jnp.int32)[:, None, None]
-    pick = jnp.any(hit, axis=2).astype(jnp.bfloat16)
+    slot_col = lax.broadcasted_iota(jnp.int32, (n_slot, tok_rows), 0)
+    pick = sum(
+        (slot_index[:, k][None, :] == slot_col).astype(jnp.bfloat16) for k in range(top_k)
+    )
     outgoing = jnp.dot(pick, tokens, preferred_element_type=jnp.float32).astype(jnp.bfloat16)
     outgoing = outgoing.reshape(n_expert, CAP, model_width)
 
@@ -461,9 +463,11 @@
     )
     returned = returned.reshape(n_slot, model_width)
 
-    weight_of = jnp.sum(
-        jnp.where(hit, combine[None, :, :], jnp.zeros_like(combine)[None, :, :]), axis=2
-    ).T
+    slot_row = lax.broadcasted_iota(jnp.int32, (tok_rows, n_slot), 1)
+    weight_of = sum(
+        jnp.where(slot_index[:, k][:, None] == slot_row, combine[:, k][:, None], 0.0)
+        for k in range(top_k)
+    )
     weight_top = lax.reduce_precision(weight_of, exponent_bits=8, mantissa_bits=7)
     weight_hi = weight_top.astype(jnp.bfloat16)
     weight_lo = (weight_of - weight_top).astype(jnp.bfloat16)

time: 194 us -> 194 us (level)
  no operation moved by 1% of the time
where the time goes in v20:
time: 194 us; the launch traced here: 190 us
  Pallas kernels  178 us (92%)
  matrix products  8.52 us (4%)
    pallas_call x1, Pallas kernels, expert_return(): pl.pallas_call(functools.partial(expert_return_kernel, n_grp), out_shape=...  90.3 us
    pallas_call x1, Pallas kernels, gather_weights(): pl.pallas_call(functools.partial(weight_kernel, n_x, n_grp), out_shape=(s...  88 us
    dot_general x1, matrix products, per_device(): jnp.dot(jnp.concatenate([weight_hi, weight_lo], axis=0), returned, prefer...  4.07 us
    dot_general x1, matrix products, per_device(): jnp.dot(pick, tokens, preferred_element_type=jnp.float32)  4.05 us

profile of v20, /device:TPU:2, one launch (start us, length us, event | category | flops | bytes accessed | tf_op | source)
XLA Modules:
  0.0 189.8 jit_solution(18127862550827496127)
XLA Ops:
  0.0 0.0 copy-start
  0.0 0.0 copy-start.1
  0.0 0.9 copy.13
  0.9 0.1 eq.123
  1.0 0.4 fusion.10
  1.4 0.1 reduce_sum.12
  1.6 0.1 copy.14
  1.6 0.0 copy-done.1
  1.7 0.0 copy-done
  1.7 4.0 %convolution_convert_fusion = bf16[1152,2048]{1,0:T(8,128)(2,1)} fusion(bf16[144,2048]{1,0:T(8,128)(2,1)S(1)} %copy-done, s32[144]{0:T(256)S(1)} %bitcast.23, s32[144]{0:T(256)S(1)} %bitcast.25, s32[144]{0:T(256)S(1)} %bitcast.27, s32[144]{0:T(256)S(1)} %bitcast.29, s32[144]{0:T(256)S(1)} %bitcast.31, s32[144]{0:T(256)S(1)} %bitcast.21), kind=kOutput, calls=%fused_computation | convolution fusion | flops 685817856 | bytes 5311872 | tf_op jit(solution)/shard_map/dot_general | solution.py:452
  5.7 88.0 %shard_map.64 = (bf16[16,88,2048]{2,1,0:T(8,128)(2,1)}, bf16[16,88,2048]{2,1,0:T(8,128)(2,1)}, bf16[16,88,2048]{2,1,0:T(8,128)(2,1)}, bf16[16,72,2048]{2,1,0:T(8,128)(2,1)}) custom-call(bf16[2,88,2048]{2,1,0:T(8,128)(2,1)} %g_in.1, bf16[2,88,2048]{2,1,0:T(8,128)(2,1)} %u_in.1, bf16[2,88,2048]{2,1,0:T(8,128)(2,1)} %d_in.1, bf16[16,72,2048]{2,1,0:T(8,128)(2,1)} %bitcast.20), custom_call_target="tpu_custom_call" | custom-call | bytes 17301504 | tf_op jit(solution)/shard_map/pallas_call | solution.py:406
  93.7 0.0 copy-start.2
  93.8 90.3 %shard_map.65 = bf16[16,72,2048]{2,1,0:T(8,128)(2,1)} custom-call(bf16[1152,2048]{1,0:T(8,128)(2,1)} %bitcast.42, bf16[1408,2048]{1,0:T(8,128)(2,1)} %bitcast.39, bf16[1408,2048]{1,0:T(8,128)(2,1)} %bitcast.40, bf16[1408,2048]{1,0:T(8,128)(2,1)} %bitcast.41), custom_call_target="tpu_custom_call" | custom-call | flops 19931332608 | bytes 31457280 | tf_op jit(solution)/shard_map/pallas_call | solution.py:279
  184.1 0.0 copy-done.2
  184.1 0.6 reduce-precision_convert_fusion
  184.7 4.1 %fusion.12 = f32[288,2048]{1,0:T(8,128)S(1)} fusion(bf16[1152,2048]{1,0:T(8,128)(2,1)} %bitcast.43, bf16[144,1152]{1,0:T(8,128)(2,1)S(1)} %get-tuple-element.14, bf16[144,1152]{1,0:T(8,128)(2,1)S(1)} %get-tuple-element.13), kind=kOutput, calls=%fused_computation.23 | convolution fusion | flops 1360281600 | bytes 7741440 | tf_op jit(solution)/shard_map/dot_general | solution.py:474
  188.8 0.9 fusion.1
  (3 shorter events, 0.0 us)
Async XLA Ops:
  0.0 1.7 copy-start
  0.0 1.6 copy-start.1
  93.7 90.3 %copy-start.2 = (f32[144,6]{0,1:T(8,128)S(1)}, f32[144,6]{0,1:T(8,128)}, u32[]{:S(2)}) copy-start(f32[144,6]{0,1:T(8,128)} %param.8) | copy-start | bytes 10372

commit v21 on v20

--- a/solution.py
+++ b/solution.py
@@ -215,9 +215,9 @@
             ).start()
 
     n_rows = rows_ref.shape[0]
-    piece = n_rows // 2
+    piece = n_rows
     nt = (((1,), (1,)), ((), ()))
-    for i in range(2):
+    for i in range(1):
         r = rows_ref[pl.ds(i * piece, piece)]
         gate_pre = lax.dot_general(r, gate_ref[...], nt, preferred_element_type=jnp.float32)
         up_pre = lax.dot_general(r, up_ref[...], nt, preferred_element_type=jnp.float32)

time: 194 us -> 194 us (level)
  no operation moved by 1% of the time
where the time goes in v21:
time: 194 us; the launch traced here: 190 us
  Pallas kernels  179 us (92%)
  matrix products  8.52 us (4%)
    pallas_call x1, Pallas kernels, expert_return(): pl.pallas_call(functools.partial(expert_return_kernel, n_grp), out_shape=...  90.6 us
    pallas_call x1, Pallas kernels, gather_weights(): pl.pallas_call(functools.partial(weight_kernel, n_x, n_grp), out_shape=(s...  88 us
    dot_general x1, matrix products, per_device(): jnp.dot(jnp.concatenate([weight_hi, weight_lo], axis=0), returned, prefer...  4.07 us
    dot_general x1, matrix products, per_device(): jnp.dot(pick, tokens, preferred_element_type=jnp.float32)  4.05 us

profile of v21, /device:TPU:2, one launch (start us, length us, event | category | flops | bytes accessed | tf_op | source)
XLA Modules:
  0.0 190.0 jit_solution(6576687709522667150)
XLA Ops:
  0.0 0.0 copy-start
  0.0 0.0 copy-start.1
  0.0 0.9 copy.13
  0.9 0.1 eq.123
  1.0 0.4 fusion.10
  1.4 0.1 reduce_sum.12
  1.6 0.1 copy.14
  1.6 0.0 copy-done.1
  1.7 0.0 copy-done
  1.7 4.0 %convolution_convert_fusion = bf16[1152,2048]{1,0:T(8,128)(2,1)} fusion(bf16[144,2048]{1,0:T(8,128)(2,1)S(1)} %copy-done, s32[144]{0:T(256)S(1)} %bitcast.23, s32[144]{0:T(256)S(1)} %bitcast.25, s32[144]{0:T(256)S(1)} %bitcast.27, s32[144]{0:T(256)S(1)} %bitcast.29, s32[144]{0:T(256)S(1)} %bitcast.31, s32[144]{0:T(256)S(1)} %bitcast.21), kind=kOutput, calls=%fused_computation | convolution fusion | flops 685817856 | bytes 5311872 | tf_op jit(solution)/shard_map/dot_general | solution.py:452
  5.7 88.0 %shard_map.64 = (bf16[16,88,2048]{2,1,0:T(8,128)(2,1)}, bf16[16,88,2048]{2,1,0:T(8,128)(2,1)}, bf16[16,88,2048]{2,1,0:T(8,128)(2,1)}, bf16[16,72,2048]{2,1,0:T(8,128)(2,1)}) custom-call(bf16[2,88,2048]{2,1,0:T(8,128)(2,1)} %g_in.1, bf16[2,88,2048]{2,1,0:T(8,128)(2,1)} %u_in.1, bf16[2,88,2048]{2,1,0:T(8,128)(2,1)} %d_in.1, bf16[16,72,2048]{2,1,0:T(8,128)(2,1)} %bitcast.20), custom_call_target="tpu_custom_call" | custom-call | bytes 17301504 | tf_op jit(solution)/shard_map/pallas_call | solution.py:406
  93.7 0.0 copy-start.2
  93.8 90.6 %shard_map.65 = bf16[16,72,2048]{2,1,0:T(8,128)(2,1)} custom-call(bf16[1152,2048]{1,0:T(8,128)(2,1)} %bitcast.42, bf16[1408,2048]{1,0:T(8,128)(2,1)} %bitcast.39, bf16[1408,2048]{1,0:T(8,128)(2,1)} %bitcast.40, bf16[1408,2048]{1,0:T(8,128)(2,1)} %bitcast.41), custom_call_target="tpu_custom_call" | custom-call | flops 19931332608 | bytes 31457280 | tf_op jit(solution)/shard_map/pallas_call | solution.py:279
  184.4 0.0 copy-done.2
  184.4 0.6 reduce-precision_convert_fusion
  185.0 4.1 %fusion.12 = f32[288,2048]{1,0:T(8,128)S(1)} fusion(bf16[1152,2048]{1,0:T(8,128)(2,1)} %bitcast.43, bf16[144,1152]{1,0:T(8,128)(2,1)S(1)} %get-tuple-element.14, bf16[144,1152]{1,0:T(8,128)(2,1)S(1)} %get-tuple-element.13), kind=kOutput, calls=%fused_computation.23 | convolution fusion | flops 1360281600 | bytes 7741440 | tf_op jit(solution)/shard_map/dot_general | solution.py:474
  189.1 0.9 fusion.1
  (3 shorter events, 0.0 us)
Async XLA Ops:
  0.0 1.7 copy-start
  0.0 1.6 copy-start.1
  93.7 90.6 %copy-start.2 = (f32[144,6]{0,1:T(8,128)S(1)}, f32[144,6]{0,1:T(8,128)}, u32[]{:S(2)}) copy-start(f32[144,6]{0,1:T(8,128)} %param.8) | copy-start | bytes 10372

commit v22 on v20

--- a/solution.py
+++ b/solution.py
@@ -82,21 +82,21 @@
     local = pltpu.make_async_copy(x_ref.at[me], y_ref.at[me], local_sem)
     local.start()
     k = 0
+    for off in direct:
+        p, dev = at(*off)
+        cp = pltpu.make_async_remote_copy(
+            src_ref=x_ref.at[p], dst_ref=y_ref.at[me], send_sem=send_sem.at[k],
+            recv_sem=recv_sem.at[me], device_id=dev, device_id_type=MESH_ID,
+        )
+        cp.start()
+        copies.append(cp)
+        k += 1
     for j, (off, rel) in enumerate(relayed):
         p, _ = at(*off)
         _, dev = at(*rel)
         cp = pltpu.make_async_remote_copy(
             src_ref=x_ref.at[p], dst_ref=stage.at[j], send_sem=send_sem.at[k],
             recv_sem=stage_sem.at[j], device_id=dev, device_id_type=MESH_ID,
-        )
-        cp.start()
-        copies.append(cp)
-        k += 1
-    for off in direct:
-        p, dev = at(*off)
-        cp = pltpu.make_async_remote_copy(
-            src_ref=x_ref.at[p], dst_ref=y_ref.at[me], send_sem=send_sem.at[k],
-            recv_sem=recv_sem.at[me], device_id=dev, device_id_type=MESH_ID,
         )
         cp.start()
         copies.append(cp)

time: 194 us -> 215 us (1.11)
  the two profiles are of different devices: /device:TPU:2 before, /device:TPU:81 now
where the time goes in v22:
time: 215 us; the launch traced here: 214 us
  Pallas kernels  203 us (94%)
  matrix products  8.52 us (4%)
    pallas_call x1, Pallas kernels, expert_return(): pl.pallas_call(functools.partial(expert_return_kernel, n_grp), out_shape=...  102 us
    pallas_call x1, Pallas kernels, gather_weights(): pl.pallas_call(functools.partial(weight_kernel, n_x, n_grp), out_shape=(s...  100 us

profile of v22, /device:TPU:81, one launch (start us, length us, event | category | flops | bytes accessed | tf_op | source)
XLA Modules:
  0.0 214.4 jit_solution(13870269550959432232)
XLA Ops:
  0.0 0.0 copy-start
  0.0 0.0 copy-start.1
  0.0 0.9 copy.13
  0.9 0.1 eq.123
  1.0 0.4 fusion.10
  1.4 0.1 reduce_sum.12
  1.6 0.1 copy.14
  1.6 0.0 copy-done.1
  1.7 0.0 copy-done
  1.7 4.0 %convolution_convert_fusion = bf16[1152,2048]{1,0:T(8,128)(2,1)} fusion(bf16[144,2048]{1,0:T(8,128)(2,1)S(1)} %copy-done, s32[144]{0:T(256)S(1)} %bitcast.23, s32[144]{0:T(256)S(1)} %bitcast.25, s32[144]{0:T(256)S(1)} %bitcast.27, s32[144]{0:T(256)S(1)} %bitcast.29, s32[144]{0:T(256)S(1)} %bitcast.31, s32[144]{0:T(256)S(1)} %bitcast.21), kind=kOutput, calls=%fused_computation | convolution fusion | flops 685817856 | bytes 5311872 | tf_op jit(solution)/shard_map/dot_general | solution.py:452
  5.7 100.5 %shard_map.64 = (bf16[16,88,2048]{2,1,0:T(8,128)(2,1)}, bf16[16,88,2048]{2,1,0:T(8,128)(2,1)}, bf16[16,88,2048]{2,1,0:T(8,128)(2,1)}, bf16[16,72,2048]{2,1,0:T(8,128)(2,1)}) custom-call(bf16[2,88,2048]{2,1,0:T(8,128)(2,1)} %g_in.1, bf16[2,88,2048]{2,1,0:T(8,128)(2,1)} %u_in.1, bf16[2,88,2048]{2,1,0:T(8,128)(2,1)} %d_in.1, bf16[16,72,2048]{2,1,0:T(8,128)(2,1)} %bitcast.20), custom_call_target="tpu_custom_call" | custom-call | bytes 17301504 | tf_op jit(solution)/shard_map/pallas_call | solution.py:406
  106.2 0.0 copy-start.2
  106.2 102.5 %shard_map.65 = bf16[16,72,2048]{2,1,0:T(8,128)(2,1)} custom-call(bf16[1152,2048]{1,0:T(8,128)(2,1)} %bitcast.42, bf16[1408,2048]{1,0:T(8,128)(2,1)} %bitcast.39, bf16[1408,2048]{1,0:T(8,128)(2,1)} %bitcast.40, bf16[1408,2048]{1,0:T(8,128)(2,1)} %bitcast.41), custom_call_target="tpu_custom_call" | custom-call | flops 19931332608 | bytes 31457280 | tf_op jit(solution)/shard_map/pallas_call | solution.py:279
  208.7 0.0 copy-done.2
  208.8 0.6 reduce-precision_convert_fusion
  209.4 4.1 %fusion.12 = f32[288,2048]{1,0:T(8,128)S(1)} fusion(bf16[1152,2048]{1,0:T(8,128)(2,1)} %bitcast.43, bf16[144,1152]{1,0:T(8,128)(2,1)S(1)} %get-tuple-element.14, bf16[144,1152]{1,0:T(8,128)(2,1)S(1)} %get-tuple-element.13), kind=kOutput, calls=%fused_computation.23 | convolution fusion | flops 1360281600 | bytes 7741440 | tf_op jit(solution)/shard_map/dot_general | solution.py:474
  213.5 0.9 fusion.1
  (3 shorter events, 0.0 us)
Async XLA Ops:
  0.0 1.7 copy-start
  0.0 1.6 copy-start.1
  106.2 102.5 %copy-start.2 = (f32[144,6]{0,1:T(8,128)S(1)}, f32[144,6]{0,1:T(8,128)}, u32[]{:S(2)}) copy-start(f32[144,6]{0,1:T(8,128)} %param.8) | copy-start | bytes 10372
